TPU v7x, 32 devices: a whole 2x2x4 slice. The times are simulated.
32 devices in a mesh: dp: 8 (over y, x, core), tensor: 4 (over z).
Axes of the slice: x: 2, y: 2, z: 4, core: 2. Of those that a mesh axis runs over, the one named last changes fastest.
Arguments:
- tokens: bfloat16 [8, 1024, 2048], P('dp', 'tensor'), may hold values from -6 to 6
- lengths: int32 [8], P('dp'), may hold values from 512 to 1024, as said below
- routes: int32 [8, 1024, 8], P('dp'), may hold values from 0 to 31, all different within a row; in each aligned block of 256 rows (0 to 255, 256 to 511, ..., all dimensions but the last counted through in order) at most 80 rows name the same one
- attn_gain: float32 [2048], replicated, may hold values from 0.5 to 1.5
- w_query: bfloat16 [2048, 2048], P(None, 'tensor'), may hold values from -0.125 to 0.125
- w_key: bfloat16 [2048, 2048], P(None, 'tensor'), may hold values from -0.125 to 0.125
- w_value: bfloat16 [2048, 2048], P(None, 'tensor'), may hold values from -0.125 to 0.125
- w_out: bfloat16 [2048, 2048], P(None, 'tensor'), may hold values from -2 to 2
- q_gain: float32 [128], replicated, may hold values from 0.5 to 1.5
- k_gain: float32 [128], replicated, may hold values from 0.5 to 1.5
- ffn_gain: float32 [2048], replicated, may hold values from 0.5 to 1.5
- router_weight: bfloat16 [2048, 32], replicated, may hold values from -0.0625 to 0.0625
- w_gate: bfloat16 [32, 2048, 1024], P('dp', None, 'tensor'), may hold values from -0.125 to 0.125
- w_up: bfloat16 [32, 2048, 1024], P('dp', None, 'tensor'), may hold values from -0.125 to 0.125
- w_down: bfloat16 [32, 1024, 2048], P('dp', 'tensor'), may hold values from -6 to 6
- cotangent: bfloat16 [8, 1024, 2048], P('dp'), may hold values from -6 to 6
Outputs:
- output: bfloat16 [8, 1024, 2048], P('dp', 'tensor')
- grad_tokens: bfloat16 [8, 1024, 2048], P('dp', 'tensor')
- grad_attn_gain: float32 [2048], P('dp')
- grad_query: float32 [2048, 2048], P('dp', 'tensor')
- grad_key: float32 [2048, 2048], P('dp', 'tensor')
- grad_value: float32 [2048, 2048], P('dp', 'tensor')
- grad_out: float32 [2048, 2048], P('dp', 'tensor')
- grad_q_gain: float32 [128], P('dp')
- grad_k_gain: float32 [128], P('dp')
- grad_ffn_gain: float32 [2048], P('dp')
- grad_router: float32 [2048, 32], P('dp')
- grad_gate: float32 [32, 2048, 1024], P('dp', None, 'tensor')
- grad_up: float32 [32, 2048, 1024], P('dp', None, 'tensor')
- grad_down: float32 [32, 1024, 2048], P('dp', 'tensor')
Inputs may be any that keep to these rules, and one draw needn't show every extreme that they name: `lengths`: at least one sequence has all 1024 positions valid. `routes`: in each aligned block of 256 positions (one sequence's positions on one index of tensor) an expert is named by at most 80 rows, and by exactly 80 in some blocks.
All inputs are finite; a program needn't handle non-finite values.
Results may differ from a plain program's by a relative error of at most 0.029.
Values may be sent and summed in bfloat16 or wider, within the bound.
A program may use at most 320 MiB of HBM per device.

v0:
```python
import jax
import jax.numpy as jnp
from jax import lax
from jax.sharding import PartitionSpec as P

EPS = 1e-06
THETA = 50000.0
NEG = -1e30


def rms_scale(values, gain):
    return values * lax.rsqrt(jnp.mean(values * values, axis=-1, keepdims=True) + EPS) * gain


def rotate(values):
    length = values.shape[-3]
    half_dim = values.shape[-1] // 2
    positions = jnp.arange(length).astype(jnp.float32)
    rates = THETA ** (-jnp.arange(half_dim).astype(jnp.float32) / half_dim)
    angles = positions[:, None] * rates[None, :]
    cosine = jnp.cos(angles)[:, None, :]
    sine = jnp.sin(angles)[:, None, :]
    first = values[..., :half_dim]
    second = values[..., half_dim:]
    return jnp.concatenate(
        [first * cosine - second * sine, second * cosine + first * sine], axis=-1
    )


def prepare(raw, gain):
    shaped = raw.reshape(raw.shape[0], -1, gain.shape[0])
    return rotate(rms_scale(shaped, gain))


def per_device(
    tokens,
    lengths,
    routes,
    attn_gain,
    w_query,
    w_key,
    w_value,
    w_out,
    q_gain,
    k_gain,
    ffn_gain,
    router_weight,
    w_gate,
    w_up,
    w_down,
    cotangent,
):
    tensor_count = lax.axis_size("tensor")
    data_count = lax.axis_size("dp")
    tensor_rank = lax.axis_index("tensor")
    block_rows = tokens.shape[1]
    width = tokens.shape[2]
    full_length = block_rows * tensor_count
    route_count = routes.shape[2]
    local_experts = w_gate.shape[0]
    all_experts = local_experts * data_count
    head_dim = q_gain.shape[0]
    local_width = w_query.shape[1]
    capacity = max(2, (block_rows * route_count * 5 + 4 * all_experts - 1) // (4 * all_experts))
    query_rows = min(512, full_length)
    scale = head_dim ** (-0.5)
    pair_count = block_rows * route_count
    own_start = tensor_rank * block_rows
    token_values = tokens[0].astype(jnp.float32)
    seq_length = lengths[0]
    own_valid = (own_start + jnp.arange(block_rows) < seq_length).astype(jnp.float32)
    all_valid = (jnp.arange(full_length) < seq_length).astype(jnp.float32)
    key_valid = jnp.arange(full_length) < seq_length
    normed = rms_scale(token_values, attn_gain).astype(jnp.bfloat16)
    gathered = lax.all_gather(normed, "tensor", axis=0, tiled=True)
    query_unrotated = jnp.dot(gathered, w_query, preferred_element_type=jnp.float32)
    key_raw = jnp.dot(gathered, w_key, preferred_element_type=jnp.float32)
    value_raw = jnp.dot(gathered, w_value, preferred_element_type=jnp.float32)
    query_low = prepare(query_unrotated, q_gain).astype(jnp.bfloat16)
    key_low = prepare(key_raw, k_gain).astype(jnp.bfloat16)
    value_low = value_raw.astype(jnp.bfloat16).reshape(full_length, -1, head_dim)

    def block_scores(query_block):
        scores = (
            jnp.einsum("qhd,khd->hqk", query_block, key_low, preferred_element_type=jnp.float32)
            * scale
        )
        return jnp.where(key_valid[None, None, :], scores, NEG)

    mixed_parts = []
    log_totals = []
    for start in range(0, full_length, query_rows):
        scores = block_scores(query_low[start : start + query_rows])
        row_peak = jnp.max(scores, axis=-1, keepdims=True)
        powers = jnp.exp(scores - row_peak)
        total = jnp.sum(powers, axis=-1, keepdims=True)
        weights = (powers / total).astype(jnp.bfloat16)
        mixed_parts.append(
            jnp.einsum("hqk,khd->qhd", weights, value_low, preferred_element_type=jnp.float32)
        )
        log_totals.append(row_peak + jnp.log(total))
    attended = (
        jnp.concatenate(mixed_parts, axis=0).reshape(full_length, local_width).astype(jnp.bfloat16)
    )
    attn_own = lax.psum_scatter(
        jnp.einsum("lh,dh->ld", attended, w_out, preferred_element_type=jnp.float32).astype(
            jnp.bfloat16
        ),
        "tensor",
        scatter_dimension=0,
        tiled=True,
    ).astype(jnp.float32)
    residual = token_values + own_valid[:, None] * attn_own
    moe_own = rms_scale(residual, ffn_gain).astype(jnp.bfloat16)
    moe_all = lax.dynamic_update_slice_in_dim(
        jnp.zeros((full_length, width), jnp.bfloat16), moe_own, own_start, 0
    )
    router_logits = jnp.dot(moe_all, router_weight, preferred_element_type=jnp.float32)
    router_probs = jax.nn.softmax(router_logits, axis=-1)
    route_all = routes[0]
    onehot = route_all[:, :, None] == jnp.arange(all_experts)[None, None, :]
    picked = jnp.sum(jnp.where(onehot, router_probs[:, None, :], 0.0), axis=-1)
    route_weight = picked * all_valid[:, None]
    pair_expert = route_all.reshape(tensor_count, pair_count)
    pair_onehot = onehot.reshape(tensor_count, pair_count, all_experts).astype(jnp.int32)
    slots = jnp.sum((jnp.cumsum(pair_onehot, axis=1) - 1) * pair_onehot, axis=2)
    block_ids = jnp.broadcast_to(jnp.arange(tensor_count)[:, None], pair_expert.shape)
    pair_ids = jnp.broadcast_to(jnp.arange(pair_count)[None, :], pair_expert.shape)
    table = jnp.full((tensor_count, all_experts, capacity), pair_count, jnp.int32)
    table = table.at[block_ids, pair_expert, slots].set(pair_ids)
    filled = table < pair_count
    block_base = jnp.arange(tensor_count)[:, None, None]
    token_slot = jnp.where(filled, block_base * block_rows + table // route_count, full_length)
    pair_slot = jnp.where(filled, block_base * pair_count + table, full_length * route_count)
    moe_padded = jnp.concatenate([moe_all, jnp.zeros((1, width), jnp.bfloat16)], axis=0)
    gate_weights, up_weights, down_weights = (
        lax.all_gather(w_gate, "tensor", axis=2, tiled=True),
        lax.all_gather(w_up, "tensor", axis=2, tiled=True),
        lax.all_gather(w_down, "tensor", axis=1, tiled=True),
    )
    row_slots = lax.dynamic_slice_in_dim(token_slot, tensor_rank, 1, 0)
    weight_slots = lax.dynamic_slice_in_dim(pair_slot, tensor_rank, 1, 0)

    def send_rows(values):
        return lax.all_to_all(values, "dp", split_axis=1, concat_axis=1, tiled=True)

    buffer_shape = (row_slots.shape[0], data_count, local_experts, capacity, width)

    def dispatch_rows():
        return send_rows(moe_padded[row_slots].reshape(buffer_shape))

    received = dispatch_rows()
    gate_pre = jnp.einsum(
        "tsecd,edf->tsecf", received, gate_weights, preferred_element_type=jnp.float32
    )
    up_pre = jnp.einsum(
        "tsecd,edf->tsecf", received, up_weights, preferred_element_type=jnp.float32
    )
    activation = (jax.nn.silu(gate_pre) * up_pre).astype(jnp.bfloat16)
    expert_sum = jnp.einsum(
        "tsecf,efd->tsecd", activation, down_weights, preferred_element_type=jnp.float32
    )[0]
    returned = lax.all_to_all(
        expert_sum.astype(jnp.bfloat16), "dp", split_axis=0, concat_axis=0, tiled=True
    )
    returned_flat = returned.reshape(all_experts * capacity, width)
    own_slots = lax.dynamic_index_in_dim(slots, tensor_rank, 0, keepdims=False).reshape(
        block_rows, route_count
    )
    own_routes = lax.dynamic_slice_in_dim(route_all, own_start, block_rows, 0)
    route_index = own_routes * capacity + own_slots
    route_values = returned_flat[route_index]
    own_weight = lax.dynamic_slice_in_dim(route_weight, own_start, block_rows, 0)
    moe_sum = jnp.einsum("rk,rkd->rd", own_weight, route_values, preferred_element_type=jnp.float32)
    output = (residual + moe_sum).astype(jnp.bfloat16)
    grad_all = cotangent[0]
    grad_own = lax.dynamic_slice_in_dim(grad_all, own_start, block_rows, 0).astype(jnp.float32)
    grad_weight = jnp.einsum(
        "rd,rkd->rk", grad_own, route_values, preferred_element_type=jnp.float32
    )
    weight_padded = jnp.concatenate([route_weight.reshape(-1), jnp.zeros((1,), jnp.float32)])
    grad_padded = jnp.concatenate([grad_all, jnp.zeros((1, width), jnp.bfloat16)], axis=0)
    slot_grads = (
        (weight_padded[weight_slots][..., None] * grad_padded[row_slots])
        .astype(jnp.bfloat16)
        .reshape(buffer_shape)
    )
    grad_received = lax.all_to_all(slot_grads, "dp", split_axis=1, concat_axis=1, tiled=True)
    rows_back = dispatch_rows()
    grad_act = jnp.einsum(
        "tsecd,efd->tsecf", grad_received, down_weights, preferred_element_type=jnp.float32
    )
    grad_down_local = jnp.einsum(
        "tsecf,tsecd->efd", activation, grad_received, preferred_element_type=jnp.float32
    )
    gate_sigmoid = jax.nn.sigmoid(gate_pre)
    grad_gate_pre = (
        grad_act * up_pre * gate_sigmoid * (1.0 + gate_pre * (1.0 - gate_sigmoid))
    ).astype(jnp.bfloat16)
    grad_up_pre = (grad_act * gate_pre * gate_sigmoid).astype(jnp.bfloat16)
    grad_gate_local = jnp.einsum(
        "tsecd,tsecf->edf", rows_back, grad_gate_pre, preferred_element_type=jnp.float32
    )
    grad_up_local = jnp.einsum(
        "tsecd,tsecf->edf", rows_back, grad_up_pre, preferred_element_type=jnp.float32
    )
    from_gate = jnp.einsum(
        "tsecf,edf->tsecd", grad_gate_pre, gate_weights, preferred_element_type=jnp.float32
    )
    from_up = jnp.einsum(
        "tsecf,edf->tsecd", grad_up_pre, up_weights, preferred_element_type=jnp.float32
    )
    input_sum = (from_gate + from_up)[0]
    grads_back = lax.all_to_all(
        input_sum.astype(jnp.bfloat16), "dp", split_axis=0, concat_axis=0, tiled=True
    )
    grad_gate = lax.psum_scatter(
        grad_gate_local.astype(jnp.bfloat16), "tensor", scatter_dimension=2, tiled=True
    ).astype(jnp.float32)
    grad_up = lax.psum_scatter(
        grad_up_local.astype(jnp.bfloat16), "tensor", scatter_dimension=2, tiled=True
    ).astype(jnp.float32)
    grad_down = lax.psum_scatter(
        grad_down_local.astype(jnp.bfloat16), "tensor", scatter_dimension=1, tiled=True
    ).astype(jnp.float32)
    grad_moe = jnp.sum(
        grads_back.reshape(all_experts * capacity, width)[route_index], axis=1, dtype=jnp.float32
    )
    own_probs = lax.dynamic_slice_in_dim(router_probs, own_start, block_rows, 0)
    own_onehot = lax.dynamic_slice_in_dim(onehot, own_start, block_rows, 0)
    grad_picked = grad_weight * own_valid[:, None]
    grad_probs = jnp.sum(jnp.where(own_onehot, grad_picked[:, :, None], 0.0), axis=1)
    grad_logits = (
        own_probs * (grad_probs - jnp.sum(own_probs * grad_probs, axis=-1, keepdims=True))
    ).astype(jnp.bfloat16)
    grad_moe = grad_moe + jnp.einsum(
        "re,de->rd", grad_logits, router_weight, preferred_element_type=jnp.float32
    )
    router_part = jnp.einsum("rd,re->de", moe_own, grad_logits, preferred_element_type=jnp.float32)
    ffn_pull = jax.vjp(rms_scale, residual, ffn_gain)[1]
    grad_res_norm, ffn_part = ffn_pull(grad_moe)
    grad_residual = grad_own + grad_res_norm
    grad_attn = (grad_residual * own_valid[:, None]).astype(jnp.bfloat16)
    grad_attn_all = lax.all_gather(grad_attn, "tensor", axis=0, tiled=True)
    grad_mixed = jnp.dot(grad_attn_all, w_out, preferred_element_type=jnp.float32).astype(
        jnp.bfloat16
    )
    grad_mixed = grad_mixed.reshape(full_length, -1, head_dim)
    out_part = jnp.einsum("ld,lh->dh", grad_attn_all, attended, preferred_element_type=jnp.float32)
    grad_query_parts = []
    grad_keys = jnp.zeros(key_low.shape, jnp.float32)
    grad_values = jnp.zeros(value_low.shape, jnp.float32)
    for order, start in enumerate(range(0, full_length, query_rows)):
        query_block = query_low[start : start + query_rows]
        grad_block = grad_mixed[start : start + query_rows]
        probs_block = jnp.exp(block_scores(query_block) - log_totals[order])
        probs_low = probs_block.astype(jnp.bfloat16)
        grad_values = grad_values + jnp.einsum(
            "hqk,qhd->khd", probs_low, grad_block, preferred_element_type=jnp.float32
        )
        grad_probs_block = jnp.einsum(
            "qhd,khd->hqk", grad_block, value_low, preferred_element_type=jnp.float32
        )
        delta = jnp.sum(probs_block * grad_probs_block, axis=-1, keepdims=True)
        grad_scores = (probs_block * (grad_probs_block - delta)).astype(jnp.bfloat16)
        grad_query_parts.append(
            jnp.einsum("hqk,khd->qhd", grad_scores, key_low, preferred_element_type=jnp.float32)
            * scale
        )
        grad_keys = (
            grad_keys
            + jnp.einsum(
                "hqk,qhd->khd", grad_scores, query_block, preferred_element_type=jnp.float32
            )
            * scale
        )
    grad_queries = jnp.concatenate(grad_query_parts, axis=0)
    query_pull = jax.vjp(prepare, query_unrotated, q_gain)[1]
    grad_query_raw, q_part = query_pull(grad_queries)
    key_pull = jax.vjp(prepare, key_raw, k_gain)[1]
    grad_key_raw, k_part = key_pull(grad_keys)
    grad_q_low = grad_query_raw.astype(jnp.bfloat16)
    grad_k_low = grad_key_raw.astype(jnp.bfloat16)
    grad_v_low = grad_values.reshape(full_length, local_width).astype(jnp.bfloat16)
    query_part = jnp.einsum("ld,lh->dh", gathered, grad_q_low, preferred_element_type=jnp.float32)
    key_part = jnp.einsum("ld,lh->dh", gathered, grad_k_low, preferred_element_type=jnp.float32)
    value_part = jnp.einsum("ld,lh->dh", gathered, grad_v_low, preferred_element_type=jnp.float32)
    from_query = jnp.einsum("lh,dh->ld", grad_q_low, w_query, preferred_element_type=jnp.float32)
    from_key = jnp.einsum("lh,dh->ld", grad_k_low, w_key, preferred_element_type=jnp.float32)
    from_value = jnp.einsum("lh,dh->ld", grad_v_low, w_value, preferred_element_type=jnp.float32)
    grad_normed = lax.psum_scatter(
        (from_query + from_key + from_value).astype(jnp.bfloat16),
        "tensor",
        scatter_dimension=0,
        tiled=True,
    ).astype(jnp.float32)
    attn_pull = jax.vjp(rms_scale, token_values, attn_gain)[1]
    grad_tok_norm, attn_part = attn_pull(grad_normed)
    grad_tokens = (grad_residual + grad_tok_norm).astype(jnp.bfloat16)
    summed = (
        lax.psum_scatter(
            query_part.astype(jnp.bfloat16), "dp", scatter_dimension=0, tiled=True
        ).astype(jnp.float32),
        lax.psum_scatter(
            key_part.astype(jnp.bfloat16), "dp", scatter_dimension=0, tiled=True
        ).astype(jnp.float32),
        lax.psum_scatter(
            value_part.astype(jnp.bfloat16), "dp", scatter_dimension=0, tiled=True
        ).astype(jnp.float32),
        lax.psum_scatter(
            out_part.astype(jnp.bfloat16), "dp", scatter_dimension=0, tiled=True
        ).astype(jnp.float32),
        lax.psum_scatter(
            router_part.astype(jnp.bfloat16), "dp", scatter_dimension=0, tiled=True
        ).astype(jnp.float32),
        lax.psum_scatter(
            attn_part.astype(jnp.bfloat16), "dp", scatter_dimension=0, tiled=True
        ).astype(jnp.float32),
        lax.psum_scatter(
            ffn_part.astype(jnp.bfloat16), "dp", scatter_dimension=0, tiled=True
        ).astype(jnp.float32),
        lax.psum_scatter(q_part.astype(jnp.bfloat16), "dp", scatter_dimension=0, tiled=True).astype(
            jnp.float32
        ),
        lax.psum_scatter(k_part.astype(jnp.bfloat16), "dp", scatter_dimension=0, tiled=True).astype(
            jnp.float32
        ),
    )
    shared = (
        lax.psum(summed[4].astype(jnp.bfloat16), "tensor").astype(jnp.float32),
        lax.psum(summed[5].astype(jnp.bfloat16), "tensor").astype(jnp.float32),
        lax.psum(summed[6].astype(jnp.bfloat16), "tensor").astype(jnp.float32),
        lax.psum(summed[7].astype(jnp.bfloat16), "tensor").astype(jnp.float32),
        lax.psum(summed[8].astype(jnp.bfloat16), "tensor").astype(jnp.float32),
    )
    return (
        output[None],
        grad_tokens[None],
        shared[1],
        summed[0],
        summed[1],
        summed[2],
        summed[3],
        shared[3],
        shared[4],
        shared[2],
        shared[0],
        grad_gate,
        grad_up,
        grad_down,
    )


def solution(mesh):
    return jax.shard_map(
        per_device,
        mesh=mesh,
        in_specs=(
            P("dp", "tensor", None),
            P("dp"),
            P("dp", None, None),
            P(),
            P(None, "tensor"),
            P(None, "tensor"),
            P(None, "tensor"),
            P(None, "tensor"),
            P(),
            P(),
            P(),
            P(),
            P("dp", None, "tensor"),
            P("dp", None, "tensor"),
            P("dp", "tensor", None),
            P("dp", None, None),
        ),
        out_specs=(
            P("dp", "tensor", None),
            P("dp", "tensor", None),
            P("dp"),
            P("dp", "tensor"),
            P("dp", "tensor"),
            P("dp", "tensor"),
            P("dp", "tensor"),
            P("dp"),
            P("dp"),
            P("dp"),
            P("dp", None),
            P("dp", None, "tensor"),
            P("dp", None, "tensor"),
            P("dp", "tensor", None),
        ),
        check_vma=False,
    )
```

profile of v0, /device:TPU:0, one launch (start us, length us, event | category | flops | bytes accessed | tf_op | source)
XLA Modules:
  0.0 2733.0 jit_solution(7826638298968352138)
XLA Ops:
  15.2 81.0 %all-gather.6.cloned.1.call-done = bf16[1024,2048]{1,0:T(8,128)(2,1)} async-done(((bf16[256,2048]{1,0:T(8,128)(2,1)}), bf16[1024,2048]{1,0:T(8,128)(2,1)}) %all-gather.6.cloned.1.call-update) | async-done | bytes 4194320 | tf_op jit(solution)/shard_map/all_gather | solution.py:75
  149.5 68.0 %reduce-window.6 = s32[4,32,16,128]{3,2,1,0:T(8,128)} reduce-window(s32[4,32,16,128]{3,2,1,0:T(8,128)} %fusion.89, s32[]{:T(128)} %constant.41.clone.1), window={size=1x1x1x128 pad=0_0x0_0x0_0x127_0}, to_apply=%region_12.13 | reduce-window | flops 33292288 | bytes 2097156 | tf_op jit(solution)/shard_map/reduce-window
  230.2 30.9 %scatter_custom_fusion = s32[10240]{0:T(1024)S(1)} fusion(s32[8192]{0:T(1024)S(1)} %bitcast.328, s32[8192]{0:T(1024)S(1)} %bitcast.329, s32[]{:T(128)} %constant.43.clone.1), kind=kCustom, calls=%fused_computation.204 | custom fusion | bytes 40964
  271.2 23.0 gather_fusion
  304.2 23.0 gather_fusion.3
  332.0 13.6 gather_fusion.2
  356.4 59.5 %all-to-all-done = bf16[1,8,4,80,2048]{4,3,2,0,1:T(8,128)(2,1)} async-done(((bf16[1,8,4,80,2048]{4,3,2,0,1:T(8,128)(2,1)}), bf16[1,8,4,80,2048]{4,3,2,0,1:T(8,128)(2,1)}, u32[]{:S(2)}, u32[]{:S(2)}) %all-to-all-start) | async-done | bytes 10485792 | tf_op jit(solution)/shard_map/all_to_all | solution.py:145
  421.2 88.1 %all-gather.10.cloned.1.call-done = bf16[4,2048,1024]{2,1,0:T(8,128)(2,1)} async-done(((bf16[4,2048,256]{2,1,0:T(8,128)(2,1)}), bf16[4,2048,1024]{2,1,0:T(8,128)(2,1)}) %all-gather.10.cloned.1.call-update) | async-done | bytes 16777232 | tf_op jit(solution)/shard_map/all_gather | solution.py:138
  509.3 20.0 fusion.3
  529.3 265.8 %all-gather.8.cloned.1.call-done = bf16[4,2048,1024]{2,1,0:T(8,128)(2,1)} async-done(((bf16[4,2048,256]{2,1,0:T(8,128)(2,1)}), bf16[4,2048,1024]{2,1,0:T(8,128)(2,1)}) %all-gather.8.cloned.1.call-update) | async-done | bytes 16777232 | tf_op jit(solution)/shard_map/all_gather | solution.py:137
  795.1 20.1 fusion.7
  815.3 266.3 %all-gather.12.cloned.1.call-done = bf16[4,1024,2048]{2,1,0:T(8,128)(2,1)} async-done(((bf16[4,256,2048]{2,1,0:T(8,128)(2,1)}), bf16[4,1024,2048]{2,1,0:T(8,128)(2,1)}) %all-gather.12.cloned.1.call-update) | async-done | bytes 16777232 | tf_op jit(solution)/shard_map/all_gather | solution.py:139
  1081.5 27.6 %fusion.17 = (bf16[1,8,4,80,1024]{4,3,1,2,0:T(8,128)(2,1)}, bf16[1,8,4,80,1024]{4,3,1,2,0:T(8,128)(2,1)}, bf16[1,8,4,80,1024]{4,3,1,2,0:T(8,128)(2,1)}) fusion(f32[4,8,80,1024]{3,2,1,0:T(8,128)} %fusion.3, f32[4,8,80,1024]{3,2,1,0:T(8,128)} %fusion.7, bf16[4,1024,2048]{2,1,0:T(8,128)(2,1)} %all-gather.12.cloned.1.call-done, ...), kind=kOutput, calls=%fused_computation.31 | convolution fusion | flops 10779361280 | bytes 63963136 | tf_op jit(solution)/shard_map/tsecd,efd->tsecf/dot_general | solution.py:190
  1109.1 19.5 fusion.1
  1128.6 21.2 fusion.13
  1165.5 20.1 convert_bitcast_fusion
  1195.8 86.3 %all-to-all-done.3 = bf16[8,4,80,2048]{3,2,1,0:T(8,128)(2,1)} async-done(((bf16[8,4,80,2048]{3,2,1,0:T(8,128)(2,1)}), bf16[8,4,80,2048]{3,2,1,0:T(8,128)(2,1)}, u32[]{:S(2)}, u32[]{:S(2)}) %all-to-all-start.3) | async-done | bytes 10485792 | tf_op jit(solution)/shard_map/all_to_all | solution.py:214
  1292.4 21.8 gather_fusion.4
  1325.5 78.2 %all-to-all-done.1 = bf16[8,4,80,2048]{3,2,1,0:T(8,128)(2,1)} async-done(((bf16[8,4,80,2048]{3,2,1,0:T(8,128)(2,1)}), bf16[8,4,80,2048]{3,2,1,0:T(8,128)(2,1)}, u32[]{:S(2)}, u32[]{:S(2)}) %all-to-all-start.1) | async-done | bytes 10485792 | tf_op jit(solution)/shard_map/all_to_all | solution.py:163
  1403.7 21.8 gather_fusion.1
  1445.4 77.2 %all-gather.14.cloned.1.call-done = bf16[1024,2048]{1,0:T(8,128)(2,1)} async-done(((bf16[256,2048]{1,0:T(8,128)(2,1)}), bf16[1024,2048]{1,0:T(8,128)(2,1)}) %all-gather.14.cloned.1.call-update) | async-done | bytes 4194320 | tf_op jit(solution)/shard_map/all_gather | solution.py:244
  1640.7 21.1 bitcast_convert_fusion.2
  1662.0 20.8 bitcast_convert_fusion.1
  1683.1 20.0 bitcast_convert_fusion
  1719.2 33.3 %reduce-scatter.21.cloned.1.call-done = bf16[256,512]{1,0:T(8,128)(2,1)} async-done(((bf16[2048,512]{1,0:T(8,128)(2,1)}), bf16[256,512]{1,0:T(8,128)(2,1)}) %reduce-scatter.21.cloned.1.call-update) | async-done | bytes 262160 | tf_op jit(solution)/shard_map/reduce_scatter | solution.py:310
  1754.3 77.9 %reduce-scatter.13.cloned.1.call-done = bf16[256,2048]{1,0:T(8,128)(2,1)} async-done(((bf16[1024,2048]{1,0:T(8,128)(2,1)}), bf16[256,2048]{1,0:T(8,128)(2,1)}) %reduce-scatter.13.cloned.1.call-update) | async-done | bytes 1048592 | tf_op jit(solution)/shard_map/reduce_scatter | solution.py:291
  1834.5 13.8 all-reduce.10
  1848.6 21.2 reduce-scatter.23.cloned.1.call-done
  1869.8 20.1 all-reduce.11
  1898.0 254.9 %reduce-scatter.25.cloned.1.call-done = bf16[4,2048,256]{2,1,0:T(8,128)(2,1)} async-done(((bf16[4,2048,1024]{2,1,0:T(8,128)(2,1)}), bf16[4,2048,256]{2,1,0:T(8,128)(2,1)}) %reduce-scatter.25.cloned.1.call-update) | async-done | bytes 4194320 | tf_op jit(solution)/shard_map/reduce_scatter | solution.py:217
  2159.2 277.1 %reduce-scatter.27.cloned.1.call-done = bf16[4,2048,256]{2,1,0:T(8,128)(2,1)} async-done(((bf16[4,2048,1024]{2,1,0:T(8,128)(2,1)}), bf16[4,2048,256]{2,1,0:T(8,128)(2,1)}) %reduce-scatter.27.cloned.1.call-update) | async-done | bytes 4194320 | tf_op jit(solution)/shard_map/reduce_scatter | solution.py:220
  2442.6 277.0 %reduce-scatter.29.cloned.1.call-done = bf16[4,256,2048]{2,1,0:T(8,128)(2,1)} async-done(((bf16[4,1024,2048]{2,1,0:T(8,128)(2,1)}), bf16[4,256,2048]{2,1,0:T(8,128)(2,1)}) %reduce-scatter.29.cloned.1.call-update) | async-done | bytes 4194320 | tf_op jit(solution)/shard_map/reduce_scatter | solution.py:223
  (374 shorter events, 345.1 us)
Async XLA Ops:
  7.2 89.0 %copy-start = (bf16[2048,512]{1,0:T(8,128)(2,1)S(1)}, bf16[2048,512]{1,0:T(8,128)(2,1)}, u32[]{:S(2)}) copy-start(bf16[2048,512]{1,0:T(8,128)(2,1)} %param.20) | copy-start | bytes 6291460
  7.2 89.0 %all-gather.6.cloned.1.call-start = ((), (), s32[]{:S(2)}) async-start(), calls=%async_computation.14 | async-start | bytes 5242880 | tf_op jit(solution)/shard_map/all_gather | solution.py:75
  12.6 251.2 %reduce-scatter.11.cloned.1.call-start = ((), (), s32[]{:S(2)}) async-start(), calls=%async_computation.15 | async-start | bytes 5242880 | tf_op jit(solution)/shard_map/reduce_scatter | solution.py:105
  13.3 123.7 %copy-start.69 = (pred[1024]{0:T(1024)(128)(4,1)}, pred[1024]{0:T(1024)(128)(4,1)S(1)}, u32[]{:S(2)}) copy-start(pred[1024]{0:T(1024)(128)(4,1)S(1)} %iota_compare_fusion.3) | copy-start | bytes 3076
  15.2 103.1 %copy-start.18 = (f32[1024,64]{1,0:T(8,128)}, f32[1024,64]{1,0:T(8,128)S(1)}, u32[]{:S(2)}) copy-start(f32[1024,64]{1,0:T(8,128)S(1)} %get-tuple-element.61) | copy-start | bytes 786436
  15.2 103.1 %copy-start.20 = (f32[1024,64]{1,0:T(8,128)}, f32[1024,64]{1,0:T(8,128)S(1)}, u32[]{:S(2)}) copy-start(f32[1024,64]{1,0:T(8,128)S(1)} %get-tuple-element.62) | copy-start | bytes 786436
  145.5 363.8 %all-gather.10.cloned.1.call-start = ((), (), s32[]{:S(2)}) async-start(), calls=%async_computation.17 | async-start | bytes 20971520 | tf_op jit(solution)/shard_map/all_gather | solution.py:138
  146.2 648.9 %all-gather.8.cloned.1.call-start = ((), (), s32[]{:S(2)}) async-start(), calls=%async_computation.16 | async-start | bytes 20971520 | tf_op jit(solution)/shard_map/all_gather | solution.py:137
  146.8 934.7 %all-gather.12.cloned.1.call-start = ((), (), s32[]{:S(2)}) async-start(), calls=%async_computation.18 | async-start | bytes 20971520 | tf_op jit(solution)/shard_map/all_gather | solution.py:139
  294.1 121.7 %all-to-all-start = ((bf16[1,8,4,80,2048]{4,3,2,0,1:T(8,128)(2,1)}), bf16[1,8,4,80,2048]{4,3,2,0,1:T(8,128)(2,1)}, u32[]{:S(2)}, u32[]{:S(2)}) async-start(bf16[1,8,4,80,2048]{4,3,2,0,1:T(8,128)(2,1)} %bitcast.303), calls=%async_computation.1 | async-start | bytes 20971520 | tf_op jit(solution)/shard_map/all_to_all | solution.py:145
  415.9 399.4 %all-to-all-start.2 = ((bf16[1,8,4,80,2048]{4,3,2,0,1:T(8,128)(2,1)}), bf16[1,8,4,80,2048]{4,3,2,0,1:T(8,128)(2,1)}, u32[]{:S(2)}, u32[]{:S(2)}) async-start(bf16[1,8,4,80,2048]{4,3,2,0,1:T(8,128)(2,1)} %fusion.14), calls=%async_computation.3 | async-start | bytes 20971520 | tf_op jit(solution)/shard_map/all_to_all | solution.py:188
  1159.9 122.2 %all-to-all-start.3 = ((bf16[8,4,80,2048]{3,2,1,0:T(8,128)(2,1)}), bf16[8,4,80,2048]{3,2,1,0:T(8,128)(2,1)}, u32[]{:S(2)}, u32[]{:S(2)}) async-start(bf16[8,4,80,2048]{3,2,1,0:T(8,128)(2,1)} %copy.131), calls=%async_computation.4 | async-start | bytes 20971520 | tf_op jit(solution)/shard_map/all_to_all | solution.py:214
  1195.8 93.5 %copy-start.42 = (s32[1,1024,8]{1,2,0:T(8,128)S(1)}, s32[1,1024,8]{1,2,0:T(8,128)}, u32[]{:S(2)}) copy-start(s32[1,1024,8]{1,2,0:T(8,128)} %param.18) | copy-start | bytes 98308
  1282.1 121.7 %all-to-all-start.1 = ((bf16[8,4,80,2048]{3,2,1,0:T(8,128)(2,1)}), bf16[8,4,80,2048]{3,2,1,0:T(8,128)(2,1)}, u32[]{:S(2)}, u32[]{:S(2)}) async-start(bf16[8,4,80,2048]{3,2,1,0:T(8,128)(2,1)} %copy.126), calls=%async_computation.2 | async-start | bytes 20971520 | tf_op jit(solution)/shard_map/all_to_all | solution.py:163
  1287.2 235.4 %all-gather.14.cloned.1.call-start = ((), (), s32[]{:S(2)}) async-start(), calls=%async_computation.19 | async-start | bytes 5242880 | tf_op jit(solution)/shard_map/all_gather | solution.py:244
  1440.7 87.2 %copy-start.75 = (f32[256]{0:T(256)}, f32[256]{0:T(256)S(1)}, u32[]{:S(2)}) copy-start(f32[256]{0:T(256)S(1)} %multiply_multiply_fusion.5) | copy-start | bytes 3076
  1445.3 268.4 %reduce-scatter.15.cloned.1.call-start = ((), (), s32[]{:S(2)}) async-start(), calls=%async_computation.21 | async-start | bytes 2359296 | tf_op jit(solution)/shard_map/reduce_scatter | solution.py:301
  1579.5 136.0 %reduce-scatter.17.cloned.1.call-start = ((), (), s32[]{:S(2)}) async-start(), calls=%async_computation.22 | async-start | bytes 2359296 | tf_op jit(solution)/shard_map/reduce_scatter | solution.py:304
  1595.9 121.5 %reduce-scatter.19.cloned.1.call-start = ((), (), s32[]{:S(2)}) async-start(), calls=%async_computation.23 | async-start | bytes 2359296 | tf_op jit(solution)/shard_map/reduce_scatter | solution.py:307
  1612.7 139.8 %reduce-scatter.21.cloned.1.call-start = ((), (), s32[]{:S(2)}) async-start(), calls=%async_computation.24 | async-start | bytes 2359296 | tf_op jit(solution)/shard_map/reduce_scatter | solution.py:310
  1619.1 213.1 %reduce-scatter.13.cloned.1.call-start = ((), (), s32[]{:S(2)}) async-start(), calls=%async_computation.20 | async-start | bytes 5242880 | tf_op jit(solution)/shard_map/reduce_scatter | solution.py:291
  1637.5 232.2 %reduce-scatter.23.cloned.1.call-start = ((), (), s32[]{:S(2)}) async-start(), calls=%async_computation.25 | async-start | bytes 147456 | tf_op jit(solution)/shard_map/reduce_scatter | solution.py:313
  1640.1 512.8 %reduce-scatter.25.cloned.1.call-start = ((), (), s32[]{:S(2)}) async-start(), calls=%async_computation.26 | async-start | bytes 20971520 | tf_op jit(solution)/shard_map/reduce_scatter | solution.py:217
  1661.8 774.5 %reduce-scatter.27.cloned.1.call-start = ((), (), s32[]{:S(2)}) async-start(), calls=%async_computation.27 | async-start | bytes 20971520 | tf_op jit(solution)/shard_map/reduce_scatter | solution.py:220
  1682.9 1036.7 %reduce-scatter.29.cloned.1.call-start = ((), (), s32[]{:S(2)}) async-start(), calls=%async_computation.28 | async-start | bytes 20971520 | tf_op jit(solution)/shard_map/reduce_scatter | solution.py:223
  1706.6 125.6 %copy-start.51 = (f32[2048]{0:T(1024)S(1)}, f32[2048]{0:T(1024)}, u32[]{:S(2)}) copy-start(f32[2048]{0:T(1024)} %param.19) | copy-start | bytes 24580
  1706.6 125.6 %copy-start.68 = (f32[256]{0:T(256)S(1)}, f32[256]{0:T(256)}, u32[]{:S(2)}) copy-start(f32[256]{0:T(256)} %copy-done.67) | copy-start | bytes 3076
  1713.7 120.8 %copy-start.66 = (bf16[2048]{0:T(1024)(128)(2,1)S(1)}, bf16[2048]{0:T(1024)(128)(2,1)}, u32[]{:S(2)}) copy-start(bf16[2048]{0:T(1024)(128)(2,1)} %get-tuple-element.18) | copy-start | bytes 12292
  1713.7 120.8 %copy-start.83 = (bf16[128]{0:T(256)(128)(2,1)S(1)}, bf16[128]{0:T(256)(128)(2,1)}, u32[]{:S(2)}) copy-start(bf16[128]{0:T(256)(128)(2,1)} %get-tuple-element.16) | copy-start | bytes 772
  1713.7 120.8 %copy-start.84 = (bf16[128]{0:T(256)(128)(2,1)S(1)}, bf16[128]{0:T(256)(128)(2,1)}, u32[]{:S(2)}) copy-start(bf16[128]{0:T(256)(128)(2,1)} %get-tuple-element.14) | copy-start | bytes 772
  1713.7 178.9 %copy-start.74 = (f32[256]{0:T(256)S(1)}, f32[256]{0:T(256)}, u32[]{:S(2)}) copy-start(f32[256]{0:T(256)} %copy-done.73) | copy-start | bytes 3076
  1713.7 179.0 %copy-start.76 = (f32[256]{0:T(256)S(1)}, f32[256]{0:T(256)}, u32[]{:S(2)}) copy-start(f32[256]{0:T(256)} %copy-done.75) | copy-start | bytes 3076
  (81 other events, 600.0 us)
Sparse Core Ops, SparseCore 0:
  12.7 83.4 all-gather.5
  145.6 75.2 reduce-scatter.10
  222.5 286.7 all-gather.9
  510.7 284.4 all-gather.7
  796.6 284.9 all-gather.11
  1445.4 77.1 all-gather.13
  1579.7 39.5 reduce-scatter.14
  1622.6 41.1 reduce-scatter.16
  1667.0 41.1 reduce-scatter.18
  1711.3 41.1 reduce-scatter.20
  1755.3 76.7 reduce-scatter.12
  1835.6 34.0 reduce-scatter.22
  1872.1 280.7 reduce-scatter.24
  2155.1 281.1 reduce-scatter.26
  2438.5 281.0 reduce-scatter.28
where the time goes:
time: 2740 us; the launch traced here: 2730 us
  waiting for transfers between devices  1950 us (71%)
  matrix products  328 us (12%)
  local copies, waits for them, and re-layouts  201 us (7%)
  other arithmetic  184 us (7%)
  blocking collectives  33.9 us (1%)
    reduce_scatter x1, waiting for transfers between devices, per_device(): lax.psum_scatter(grad_up_local.astype(jnp.bfloat16), 'tensor', scatter_di...  277 us
    reduce_scatter x1, waiting for transfers between devices, per_device(): lax.psum_scatter(grad_down_local.astype(jnp.bfloat16), 'tensor', scatter_...  277 us
    all_gather x1, waiting for transfers between devices, per_device(): lax.all_gather(w_down, 'tensor', axis=1, tiled=True)  266 us
    all_gather x1, waiting for transfers between devices, per_device(): lax.all_gather(w_gate, 'tensor', axis=2, tiled=True)  266 us
    reduce_scatter x1, waiting for transfers between devices, per_device(): lax.psum_scatter(grad_gate_local.astype(jnp.bfloat16), 'tensor', scatter_...  255 us
    all_gather x1, waiting for transfers between devices, per_device(): lax.all_gather(w_up, 'tensor', axis=2, tiled=True)  88.1 us
    all_to_all x1, waiting for transfers between devices, per_device(): lax.all_to_all(input_sum.astype(jnp.bfloat16), 'dp', split_axis=0, concat...  86.3 us
    all_gather x1, waiting for transfers between devices, per_device(): gathered = lax.all_gather(normed, 'tensor', axis=0, tiled=True)  81 us
  transfers between devices with their start and end apart: 19, of which 14 were waited for; matrix products, arithmetic and copies ran while one was open for 17% of the time, Pallas kernels for 0%

commit v1 on v0

v1 whole, which is shorter than its diff:
```python
import functools

import jax
import jax.numpy as jnp
from jax import lax
from jax.experimental import pallas as pl
from jax.experimental.pallas import tpu as pltpu
from jax.sharding import PartitionSpec as P

EPS = 1e-06
THETA = 50000.0
NEG = -1e30


def rms_scale(values, gain):
    return values * lax.rsqrt(jnp.mean(values * values, axis=-1, keepdims=True) + EPS) * gain


def rotate(values):
    length = values.shape[-3]
    half_dim = values.shape[-1] // 2
    positions = jnp.arange(length).astype(jnp.float32)
    rates = THETA ** (-jnp.arange(half_dim).astype(jnp.float32) / half_dim)
    angles = positions[:, None] * rates[None, :]
    cosine = jnp.cos(angles)[:, None, :]
    sine = jnp.sin(angles)[:, None, :]
    first = values[..., :half_dim]
    second = values[..., half_dim:]
    return jnp.concatenate(
        [first * cosine - second * sine, second * cosine + first * sine], axis=-1
    )


def prepare(raw, gain):
    shaped = raw.reshape(raw.shape[0], -1, gain.shape[0])
    return rotate(rms_scale(shaped, gain))


def dot_nt(a, b):
    return lax.dot_general(a, b, (((1,), (1,)), ((), ())), preferred_element_type=jnp.float32)


def dot_nn(a, b):
    return jnp.dot(a, b, preferred_element_type=jnp.float32)


def largest_tile(total, limit, unit):
    best = unit
    for tile in range(unit, limit + 1, unit):
        if total % tile == 0:
            best = tile
    return best


def expert_kernel(
    sizes,
    first,
    table_ref,
    x_ref,
    c_ref,
    pick_ref,
    wg_ref,
    wu_ref,
    wd_ref,
    *rest,
):
    blocks, experts, slots, rows, width, extra, hidden, all_experts = sizes
    if first:
        acc_in = None
        y0_ref, y1_ref, g0_ref, g1_ref, acc_out = rest[:5]
        scratch = rest[5:]
    else:
        acc_in, y0_ref, y1_ref, g0_ref, g1_ref, acc_out = rest[:6]
        scratch = rest[6:]
    rows_s, crow_s, mrow_s, meta_s, aw_s, gg_s, gu_s, turn_s, acc_s, load_sem, store_sem = scratch
    step = pl.program_id(0)
    total = blocks * slots
    half = blocks // 2

    def load(e, slot):
        return pltpu.make_async_copy(acc_in.at[e], acc_s.at[slot], load_sem.at[slot])

    def store(e, slot):
        return pltpu.make_async_copy(acc_s.at[slot], acc_out.at[e], store_sem.at[slot])

    if not first:

        @pl.when(step == 0)
        def _():
            load(0, 0).start()

    @pl.when(step < blocks)
    def _():
        meta = x_ref[0, :, width:]
        picks = (dot_nt(pick_ref[...], meta) == 0.0).astype(jnp.bfloat16)
        at = pl.multiple_of(step * slots, slots)
        got = dot_nn(picks, x_ref[0]).astype(jnp.bfloat16)
        cot = dot_nn(picks, c_ref[0]).astype(jnp.bfloat16)
        for e in range(experts):
            part = slice(e * slots, (e + 1) * slots)
            rows_s[e, pl.ds(at, slots), :] = got[part, :width]
            mrow_s[e, pl.ds(at, slots), :] = got[part, width:]
            crow_s[e, pl.ds(at, slots), :] = cot[part]
        meta_s[step] = meta

    @pl.when((step >= blocks) & (step < blocks + experts))
    def _():
        e = step - blocks
        slot = lax.rem(e, 2)
        tile = largest_tile(total, 320, 16)
        expert = table_ref[0] + e
        wg = wg_ref[0]
        wu = wu_ref[0]
        wd = wd_ref[0]

        @pl.loop(0, total // tile)
        def _(m):
            ds = pl.ds(pl.multiple_of(m * tile, tile), tile)
            picked_rows = rows_s[e, ds, :]
            gate = dot_nn(picked_rows, wg)
            up = dot_nn(picked_rows, wu)
            grad_act = dot_nt(crow_s[e, ds, :], wd)
            meta = mrow_s[e, ds, :].astype(jnp.float32)
            column = lax.broadcasted_iota(jnp.int32, meta.shape, 1)
            wanted = (column == expert) | (column == expert + all_experts)
            weight = jnp.sum(jnp.where(wanted, meta, 0.0), axis=1, keepdims=True)
            sig = jax.nn.sigmoid(gate)
            silu = gate * sig
            act = silu * up
            g_pick = jnp.sum(act * grad_act, axis=1, keepdims=True)
            scaled = weight * grad_act
            aw_s[ds, :] = (weight * act).astype(jnp.bfloat16)
            gg_s[ds, :] = (scaled * up * sig * (1.0 + gate * (1.0 - sig))).astype(jnp.bfloat16)
            gu_s[ds, :] = (scaled * silu).astype(jnp.bfloat16)
            mrow_s[e, ds, :] = jnp.where(column == expert, g_pick, 0.0).astype(jnp.bfloat16)

        if not first:
            load(e, slot).wait()

            @pl.when(e >= 1)
            def _():
                store(e - 1, 1 - slot).wait()

            @pl.when(e + 1 < experts)
            def _():
                load(e + 1, 1 - slot).start()

        else:

            @pl.when(e >= 2)
            def _():
                store(e - 2, slot).wait()

        cols = largest_tile(width, 512, 128)
        for which, (left, right) in enumerate(((gg_s, rows_s), (gu_s, rows_s), (aw_s, crow_s))):
            turn_s[...] = left[...].T

            @pl.loop(0, width // cols)
            def _(n):
                ds = pl.ds(pl.multiple_of(n * cols, cols), cols)
                add = dot_nn(turn_s[...], right[e, :, ds])
                if first:
                    acc_s[slot, which, :, ds] = add
                else:
                    acc_s[slot, which, :, ds] = acc_s[slot, which, :, ds] + add

        store(e, slot).start()

        @pl.loop(0, total // tile)
        def _(m):
            ds = pl.ds(pl.multiple_of(m * tile, tile), tile)
            crow_s[e, ds, :] = dot_nn(aw_s[ds, :], wd).astype(jnp.bfloat16)
            back = dot_nt(gg_s[ds, :], wg) + dot_nt(gu_s[ds, :], wu)
            rows_s[e, ds, :] = back.astype(jnp.bfloat16)

    @pl.when(step >= blocks + experts)
    def _():
        order = step - blocks - experts
        b = table_ref[2 + blocks + jnp.where(order < half, order + half, order - half)]
        at = pl.multiple_of(b * slots, slots)
        picks = (dot_nt(meta_s[b], pick_ref[...]) == 0.0).astype(jnp.bfloat16)
        flat = (experts * slots, width)
        y = dot_nn(picks, crow_s[:, pl.ds(at, slots), :].reshape(flat)).astype(jnp.bfloat16)
        g = dot_nn(picks, rows_s[:, pl.ds(at, slots), :].reshape(flat)).astype(jnp.bfloat16)
        flat = (experts * slots, extra)
        p = dot_nn(picks, mrow_s[:, pl.ds(at, slots), :].reshape(flat)).astype(jnp.bfloat16)

        @pl.when(order < half)
        def _():
            y1_ref[0] = y
            g1_ref[0, :, :width] = g
            g1_ref[0, :, width:] = p

        @pl.when(order >= half)
        def _():
            y0_ref[0] = y
            g0_ref[0, :, :width] = g
            g0_ref[0, :, width:] = p

    @pl.when(step == 2 * blocks + experts - 1)
    def _():
        if first:
            store(experts - 2, (experts - 2) % 2).wait()
        store(experts - 1, (experts - 1) % 2).wait()


def expert_chunk(table, x, c, picks, wg, wu, wd, acc, slots, all_experts):
    blocks, rows, full = x.shape
    width = c.shape[2]
    extra = full - width
    experts, _, hidden = wg.shape
    total = blocks * slots
    half = blocks // 2
    first = acc is None
    sizes = (blocks, experts, slots, rows, width, extra, hidden, all_experts)

    def clip(v, top):
        return jnp.clip(v, 0, top)

    def block_at(i, table):
        return (jnp.minimum(i, blocks - 1), 0, 0)

    def cot_at(i, table):
        return (table[2 + jnp.minimum(i, blocks - 1)], table[1], 0)

    def expert_at(i, table):
        return (clip(i - blocks, experts - 1), 0, 0)

    def late(i, table):
        return (clip(i - blocks - experts, half - 1), 0, 0)

    def early(i, table):
        return (clip(i - blocks - experts - half, half - 1), 0, 0)

    in_specs = [
        pl.BlockSpec((1, rows, full), block_at),
        pl.BlockSpec((1, rows, width), cot_at),
        pl.BlockSpec(picks.shape, lambda i, table: (0, 0)),
        pl.BlockSpec((1, width, hidden), expert_at),
        pl.BlockSpec((1, width, hidden), expert_at),
        pl.BlockSpec((1, hidden, width), expert_at),
    ]
    args = [table, x, c, picks, wg, wu, wd]
    if not first:
        in_specs.append(pl.BlockSpec(memory_space=pl.ANY))
        args.append(acc)
    out_specs = [
        pl.BlockSpec((1, rows, width), early),
        pl.BlockSpec((1, rows, width), late),
        pl.BlockSpec((1, rows, full), early),
        pl.BlockSpec((1, rows, full), late),
        pl.BlockSpec(memory_space=pl.ANY),
    ]
    out_shape = [
        jax.ShapeDtypeStruct((half, rows, width), jnp.bfloat16),
        jax.ShapeDtypeStruct((half, rows, width), jnp.bfloat16),
        jax.ShapeDtypeStruct((half, rows, full), jnp.bfloat16),
        jax.ShapeDtypeStruct((half, rows, full), jnp.bfloat16),
        jax.ShapeDtypeStruct((experts, 3, hidden, width), jnp.float32),
    ]
    scratch = [
        pltpu.VMEM((experts, total, width), jnp.bfloat16),
        pltpu.VMEM((experts, total, width), jnp.bfloat16),
        pltpu.VMEM((experts, total, extra), jnp.bfloat16),
        pltpu.VMEM((blocks, rows, extra), jnp.bfloat16),
        pltpu.VMEM((total, hidden), jnp.bfloat16),
        pltpu.VMEM((total, hidden), jnp.bfloat16),
        pltpu.VMEM((total, hidden), jnp.bfloat16),
        pltpu.VMEM((hidden, total), jnp.bfloat16),
        pltpu.VMEM((2, 3, hidden, width), jnp.float32),
        pltpu.SemaphoreType.DMA((2,)),
        pltpu.SemaphoreType.DMA((2,)),
    ]
    flops = 2 * experts * total * width * (hidden * 9 + 4 * rows)
    return pl.pallas_call(
        functools.partial(expert_kernel, sizes, first),
        grid_spec=pltpu.PrefetchScalarGridSpec(
            num_scalar_prefetch=1,
            grid=(2 * blocks + experts,),
            in_specs=in_specs,
            out_specs=out_specs,
            scratch_shapes=scratch,
        ),
        out_shape=out_shape,
        input_output_aliases={} if first else {7: 4},
        compiler_params=pltpu.CompilerParams(
            dimension_semantics=("arbitrary",), vmem_limit_bytes=66_000_000
        ),
        cost_estimate=pl.CostEstimate(
            flops=flops, bytes_accessed=4 * blocks * rows * full * 2 + 40_000_000, transcendentals=0
        ),
        name="experts",
    )(*args)


def wide(values):
    return values.astype(jnp.float32)


def low(values):
    return values.astype(jnp.bfloat16)


def tie(*values):
    return lax.optimization_barrier(values)


def ring_sum(values, count):
    total = wide(values)
    for step in range(1, count):
        pairs = [(i, (i + step) % count) for i in range(count)]
        total = total + wide(lax.ppermute(low(values), "tensor", pairs))
    return total


class Plane:
    def __init__(self, count):
        self.outer = count // 4
        everyone = range(count)
        self.core = [(i, i ^ 1) for i in everyone]
        self.inner = [(i, i ^ 2) for i in everyone]
        self.count = count

    def pull(self, values, k):
        pairs = [((i + 4 * k) % self.count, i) for i in range(self.count)]
        return lax.ppermute(values, "dp", pairs)

    def push(self, values, k):
        pairs = [(i, (i + 4 * k) % self.count) for i in range(self.count)]
        return lax.ppermute(values, "dp", pairs)

    def swap_inner(self, values):
        return lax.ppermute(values, "dp", self.inner)

    def swap_core(self, values):
        return lax.ppermute(values, "dp", self.core)

    def gather(self, own):
        half = own.shape[0] // 2
        near = self.swap_inner(own)
        far = [self.pull(own, k) for k in range(1, self.outer)]
        mine = [own, near]
        for k in range(1, self.outer):
            top = self.pull(near[:half], k)
            bottom = self.swap_inner(far[k - 1][half:])
            mine += [far[k - 1], jnp.concatenate([top, bottom], axis=0)]
        other = [self.swap_core(part) for part in mine]
        return mine + other

    def fold_core(self, same, other):
        return low(wide(same) + wide(self.swap_core(other)))

    def fold_diagonal(self, both):
        half = both.shape[1] // 2
        near = wide(both[1])
        fars = []
        for k in range(1, self.outer):
            diagonal = both[2 * k + 1]
            top = self.push(diagonal[:half], k)
            bottom = self.swap_inner(diagonal[half:])
            near = near + wide(jnp.concatenate([top, jnp.zeros_like(top)], axis=0))
            fars.append(
                low(wide(both[2 * k]) + wide(jnp.concatenate([jnp.zeros_like(bottom), bottom], axis=0)))
            )
        return both[0], low(near), fars

    def fold_rest(self, own, near, fars):
        total = wide(own) + wide(self.swap_inner(near))
        for k, far in enumerate(fars):
            total = total + wide(self.push(far, k + 1))
        return total

    def tables(self):
        here = lax.axis_index("dp")
        outer, rest = here // 4, lax.rem(here, 4)
        core, inner = lax.rem(rest, 2), rest // 2
        half = self.count // 2
        place = jnp.arange(self.count)
        k, b, c = place // 4, place // 2 % 2, place % 2
        to_relative = (c ^ core) * half + lax.rem(k - outer + self.outer, self.outer) * 2 + (b ^ inner)
        c, k, b = place // half, place % half // 2, place % 2
        to_absolute = lax.rem(k + outer, self.outer) * 4 + (b ^ inner) * 2 + (c ^ core)
        return to_relative.astype(jnp.int32), to_absolute.astype(jnp.int32)


def per_device(
    tokens,
    lengths,
    routes,
    attn_gain,
    w_query,
    w_key,
    w_value,
    w_out,
    q_gain,
    k_gain,
    ffn_gain,
    router_weight,
    w_gate,
    w_up,
    w_down,
    cotangent,
):
    tensor_count = lax.axis_size("tensor")
    data_count = lax.axis_size("dp")
    tensor_rank = lax.axis_index("tensor")
    block_rows = tokens.shape[1]
    width = tokens.shape[2]
    full_length = block_rows * tensor_count
    route_count = routes.shape[2]
    local_experts = w_gate.shape[0]
    all_experts = local_experts * data_count
    head_dim = q_gain.shape[0]
    local_width = w_query.shape[1]
    capacity = max(2, (block_rows * route_count * 5 + 4 * all_experts - 1) // (4 * all_experts))
    query_rows = min(512, full_length)
    scale = head_dim ** (-0.5)
    own_start = tensor_rank * block_rows
    token_values = tokens[0].astype(jnp.float32)
    seq_length = lengths[0]
    own_valid = (own_start + jnp.arange(block_rows) < seq_length).astype(jnp.float32)
    key_valid = jnp.arange(full_length) < seq_length
    normed = rms_scale(token_values, attn_gain).astype(jnp.bfloat16)
    gathered = lax.all_gather(normed, "tensor", axis=0, tiled=True)
    plane = Plane(data_count)
    cot_all = jnp.stack(plane.gather(cotangent[0]))
    query_unrotated = jnp.dot(gathered, w_query, preferred_element_type=jnp.float32)
    key_raw = jnp.dot(gathered, w_key, preferred_element_type=jnp.float32)
    value_raw = jnp.dot(gathered, w_value, preferred_element_type=jnp.float32)
    query_low = prepare(query_unrotated, q_gain).astype(jnp.bfloat16)
    key_low = prepare(key_raw, k_gain).astype(jnp.bfloat16)
    value_low = value_raw.astype(jnp.bfloat16).reshape(full_length, -1, head_dim)

    def block_scores(query_block):
        scores = (
            jnp.einsum("qhd,khd->hqk", query_block, key_low, preferred_element_type=jnp.float32)
            * scale
        )
        return jnp.where(key_valid[None, None, :], scores, NEG)

    mixed_parts = []
    log_totals = []
    for start in range(0, full_length, query_rows):
        scores = block_scores(query_low[start : start + query_rows])
        row_peak = jnp.max(scores, axis=-1, keepdims=True)
        powers = jnp.exp(scores - row_peak)
        total = jnp.sum(powers, axis=-1, keepdims=True)
        weights = (powers / total).astype(jnp.bfloat16)
        mixed_parts.append(
            jnp.einsum("hqk,khd->qhd", weights, value_low, preferred_element_type=jnp.float32)
        )
        log_totals.append(row_peak + jnp.log(total))
    attended = (
        jnp.concatenate(mixed_parts, axis=0).reshape(full_length, local_width).astype(jnp.bfloat16)
    )
    attn_own = lax.psum_scatter(
        jnp.einsum("lh,dh->ld", attended, w_out, preferred_element_type=jnp.float32).astype(
            jnp.bfloat16
        ),
        "tensor",
        scatter_dimension=0,
        tiled=True,
    ).astype(jnp.float32)
    residual = token_values + own_valid[:, None] * attn_own
    moe_own = rms_scale(residual, ffn_gain).astype(jnp.bfloat16)
    router_logits = jnp.dot(moe_own, router_weight, preferred_element_type=jnp.float32)
    own_probs = jax.nn.softmax(router_logits, axis=-1)
    own_routes = lax.dynamic_slice_in_dim(routes[0], own_start, block_rows, 0)
    onehot = own_routes[:, :, None] == jnp.arange(all_experts)[None, None, :]
    named = jnp.any(onehot, axis=1) & (own_valid[:, None] > 0.0)
    named_low = named.astype(jnp.bfloat16)
    before = jnp.arange(block_rows)[:, None] > jnp.arange(block_rows)[None, :]
    order = jnp.dot(before.astype(jnp.bfloat16), named_low, preferred_element_type=jnp.float32)
    place = jnp.where(named, order, -1.0).astype(jnp.bfloat16)
    weight = jnp.where(named, own_probs, 0.0)
    weight_high = weight.astype(jnp.bfloat16)
    weight_low = (weight - weight_high.astype(jnp.float32)).astype(jnp.bfloat16)
    used = 3 * all_experts + 1
    extra = (used + 127) // 128 * 128
    meta = jnp.concatenate(
        [
            weight_high,
            weight_low,
            place,
            jnp.ones((block_rows, 1), jnp.bfloat16),
            jnp.zeros((block_rows, extra - used), jnp.bfloat16),
        ],
        axis=1,
    )
    slots = (capacity + 15) // 16 * 16
    first_expert = lax.axis_index("dp") * local_experts
    slot_row = jnp.arange(local_experts * slots)[:, None]
    slot_column = jnp.arange(extra)[None, :]
    picks = jnp.where(
        slot_column == 2 * all_experts + first_expert + slot_row // slots,
        1.0,
        jnp.where(slot_column == 3 * all_experts, -(slot_row % slots).astype(jnp.float32), 0.0),
    ).astype(jnp.bfloat16)
    packed = jnp.concatenate([moe_own, meta], axis=1)
    to_relative, to_absolute = plane.tables()
    sums = None
    shift_in = [
        [((i + step) % tensor_count, i) for i in range(tensor_count)] for step in range(tensor_count)
    ]
    shift_out = [
        [(i, (i + step) % tensor_count) for i in range(tensor_count)] for step in range(tensor_count)
    ]
    gathered_rows = [
        lax.all_gather(
            packed if step == 0 else lax.ppermute(packed, "tensor", shift_in[step]), "dp", axis=0
        )
        for step in range(tensor_count)
    ]
    out_parts = []
    cores = {}
    ends = {}
    grad_parts = []
    for step in range(tensor_count):
        x_all = gathered_rows[step]
        if step >= 2:
            x_all, cores[step - 2] = tie(x_all, cores[step - 2])
        if step >= 3:
            x_all, ends[step - 3] = tie(x_all, ends[step - 3])
        here = lax.rem(tensor_rank + step, tensor_count)
        head = jnp.stack([first_expert, here]).astype(jnp.int32)
        table = jnp.concatenate([head, to_relative, to_absolute])
        y0, y1, g0, g1, sums = expert_chunk(
            table, x_all, cot_all, picks, w_gate, w_up, w_down, sums, slots, all_experts
        )
        out_parts.append((y0, y1))
        cores[step] = plane.fold_core(g0, g1)
        if step >= 1:
            ends[step - 1] = plane.fold_diagonal(cores[step - 1])
    ends[tensor_count - 1] = plane.fold_diagonal(cores[tensor_count - 1])
    for step in range(tensor_count):
        part = plane.fold_rest(*ends[step])
        if step > 0:
            part = wide(lax.ppermute(low(part), "tensor", shift_out[step]))
        grad_parts.append(part)
    grad_gate = jnp.swapaxes(sums[:, 0], 1, 2)
    grad_up = jnp.swapaxes(sums[:, 1], 1, 2)
    grad_down = sums[:, 2]
    grad_sum = sum(grad_parts[1:], grad_parts[0])
    grad_moe = grad_sum[:, :width]
    grad_probs = grad_sum[:, width : width + all_experts]
    grad_own = lax.dynamic_slice_in_dim(cotangent[0], own_start, block_rows, 0).astype(jnp.float32)
    grad_logits = (
        own_probs * (grad_probs - jnp.sum(own_probs * grad_probs, axis=-1, keepdims=True))
    ).astype(jnp.bfloat16)
    grad_moe = grad_moe + jnp.einsum(
        "re,de->rd", grad_logits, router_weight, preferred_element_type=jnp.float32
    )
    router_part = jnp.einsum("rd,re->de", moe_own, grad_logits, preferred_element_type=jnp.float32)
    ffn_pull = jax.vjp(rms_scale, residual, ffn_gain)[1]
    grad_res_norm, ffn_part = ffn_pull(grad_moe)
    grad_residual = grad_own + grad_res_norm
    grad_attn = (grad_residual * own_valid[:, None]).astype(jnp.bfloat16)
    out_cores = [plane.fold_core(y0, y1) for y0, y1 in out_parts]
    grad_attn, out_cores = tie(grad_attn, out_cores)
    grad_attn_all = lax.all_gather(grad_attn, "tensor", axis=0, tiled=True)
    out_ends = [plane.fold_diagonal(both) for both in out_cores]
    grad_attn_all, out_ends = tie(grad_attn_all, out_ends)
    grad_mixed = jnp.dot(grad_attn_all, w_out, preferred_element_type=jnp.float32).astype(
        jnp.bfloat16
    )
    grad_mixed = grad_mixed.reshape(full_length, -1, head_dim)
    out_part = jnp.einsum("ld,lh->dh", grad_attn_all, attended, preferred_element_type=jnp.float32)
    grad_query_parts = []
    grad_keys = jnp.zeros(key_low.shape, jnp.float32)
    grad_values = jnp.zeros(value_low.shape, jnp.float32)
    for order, start in enumerate(range(0, full_length, query_rows)):
        query_block = query_low[start : start + query_rows]
        grad_block = grad_mixed[start : start + query_rows]
        probs_block = jnp.exp(block_scores(query_block) - log_totals[order])
        probs_low = probs_block.astype(jnp.bfloat16)
        grad_values = grad_values + jnp.einsum(
            "hqk,qhd->khd", probs_low, grad_block, preferred_element_type=jnp.float32
        )
        grad_probs_block = jnp.einsum(
            "qhd,khd->hqk", grad_block, value_low, preferred_element_type=jnp.float32
        )
        delta = jnp.sum(probs_block * grad_probs_block, axis=-1, keepdims=True)
        grad_scores = (probs_block * (grad_probs_block - delta)).astype(jnp.bfloat16)
        grad_query_parts.append(
            jnp.einsum("hqk,khd->qhd", grad_scores, key_low, preferred_element_type=jnp.float32)
            * scale
        )
        grad_keys = (
            grad_keys
            + jnp.einsum(
                "hqk,qhd->khd", grad_scores, query_block, preferred_element_type=jnp.float32
            )
            * scale
        )
    grad_queries = jnp.concatenate(grad_query_parts, axis=0)
    query_pull = jax.vjp(prepare, query_unrotated, q_gain)[1]
    grad_query_raw, q_part = query_pull(grad_queries)
    key_pull = jax.vjp(prepare, key_raw, k_gain)[1]
    grad_key_raw, k_part = key_pull(grad_keys)
    grad_q_low = grad_query_raw.astype(jnp.bfloat16)
    grad_k_low = grad_key_raw.astype(jnp.bfloat16)
    grad_v_low = grad_values.reshape(full_length, local_width).astype(jnp.bfloat16)
    query_part = jnp.einsum("ld,lh->dh", gathered, grad_q_low, preferred_element_type=jnp.float32)
    key_part = jnp.einsum("ld,lh->dh", gathered, grad_k_low, preferred_element_type=jnp.float32)
    value_part = jnp.einsum("ld,lh->dh", gathered, grad_v_low, preferred_element_type=jnp.float32)
    from_query = jnp.einsum("lh,dh->ld", grad_q_low, w_query, preferred_element_type=jnp.float32)
    from_key = jnp.einsum("lh,dh->ld", grad_k_low, w_key, preferred_element_type=jnp.float32)
    from_value = jnp.einsum("lh,dh->ld", grad_v_low, w_value, preferred_element_type=jnp.float32)
    output = residual
    for step in range(tensor_count):
        part = plane.fold_rest(*out_ends[step])
        if step > 0:
            part = wide(lax.ppermute(low(part), "tensor", shift_out[step]))
        output = output + part
    output = low(output)
    early = jnp.concatenate(
        [
            low(out_part),
            low(value_part),
            low(ring_sum(jnp.concatenate([router_part, ffn_part[:, None]], axis=1), tensor_count)),
        ],
        axis=1,
    )
    early = wide(lax.psum_scatter(early, "dp", scatter_dimension=0, tiled=True))
    grad_normed = wide(
        lax.psum_scatter(
            low(from_query + from_key + from_value), "tensor", scatter_dimension=0, tiled=True
        )
    )
    attn_pull = jax.vjp(rms_scale, token_values, attn_gain)[1]
    grad_tok_norm, attn_part = attn_pull(grad_normed)
    grad_tokens = (grad_residual + grad_tok_norm).astype(jnp.bfloat16)
    piece = head_dim // data_count
    gains = jnp.stack([q_part, k_part]).reshape(2, data_count, piece)
    gains = jnp.pad(gains, ((0, 0), (0, 0), (0, width // data_count - piece)))
    small = jnp.concatenate([attn_part[:, None], gains.reshape(2, width).T], axis=1)
    late = jnp.concatenate(
        [low(query_part), low(key_part), low(ring_sum(small, tensor_count))], axis=1
    )
    late = wide(lax.psum_scatter(late, "dp", scatter_dimension=0, tiled=True))
    end = 2 * local_width
    return (
        output[None],
        grad_tokens[None],
        late[:, end],
        late[:, :local_width],
        late[:, local_width:end],
        early[:, local_width:end],
        early[:, :local_width],
        late[:piece, end + 1],
        late[:piece, end + 2],
        early[:, end + all_experts],
        early[:, end : end + all_experts],
        grad_gate,
        grad_up,
        grad_down,
    )


def solution(mesh):
    return jax.shard_map(
        per_device,
        mesh=mesh,
        in_specs=(
            P("dp", "tensor", None),
            P("dp"),
            P("dp", None, None),
            P(),
            P(None, "tensor"),
            P(None, "tensor"),
            P(None, "tensor"),
            P(None, "tensor"),
            P(),
            P(),
            P(),
            P(),
            P("dp", None, "tensor"),
            P("dp", None, "tensor"),
            P("dp", "tensor", None),
            P("dp", None, None),
        ),
        out_specs=(
            P("dp", "tensor", None),
            P("dp", "tensor", None),
            P("dp"),
            P("dp", "tensor"),
            P("dp", "tensor"),
            P("dp", "tensor"),
            P("dp", "tensor"),
            P("dp"),
            P("dp"),
            P("dp"),
            P("dp", None),
            P("dp", None, "tensor"),
            P("dp", None, "tensor"),
            P("dp", "tensor", None),
        ),
        check_vma=False,
    )
```

time: 2740 us -> 1590 us (0.58)
  waiting for transfers between devices: 1950 us -> 842 us
  Pallas kernels: 0 us -> 290 us
  matrix products: 328 us -> 96.7 us
  local copies, waits for them, and re-layouts: 201 us -> 128 us
  other arithmetic: 184 us -> 132 us
  starting transfers between devices: 23.3 us -> 66.4 us
  blocking collectives: 33.9 us -> 0 us
    reduce_scatter x9 -> x3, waiting for transfers between devices: 941 us -> 38.4 us  [the longest x1 38.3 us: per_device(): lax.psum_scatter(low(from_query + from_key + from_value), 'tensor', scatt...]
    all_gather x3 -> x4, waiting for transfers between devices: 620 us -> 0.01 us  [per_device(): lax.all_gather(packed if step == 0 else lax.ppermute(packed, 'tensor', sh...]
    ppermute x0 -> x63, waiting for transfers between devices: none -> 597 us  [the longest x18 324 us: swap_inner(): return lax.ppermute(values, 'dp', self.inner)]
    pallas_call x0 -> x4, Pallas kernels: none -> 290 us  [expert_chunk(): pl.pallas_call(functools.partial(expert_kernel, sizes, first), grid_spec=...]
    all_to_all x4 -> x0, waiting for transfers between devices: 224 us -> none  [the longest x1 86.3 us: per_device(): lax.all_to_all(input_sum.astype(jnp.bfloat16), 'dp', split_axis=0, concat...]
    dot_general x12 -> x2, matrix products: 210 us -> 0.7 us  [the longest x1 0.44 us: per_device(): jnp.dot(moe_own, router_weight, preferred_element_type=jnp.float32)]
    gather x5 -> x0, local copies, waits for them, and re-layouts: 103 us -> none  [the longest x1 23 us: per_device(): grad_padded[row_slots]]
    reduce_scatter x1, waiting for transfers between devices: 0.02 us -> 74.1 us  [per_device(): lax.psum_scatter(jnp.einsum('lh,dh->ld', attended, w_out, preferred_eleme...]
  transfers between devices with their start and end apart: 19 -> 73, of which waited for: 14 -> 33; matrix products, arithmetic and copies ran while one was open for 17% -> 13% of each run, Pallas kernels for 0% -> 18%
where the time goes in v1:
time: 1590 us; the launch traced here: 1570 us
  waiting for transfers between devices  842 us (53%)
  Pallas kernels  290 us (18%)
  other arithmetic  132 us (8%)
  local copies, waits for them, and re-layouts  128 us (8%)
  matrix products  96.7 us (6%)
  starting transfers between devices  66.4 us (4%)
  between operations  16.8 us (1%)
    ppermute x18, waiting for transfers between devices, swap_inner(): return lax.ppermute(values, 'dp', self.inner)  324 us
    pallas_call x4, Pallas kernels, expert_chunk(): pl.pallas_call(functools.partial(expert_kernel, sizes, first), grid_spec=...  290 us
    ppermute x3, waiting for transfers between devices, per_device(): lax.ppermute(packed, 'tensor', shift_in[step])  96.4 us
    all_gather x1, waiting for transfers between devices, per_device(): gathered = lax.all_gather(normed, 'tensor', axis=0, tiled=True)  81 us
    reduce_scatter x1, waiting for transfers between devices, per_device(): lax.psum_scatter(jnp.einsum('lh,dh->ld', attended, w_out, preferred_eleme...  74.1 us
    convert_element_type x26, other arithmetic, low(): return values.astype(jnp.bfloat16)  71.4 us
    ppermute x16, waiting for transfers between devices, push(): return lax.ppermute(values, 'dp', pairs)  70.2 us
    unnamed x255, local copies, waits for them, and re-layouts  63.1 us
  transfers between devices with their start and end apart: 73, of which 33 were waited for; matrix products, arithmetic and copies ran while one was open for 13% of the time, Pallas kernels for 18%

profile of v1, /device:TPU:0, one launch (start us, length us, event | category | flops | bytes accessed | tf_op | source)
XLA Modules:
  0.0 1571.2 jit_solution(7995822248700288448)
XLA Ops:
  15.1 81.0 %all-gather.11.cloned.1.call-done = bf16[1024,2048]{1,0:T(8,128)(2,1)} async-done(((bf16[256,2048]{1,0:T(8,128)(2,1)}), bf16[1024,2048]{1,0:T(8,128)(2,1)}) %all-gather.11.cloned.1.call-update) | async-done | bytes 4194320 | tf_op jit(solution)/shard_map/all_gather | solution.py:424
  143.8 74.1 %reduce-scatter.5.cloned.1.call-done = bf16[256,2048]{1,0:T(8,128)(2,1)} async-done(((bf16[1024,2048]{1,0:T(8,128)(2,1)}), bf16[256,2048]{1,0:T(8,128)(2,1)}) %reduce-scatter.5.cloned.1.call-update) | async-done | bytes 1048592 | tf_op jit(solution)/shard_map/reduce_scatter | solution.py:456
  227.0 24.3 %collective-permute-done.1 = bf16[256,2176]{1,0:T(8,128)(2,1)S(1)} collective-permute-done((bf16[256,2176]{1,0:T(8,128)(2,1)}, bf16[256,2176]{1,0:T(8,128)(2,1)S(1)}, u32[]{:S(2)}, u32[]{:S(2)}) %collective-permute-start.1) | collective-permute-done | bytes 1114144 | tf_op jit(solution)/shard_map/ppermute | solution.py:510
  254.9 47.9 %collective-permute-done.21 = bf16[256,2176]{1,0:T(8,128)(2,1)S(1)} collective-permute-done((bf16[256,2176]{1,0:T(8,128)(2,1)S(1)}, bf16[256,2176]{1,0:T(8,128)(2,1)S(1)}, u32[]{:S(2)}, u32[]{:S(2)}) %collective-permute-start.21) | collective-permute-done | bytes 1114144 | tf_op jit(solution)/shard_map/ppermute | solution.py:510
  306.7 148.0 %collective-permute-done.2 = bf16[1024,2048]{1,0:T(8,128)(2,1)S(1)} collective-permute-done((bf16[1024,2048]{1,0:T(8,128)(2,1)}, bf16[1024,2048]{1,0:T(8,128)(2,1)S(1)}, u32[]{:S(2)}, u32[]{:S(2)}) %collective-permute-start.2) | collective-permute-done | bytes 4194336 | tf_op jit(solution)/shard_map/ppermute | solution.py:333
  468.9 31.9 %collective-permute-done.4 = bf16[512,2048]{1,0:T(8,128)(2,1)S(1)} collective-permute-done((bf16[512,2048]{1,0:T(8,128)(2,1)}, bf16[512,2048]{1,0:T(8,128)(2,1)S(1)}, u32[]{:S(2)}, u32[]{:S(2)}) %collective-permute-start.4) | collective-permute-done | bytes 2097184 | tf_op jit(solution)/shard_map/ppermute | solution.py:326
  530.2 24.3 %collective-permute-done = bf16[256,2176]{1,0:T(8,128)(2,1)S(1)} collective-permute-done((bf16[256,2176]{1,0:T(8,128)(2,1)S(1)}, bf16[256,2176]{1,0:T(8,128)(2,1)S(1)}, u32[]{:S(2)}, u32[]{:S(2)}) %collective-permute-start) | collective-permute-done | bytes 1114144 | tf_op jit(solution)/shard_map/ppermute | solution.py:510
  560.5 72.0 %experts.4 = (bf16[4,256,2048]{2,1,0:T(8,128)(2,1)}, bf16[4,256,2048]{2,1,0:T(8,128)(2,1)}, bf16[4,256,2176]{2,1,0:T(8,128)(2,1)}, bf16[4,256,2176]{2,1,0:T(8,128)(2,1)}, f32[4,3,256,2048]{3,2,1,0:T(8,128)}) custom-call(s32[18]{0:T(128)} %get-tuple-element.236.table_ref, bf16[8,256,2176]{2,1,0:T(8,128)(2,1)} %bitcast.314, ...), custom_call_target="tpu_custom_call" | custom-call | flops 34896609280 | bytes 75651584 | tf_op jit(solution)/shard_map/experts/pallas_call | solution.py:275
  633.7 72.8 %experts.5 = (bf16[4,256,2048]{2,1,0:T(8,128)(2,1)}, bf16[4,256,2048]{2,1,0:T(8,128)(2,1)}, bf16[4,256,2176]{2,1,0:T(8,128)(2,1)}, bf16[4,256,2176]{2,1,0:T(8,128)(2,1)}, f32[4,3,256,2048]{3,2,1,0:T(8,128)}) custom-call(s32[18]{0:T(128)} %get-tuple-element.237.table_ref, bf16[8,256,2176]{2,1,0:T(8,128)(2,1)} %bitcast.313, ...), custom_call_target="tpu_custom_call", output_to_operand_aliasing={{4}: (7, {})} | custom-call | flops 34896609280 | bytes 75651584 | tf_op jit(solution)/shard_map/experts/pallas_call | solution.py:275
  717.8 72.4 %experts.6 = (bf16[4,256,2048]{2,1,0:T(8,128)(2,1)}, bf16[4,256,2048]{2,1,0:T(8,128)(2,1)}, bf16[4,256,2176]{2,1,0:T(8,128)(2,1)}, bf16[4,256,2176]{2,1,0:T(8,128)(2,1)}, f32[4,3,256,2048]{3,2,1,0:T(8,128)}) custom-call(s32[18]{0:T(128)} %get-tuple-element.235.table_ref, bf16[8,256,2176]{2,1,0:T(8,128)(2,1)} %bitcast.312, ...), custom_call_target="tpu_custom_call", output_to_operand_aliasing={{4}: (7, {})} | custom-call | flops 34896609280 | bytes 75651584 | tf_op jit(solution)/shard_map/experts/pallas_call | solution.py:275
  803.1 72.7 %experts.7 = (bf16[4,256,2048]{2,1,0:T(8,128)(2,1)}, bf16[4,256,2048]{2,1,0:T(8,128)(2,1)}, bf16[4,256,2176]{2,1,0:T(8,128)(2,1)}, bf16[4,256,2176]{2,1,0:T(8,128)(2,1)}, f32[4,3,256,2048]{3,2,1,0:T(8,128)}) custom-call(s32[18]{0:T(128)} %get-tuple-element.238.table_ref, bf16[8,256,2176]{2,1,0:T(8,128)(2,1)} %bitcast.315, ...), custom_call_target="tpu_custom_call", output_to_operand_aliasing={{4}: (7, {})} | custom-call | flops 34896609280 | bytes 75651584 | tf_op jit(solution)/shard_map/experts/pallas_call | solution.py:275
  879.7 7.9 add_convert_fusion.8
  906.1 8.3 collective-permute-done.23
  914.4 19.1 %collective-permute-done.25 = bf16[128,2176]{1,0:T(8,128)(2,1)} collective-permute-done((bf16[128,2176]{1,0:T(8,128)(2,1)}, bf16[128,2176]{1,0:T(8,128)(2,1)}, u32[]{:S(2)}, u32[]{:S(2)}) %collective-permute-start.25) | collective-permute-done | bytes 557088 | tf_op jit(solution)/shard_map/ppermute | solution.py:333
  938.8 10.2 collective-permute-done.29
  955.9 19.7 %collective-permute-done.31 = bf16[128,2176]{1,0:T(8,128)(2,1)} collective-permute-done((bf16[128,2176]{1,0:T(8,128)(2,1)S(1)}, bf16[128,2176]{1,0:T(8,128)(2,1)}, u32[]{:S(2)}, u32[]{:S(2)}) %collective-permute-start.31) | collective-permute-done | bytes 557088 | tf_op jit(solution)/shard_map/ppermute | solution.py:333
  981.2 21.8 %collective-permute-done.26 = bf16[256,2176]{1,0:T(8,128)(2,1)S(1)} collective-permute-done((bf16[256,2176]{1,0:T(8,128)(2,1)S(1)}, bf16[256,2176]{1,0:T(8,128)(2,1)S(1)}, u32[]{:S(2)}, u32[]{:S(2)}) %collective-permute-start.26) | collective-permute-done | bytes 1114144 | tf_op jit(solution)/shard_map/ppermute | solution.py:330
  1006.6 20.2 %collective-permute-done.32 = bf16[256,2176]{1,0:T(8,128)(2,1)S(1)} collective-permute-done((bf16[256,2176]{1,0:T(8,128)(2,1)S(1)}, bf16[256,2176]{1,0:T(8,128)(2,1)S(1)}, u32[]{:S(2)}, u32[]{:S(2)}) %collective-permute-start.32) | collective-permute-done | bytes 1114144 | tf_op jit(solution)/shard_map/ppermute | solution.py:330
  1047.7 8.5 collective-permute-done.20
  1056.2 40.8 %collective-permute-done.27 = bf16[256,2176]{1,0:T(8,128)(2,1)S(1)} collective-permute-done((bf16[256,2176]{1,0:T(8,128)(2,1)S(1)}, bf16[256,2176]{1,0:T(8,128)(2,1)S(1)}, u32[]{:S(2)}, u32[]{:S(2)}) %collective-permute-start.27) | collective-permute-done | bytes 1114144 | tf_op jit(solution)/shard_map/ppermute | solution.py:538
  1154.3 51.4 %all-gather.13.cloned.1.call-done = bf16[1024,2048]{1,0:T(8,128)(2,1)} async-done(((bf16[256,2048]{1,0:T(8,128)(2,1)}), bf16[1024,2048]{1,0:T(8,128)(2,1)}) %all-gather.13.cloned.1.call-update) | async-done | bytes 4194320 | tf_op jit(solution)/shard_map/all_gather | solution.py:560
  1222.8 9.9 multiply_reduce_fusion.1
  1232.8 8.6 multiply_convert_fusion.1
  1285.8 10.1 collective-permute-done.62
  1296.0 15.1 collective-permute-done.61
  1325.9 38.3 %reduce-scatter.7.cloned.1.call-done = bf16[256,2048]{1,0:T(8,128)(2,1)} async-done(((bf16[1024,2048]{1,0:T(8,128)(2,1)}), bf16[256,2048]{1,0:T(8,128)(2,1)}) %reduce-scatter.7.cloned.1.call-update) | async-done | bytes 1048592 | tf_op jit(solution)/shard_map/reduce_scatter | solution.py:626
  1387.1 32.3 %collective-permute-done.48 = bf16[256,2048]{1,0:T(8,128)(2,1)S(1)} collective-permute-done((bf16[256,2048]{1,0:T(8,128)(2,1)}, bf16[256,2048]{1,0:T(8,128)(2,1)S(1)}, u32[]{:S(2)}, u32[]{:S(2)}) %collective-permute-start.48) | collective-permute-done | bytes 1048608 | tf_op jit(solution)/shard_map/ppermute | solution.py:333
  1424.0 23.8 %collective-permute-done.51 = bf16[256,2048]{1,0:T(8,128)(2,1)S(1)} collective-permute-done((bf16[256,2048]{1,0:T(8,128)(2,1)}, bf16[256,2048]{1,0:T(8,128)(2,1)S(1)}, u32[]{:S(2)}, u32[]{:S(2)}) %collective-permute-start.51) | collective-permute-done | bytes 1048608 | tf_op jit(solution)/shard_map/ppermute | solution.py:333
  1450.8 56.2 %collective-permute-done.54 = bf16[256,2048]{1,0:T(8,128)(2,1)S(1)} collective-permute-done((bf16[256,2048]{1,0:T(8,128)(2,1)}, bf16[256,2048]{1,0:T(8,128)(2,1)S(1)}, u32[]{:S(2)}, u32[]{:S(2)}) %collective-permute-start.54) | collective-permute-done | bytes 1048608 | tf_op jit(solution)/shard_map/ppermute | solution.py:333
  1509.5 17.8 %slice_bitcast_fusion = (f32[4,256,2048]{2,1,0:T(8,128)}, f32[4,2048,256]{1,2,0:T(8,128)}, f32[4,2048,256]{1,2,0:T(8,128)}) fusion(f32[4,3,256,2048]{3,2,1,0:T(8,128)} %get-tuple-element.101), kind=kLoop, calls=%fused_computation.4 | loop fusion | bytes 50331648 | tf_op jit(solution)/shard_map/squeeze | solution.py:542
  1527.3 8.7 copy.145
  1536.0 8.7 copy.144
  (530 shorter events, 395.5 us)
Async XLA Ops:
  7.2 88.9 %all-gather.11.cloned.1.call-start = ((), (), s32[]{:S(2)}) async-start(), calls=%async_computation.4 | async-start | bytes 5242880 | tf_op jit(solution)/shard_map/all_gather | solution.py:424
  12.5 205.5 %reduce-scatter.5.cloned.1.call-start = ((), (), s32[]{:S(2)}) async-start(), calls=%async_computation.5 | async-start | bytes 5242880 | tf_op jit(solution)/shard_map/reduce_scatter | solution.py:456
  142.5 418.0 %all-gather.19.cloned.1.call-start = ((), (), s32[]{:S(2)}) async-start(), calls=%async_computation.12 | async-start | bytes 10027008 | tf_op jit(solution)/shard_map/all_gather | solution.py:509
  224.3 409.4 %all-gather.17.cloned.1.call-start = ((), (), s32[]{:S(2)}) async-start(), calls=%async_computation.11 | async-start | bytes 10027008 | tf_op jit(solution)/shard_map/all_gather | solution.py:509
  252.3 461.0 %all-gather.21.cloned.1.call-start = ((), (), s32[]{:S(2)}) async-start(), calls=%async_computation.13 | async-start | bytes 10027008 | tf_op jit(solution)/shard_map/all_gather | solution.py:509
  303.8 499.2 %all-gather.15.cloned.1.call-start = ((), (), s32[]{:S(2)}) async-start(), calls=%async_computation.10 | async-start | bytes 10027008 | tf_op jit(solution)/shard_map/all_gather | solution.py:509
  303.9 150.8 %collective-permute-start.2 = (bf16[1024,2048]{1,0:T(8,128)(2,1)}, bf16[1024,2048]{1,0:T(8,128)(2,1)S(1)}, u32[]{:S(2)}, u32[]{:S(2)}) collective-permute-start(bf16[1024,2048]{1,0:T(8,128)(2,1)} %bitcast.15), channel_id=1, source_target_pairs={{0,8},{4,12},{8,0},{12,4},{16,24},{20,28},{24,16},{28,20},{1,9},{5... | collective-permute-start | bytes 12582920 | tf_op jit(solution)/shard_map/ppermute | solution.py:333
  305.2 152.3 %collective-permute-start.3 = (bf16[1024,2048]{1,0:T(8,128)(2,1)}, bf16[1024,2048]{1,0:T(8,128)(2,1)S(1)}, u32[]{:S(2)}, u32[]{:S(2)}) collective-permute-start(bf16[1024,2048]{1,0:T(8,128)(2,1)} %bitcast.15), channel_id=1, source_target_pairs={{16,0},{20,4},{24,8},{28,12},{0,16},{4,20},{8,24},{12,28},{17,1},{... | collective-permute-start | bytes 12582920 | tf_op jit(solution)/shard_map/ppermute | solution.py:326
  462.6 62.9 %collective-permute-start.7 = (bf16[1024,2048]{1,0:T(8,128)(2,1)}, bf16[1024,2048]{1,0:T(8,128)(2,1)S(1)}, u32[]{:S(2)}, u32[]{:S(2)}) collective-permute-start(bf16[1024,2048]{1,0:T(8,128)(2,1)} %copy-done.28), channel_id=1, source_target_pairs={{0,4},{4,0},{8,12},{12,8},{16,20},{20,16},{24,28},{28,24},{1,5},{5... | collective-permute-start | bytes 12582920 | tf_op jit(solution)/shard_map/ppermute | solution.py:336
  468.8 59.1 %collective-permute-start.8 = (bf16[1024,2048]{1,0:T(8,128)(2,1)S(1)}, bf16[1024,2048]{1,0:T(8,128)(2,1)S(1)}, u32[]{:S(2)}, u32[]{:S(2)}) collective-permute-start(bf16[1024,2048]{1,0:T(8,128)(2,1)S(1)} %copy-done.27), channel_id=1, source_target_pairs={{0,4},{4,0},{8,12},{12,8},{16,20},{20,16},{24,28},{28,24},{1,5},{5... | collective-permute-start | bytes 12582920 | tf_op jit(solution)/shard_map/ppermute | solution.py:336
  555.5 650.2 %all-gather.13.cloned.1.call-start = ((), (), s32[]{:S(2)}) async-start(), calls=%async_computation.6 | async-start | bytes 5242880 | tf_op jit(solution)/shard_map/all_gather | solution.py:560
  632.6 74.1 %collective-permute-start.11 = (bf16[4,256,2176]{2,1,0:T(8,128)(2,1)}, bf16[4,256,2176]{2,1,0:T(8,128)(2,1)}, u32[]{:S(2)}, u32[]{:S(2)}) collective-permute-start(bf16[4,256,2176]{2,1,0:T(8,128)(2,1)} %get-tuple-element.63), channel_id=1, source_target_pairs={{0,4},{4,0},{8,12},{12,8},{16,20},{20,16},{24,28},{28,24},{1,5},{5... | collective-permute-start | bytes 13369352 | tf_op jit(solution)/shard_map/ppermute | solution.py:336
  633.2 246.2 %collective-permute-start.34 = (bf16[4,256,2048]{2,1,0:T(8,128)(2,1)}, bf16[4,256,2048]{2,1,0:T(8,128)(2,1)}, u32[]{:S(2)}, u32[]{:S(2)}) collective-permute-start(bf16[4,256,2048]{2,1,0:T(8,128)(2,1)} %get-tuple-element.76), channel_id=1, source_target_pairs={{0,4},{4,0},{8,12},{12,8},{16,20},{20,16},{24,28},{28,24},{1,5},{5... | collective-permute-start | bytes 12582920 | tf_op jit(solution)/shard_map/ppermute | solution.py:336
  706.6 89.6 %collective-permute-start.10 = (bf16[4,256,2176]{2,1,0:T(8,128)(2,1)}, bf16[4,256,2176]{2,1,0:T(8,128)(2,1)}, u32[]{:S(2)}, u32[]{:S(2)}) collective-permute-start(bf16[4,256,2176]{2,1,0:T(8,128)(2,1)} %get-tuple-element.60), channel_id=1, source_target_pairs={{0,4},{4,0},{8,12},{12,8},{16,20},{20,16},{24,28},{28,24},{1,5},{5... | collective-permute-start | bytes 13369352 | tf_op jit(solution)/shard_map/ppermute | solution.py:336
  715.5 77.1 %collective-permute-start.13 = (bf16[128,2176]{1,0:T(8,128)(2,1)}, bf16[128,2176]{1,0:T(8,128)(2,1)}, u32[]{:S(2)}, u32[]{:S(2)}) collective-permute-start(bf16[128,2176]{1,0:T(8,128)(2,1)} %get-tuple-element.189), channel_id=1, source_target_pairs={{0,8},{4,12},{8,0},{12,4},{16,24},{20,28},{24,16},{28,20},{1,9},{5... | collective-permute-start | bytes 1671176 | tf_op jit(solution)/shard_map/ppermute | solution.py:333
  717.3 75.3 %collective-permute-start.12 = (bf16[128,2176]{1,0:T(8,128)(2,1)S(1)}, bf16[128,2176]{1,0:T(8,128)(2,1)}, u32[]{:S(2)}, u32[]{:S(2)}) collective-permute-start(bf16[128,2176]{1,0:T(8,128)(2,1)S(1)} %get-tuple-element.190), channel_id=1, source_target_pairs={{0,16},{4,20},{8,24},{12,28},{16,0},{20,4},{24,8},{28,12},{1,17},{... | collective-permute-start | bytes 1671176 | tf_op jit(solution)/shard_map/ppermute | solution.py:330
  790.2 105.6 %collective-permute-start.22 = (bf16[4,256,2176]{2,1,0:T(8,128)(2,1)}, bf16[4,256,2176]{2,1,0:T(8,128)(2,1)}, u32[]{:S(2)}, u32[]{:S(2)}) collective-permute-start(bf16[4,256,2176]{2,1,0:T(8,128)(2,1)} %get-tuple-element.70), channel_id=1, source_target_pairs={{0,4},{4,0},{8,12},{12,8},{16,20},{20,16},{24,28},{28,24},{1,5},{5... | collective-permute-start | bytes 13369352 | tf_op jit(solution)/shard_map/ppermute | solution.py:336
  876.3 61.2 %collective-permute-start.35 = (bf16[4,256,2048]{2,1,0:T(8,128)(2,1)}, bf16[4,256,2048]{2,1,0:T(8,128)(2,1)}, u32[]{:S(2)}, u32[]{:S(2)}) collective-permute-start(bf16[4,256,2048]{2,1,0:T(8,128)(2,1)} %get-tuple-element.78), channel_id=1, source_target_pairs={{0,4},{4,0},{8,12},{12,8},{16,20},{20,16},{24,28},{28,24},{1,5},{5... | collective-permute-start | bytes 12582920 | tf_op jit(solution)/shard_map/ppermute | solution.py:336
  892.9 134.4 %collective-permute-start.36 = (bf16[4,256,2048]{2,1,0:T(8,128)(2,1)}, bf16[4,256,2048]{2,1,0:T(8,128)(2,1)}, u32[]{:S(2)}, u32[]{:S(2)}) collective-permute-start(bf16[4,256,2048]{2,1,0:T(8,128)(2,1)} %get-tuple-element.80), channel_id=1, source_target_pairs={{0,4},{4,0},{8,12},{12,8},{16,20},{20,16},{24,28},{28,24},{1,5},{5... | collective-permute-start | bytes 12582920 | tf_op jit(solution)/shard_map/ppermute | solution.py:336
  914.4 114.8 %collective-permute-start.37 = (bf16[4,256,2048]{2,1,0:T(8,128)(2,1)}, bf16[4,256,2048]{2,1,0:T(8,128)(2,1)}, u32[]{:S(2)}, u32[]{:S(2)}) collective-permute-start(bf16[4,256,2048]{2,1,0:T(8,128)(2,1)} %get-tuple-element.82), channel_id=1, source_target_pairs={{0,4},{4,0},{8,12},{12,8},{16,20},{20,16},{24,28},{28,24},{1,5},{5... | collective-permute-start | bytes 12582920 | tf_op jit(solution)/shard_map/ppermute | solution.py:336
  1027.3 69.7 %collective-permute-start.27 = (bf16[256,2176]{1,0:T(8,128)(2,1)S(1)}, bf16[256,2176]{1,0:T(8,128)(2,1)S(1)}, u32[]{:S(2)}, u32[]{:S(2)}) collective-permute-start(bf16[256,2176]{1,0:T(8,128)(2,1)S(1)} %fusion.23), channel_id=1, source_target_pairs={{0,2},{1,3},{2,0},{3,1},{4,6},{5,7},{6,4},{7,5},{8,10},{9,11},{10,... | collective-permute-start | bytes 3342344 | tf_op jit(solution)/shard_map/ppermute | solution.py:538
  1029.1 67.8 %collective-permute-start.33 = (bf16[256,2176]{1,0:T(8,128)(2,1)S(1)}, bf16[256,2176]{1,0:T(8,128)(2,1)S(1)}, u32[]{:S(2)}, u32[]{:S(2)}) collective-permute-start(bf16[256,2176]{1,0:T(8,128)(2,1)S(1)} %fusion.19), channel_id=1, source_target_pairs={{0,3},{1,0},{2,1},{3,2},{4,7},{5,4},{6,5},{7,6},{8,11},{9,8},{10,9... | collective-permute-start | bytes 3342344 | tf_op jit(solution)/shard_map/ppermute | solution.py:538
  1103.8 260.4 %reduce-scatter.7.cloned.1.call-start = ((), (), s32[]{:S(2)}) async-start(), calls=%async_computation.7 | async-start | bytes 5242880 | tf_op jit(solution)/shard_map/reduce_scatter | solution.py:626
  1279.9 264.8 %reduce-scatter.11.cloned.1.call-start = ((), (), s32[]{:S(2)}) async-start(), calls=%async_computation.9 | async-start | bytes 4902912 | tf_op jit(solution)/shard_map/reduce_scatter | solution.py:624
  1320.6 239.3 %reduce-scatter.9.cloned.1.call-start = ((), (), s32[]{:S(2)}) async-start(), calls=%async_computation.8 | async-start | bytes 4755456 | tf_op jit(solution)/shard_map/reduce_scatter | solution.py:640
  1384.5 63.2 %collective-permute-start.51 = (bf16[256,2048]{1,0:T(8,128)(2,1)}, bf16[256,2048]{1,0:T(8,128)(2,1)S(1)}, u32[]{:S(2)}, u32[]{:S(2)}) collective-permute-start(bf16[256,2048]{1,0:T(8,128)(2,1)} %get-tuple-element.95), channel_id=1, source_target_pairs={{0,8},{4,12},{8,0},{12,4},{16,24},{20,28},{24,16},{28,20},{1,9},{5... | collective-permute-start | bytes 3145736 | tf_op jit(solution)/shard_map/ppermute | solution.py:333
  1385.0 64.2 %collective-permute-start.52 = (bf16[256,2048]{1,0:T(8,128)(2,1)}, bf16[256,2048]{1,0:T(8,128)(2,1)S(1)}, u32[]{:S(2)}, u32[]{:S(2)}) collective-permute-start(bf16[256,2048]{1,0:T(8,128)(2,1)} %get-tuple-element.96), channel_id=1, source_target_pairs={{0,16},{4,20},{8,24},{12,28},{16,0},{20,4},{24,8},{28,12},{1,17},{... | collective-permute-start | bytes 3145736 | tf_op jit(solution)/shard_map/ppermute | solution.py:330
  1385.5 168.1 %collective-permute-start.46 = (bf16[256,2048]{1,0:T(8,128)(2,1)}, bf16[256,2048]{1,0:T(8,128)(2,1)}, u32[]{:S(2)}, u32[]{:S(2)}) collective-permute-start(bf16[256,2048]{1,0:T(8,128)(2,1)} %get-tuple-element.89), channel_id=1, source_target_pairs={{0,8},{4,12},{8,0},{12,4},{16,24},{20,28},{24,16},{28,20},{1,9},{5... | collective-permute-start | bytes 3145736 | tf_op jit(solution)/shard_map/ppermute | solution.py:333
  1419.4 87.6 %collective-permute-start.54 = (bf16[256,2048]{1,0:T(8,128)(2,1)}, bf16[256,2048]{1,0:T(8,128)(2,1)S(1)}, u32[]{:S(2)}, u32[]{:S(2)}) collective-permute-start(bf16[256,2048]{1,0:T(8,128)(2,1)} %get-tuple-element.98), channel_id=1, source_target_pairs={{0,8},{4,12},{8,0},{12,4},{16,24},{20,28},{24,16},{28,20},{1,9},{5... | collective-permute-start | bytes 3145736 | tf_op jit(solution)/shard_map/ppermute | solution.py:333
  1420.9 86.0 %collective-permute-start.55 = (bf16[256,2048]{1,0:T(8,128)(2,1)S(1)}, bf16[256,2048]{1,0:T(8,128)(2,1)S(1)}, u32[]{:S(2)}, u32[]{:S(2)}) collective-permute-start(bf16[256,2048]{1,0:T(8,128)(2,1)S(1)} %copy-done.59), channel_id=1, source_target_pairs={{0,16},{4,20},{8,24},{12,28},{16,0},{20,4},{24,8},{28,12},{1,17},{... | collective-permute-start | bytes 3145736 | tf_op jit(solution)/shard_map/ppermute | solution.py:330
  1447.7 105.9 %collective-permute-start.47 = (bf16[256,2048]{1,0:T(8,128)(2,1)}, bf16[256,2048]{1,0:T(8,128)(2,1)}, u32[]{:S(2)}, u32[]{:S(2)}) collective-permute-start(bf16[256,2048]{1,0:T(8,128)(2,1)} %get-tuple-element.90), channel_id=1, source_target_pairs={{0,16},{4,20},{8,24},{12,28},{16,0},{20,4},{24,8},{28,12},{1,17},{... | collective-permute-start | bytes 3145736 | tf_op jit(solution)/shard_map/ppermute | solution.py:330
  1449.3 104.4 %collective-permute-start.50 = (bf16[256,2048]{1,0:T(8,128)(2,1)}, bf16[256,2048]{1,0:T(8,128)(2,1)}, u32[]{:S(2)}, u32[]{:S(2)}) collective-permute-start(bf16[256,2048]{1,0:T(8,128)(2,1)} %add_convert_fusion.13), channel_id=1, source_target_pairs={{0,1},{1,2},{2,3},{3,0},{4,5},{5,6},{6,7},{7,4},{8,9},{9,10},{10,1... | collective-permute-start | bytes 3145736 | tf_op jit(solution)/shard_map/ppermute | solution.py:613
  (161 other events, 3675.0 us)
Sparse Core Ops, SparseCore 0:
  12.6 83.4 all-gather.10
  142.6 75.2 reduce-scatter.4
  224.4 56.9 all-gather.18
  283.2 82.4 all-gather.16
  367.4 90.8 all-gather.20
  555.6 55.3 all-gather.14
  1103.9 101.7 all-gather.12
  1280.0 84.1 reduce-scatter.6
  1367.7 73.4 reduce-scatter.10
  1444.5 65.8 reduce-scatter.8

commit v2 on v1

v2 whole, which is shorter than its diff:
```python
import functools

import jax
import jax.numpy as jnp
from jax import lax
from jax.experimental import pallas as pl
from jax.experimental.pallas import tpu as pltpu
from jax.sharding import PartitionSpec as P

EPS = 1e-06
THETA = 50000.0
NEG = -1e30


def rms_scale(values, gain):
    return values * lax.rsqrt(jnp.mean(values * values, axis=-1, keepdims=True) + EPS) * gain


def rotate(values):
    length = values.shape[-3]
    half_dim = values.shape[-1] // 2
    positions = jnp.arange(length).astype(jnp.float32)
    rates = THETA ** (-jnp.arange(half_dim).astype(jnp.float32) / half_dim)
    angles = positions[:, None] * rates[None, :]
    cosine = jnp.cos(angles)[:, None, :]
    sine = jnp.sin(angles)[:, None, :]
    first = values[..., :half_dim]
    second = values[..., half_dim:]
    return jnp.concatenate(
        [first * cosine - second * sine, second * cosine + first * sine], axis=-1
    )


def prepare(raw, gain):
    shaped = raw.reshape(raw.shape[0], -1, gain.shape[0])
    return rotate(rms_scale(shaped, gain))


def dot_nt(a, b):
    return lax.dot_general(a, b, (((1,), (1,)), ((), ())), preferred_element_type=jnp.float32)


def dot_nn(a, b):
    return jnp.dot(a, b, preferred_element_type=jnp.float32)


def largest_tile(total, limit, unit):
    best = unit
    for tile in range(unit, limit + 1, unit):
        if total % tile == 0:
            best = tile
    return best


def moe_kernel(
    sizes,
    own_ref,
    cot_ref,
    pick_ref,
    wg_ref,
    wu_ref,
    wd_ref,
    final_ref,
    acc_ref,
    mine_ref,
    gather_ref,
    other_ref,
    both_ref,
    core_in,
    top_in,
    bottom_in,
    near_in,
    far_in,
    ring_out,
    ring_in,
    in_s,
    out_s,
    rows_s,
    crow_s,
    mrow_s,
    meta_s,
    aw_s,
    gg_s,
    gu_s,
    turn_s,
    acc_s,
    load_sem,
    store_sem,
    x_sem,
    c_sem,
    out_sem,
    fold_sem,
    plane_send,
    plane_recv,
    sum_send,
    sum_recv,
    ring_send,
    ring_recv,
    last_send,
    last_recv,
):
    outer, chunks, experts, slots, rows, width, extra, all_experts = sizes
    blocks, half, cut = 4 * outer, 2 * outer, rows // 2
    full = width + extra
    span = full + width
    total = blocks * slots
    ring = gather_ref.shape[0]
    j = pl.program_id(0)
    s = pl.program_id(1)
    steps = 2 * blocks + experts
    me = lax.axis_index("dp")
    z = lax.axis_index("tensor")
    a, rest = me // 4, me % 4
    inner_id = me + 2 - 4 * ((me // 2) % 2)
    core_id = me + 1 - 2 * (me % 2)
    upper, lower = pl.ds(0, cut), pl.ds(cut, cut)
    x_part, y_part = pl.ds(0, full), pl.ds(full, width)

    def outer_id(k):
        return ((a + k + outer) % outer) * 4 + rest

    def remote(src, dst, send, recv, where, axis="dp"):
        return pltpu.make_async_remote_copy(
            src_ref=src,
            dst_ref=dst,
            send_sem=send,
            recv_sem=recv,
            device_id={axis: where},
            device_id_type=pl.DeviceIdType.MESH,
        )

    def plane_copy(c, src, dst, rows_at, ident, where):
        first = isinstance(src, int) and src == 0
        near = src if isinstance(src, int) else dst
        source = mine_ref.at[c] if first else gather_ref.at[c % ring, near - 1]
        target = gather_ref.at[c % ring, dst - 1]
        if rows_at is not None:
            source, target = source.at[rows_at], target.at[rows_at]
        return remote(source, target, plane_send.at[c, ident], plane_recv.at[c, ident], where)

    def near_copy(c):
        return plane_copy(c, 0, 1, None, 0, inner_id)

    def far_copy(c, k):
        return plane_copy(c, 0, 2 * k, None, k, outer_id(-k))

    def top_copy(c, k):
        return plane_copy(c, 1, 2 * k + 1, upper, outer - 1 + k, outer_id(-k))

    def bottom_copy(c, k):
        return plane_copy(c, 2 * k, 2 * k + 1, lower, 2 * outer - 2 + k, inner_id)

    def core_copy(c, q):
        return plane_copy(c, q, half + q, None, 3 * outer - 2 + q, core_id)

    def ring_copy(k):
        where = (z - k + chunks) % chunks
        return remote(own_ref, mine_ref.at[k], ring_send.at[k], ring_recv.at[k], where, "tensor")

    others = range(1, outer)

    def first_hop(c):
        near_copy(c).start()
        for k in others:
            far_copy(c, k).start()
        core_copy(c, 0).start()

    def second_hop(c):
        near_copy(c).wait_recv()
        for k in others:
            top_copy(c, k).start()
        for k in others:
            far_copy(c, k).wait_recv()
            bottom_copy(c, k).start()
        for q in [1] + [2 * k for k in others]:
            core_copy(c, q).start()

    def third_hop(c):
        for k in others:
            top_copy(c, k).wait_recv()
            bottom_copy(c, k).wait_recv()
            core_copy(c, 2 * k + 1).start()

    def drain_gather(c):
        near_copy(c).wait_send()
        for k in others:
            far_copy(c, k).wait_send()
            top_copy(c, k).wait_send()
            bottom_copy(c, k).wait_send()
        for q in range(half):
            core_copy(c, q).wait_send()

    def sum_copy(c, src, dst, ident, where):
        return remote(src, dst, sum_send.at[c, ident], sum_recv.at[c, ident], where)

    def swap_copy(c, q):
        return sum_copy(c, other_ref.at[c % 2, q], core_in.at[c % 2, q], q, core_id)

    def both_at(c, q, rows_at):
        return both_ref.at[c % 2, q, rows_at]

    def up_copy(c, k):
        ident = half + k - 1
        return sum_copy(c, both_at(c, 2 * k + 1, upper), top_in.at[c % 2, k - 1], ident, outer_id(k))

    def down_copy(c, k):
        ident = half + outer - 1 + k - 1
        source = both_at(c, 2 * k + 1, lower)
        return sum_copy(c, source, bottom_in.at[c % 2, k - 1], ident, inner_id)

    def home_near(c, part):
        rows_at = (upper, lower)[part]
        ident = half + 2 * outer - 2 + part
        return sum_copy(c, both_at(c, 1, rows_at), near_in.at[c % 2, rows_at], ident, inner_id)

    def home_far(c, k, part):
        rows_at = (upper, lower)[part]
        ident = half + 2 * outer + 2 * (k - 1) + part
        target = far_in.at[c % 2, k - 1, rows_at]
        return sum_copy(c, both_at(c, 2 * k, rows_at), target, ident, outer_id(k))

    def last_copy(c):
        where = (z + c) % chunks
        return remote(ring_out.at[c], ring_in.at[c], last_send.at[c], last_recv.at[c], where, "tensor")

    def local(src, dst, sem):
        return pltpu.make_async_copy(src, dst, sem)

    def together(*copies):
        for copy in copies:
            copy.start()
        for copy in copies:
            copy.wait()

    def fold_halves(c):
        for k in others:
            up_copy(c, k).wait_recv()
            down_copy(c, k).wait_recv()
            copies = [
                local(both_at(c, 2 * k, lower), in_s.at[0, lower], fold_sem.at[0]),
                local(top_in.at[c % 2, k - 1], in_s.at[1, upper], fold_sem.at[1]),
                local(bottom_in.at[c % 2, k - 1], in_s.at[1, lower], fold_sem.at[2]),
            ]
            if k == 1:
                copies.append(local(both_at(c, 1, upper), in_s.at[0, upper], fold_sem.at[3]))
            together(*copies)

            @pl.loop(0, rows // 16)
            def _(i):
                at = pl.ds(pl.multiple_of(i * 16, 16), 16)
                in_s[0, at, :] = low(wide(in_s[0, at, :]) + wide(in_s[1, at, :]))

            together(local(in_s.at[0, lower], both_at(c, 2 * k, lower), fold_sem.at[0]))
        together(local(in_s.at[0, upper], both_at(c, 1, upper), fold_sem.at[0]))
        for k in others:
            home_far(c, k, 1).start()
        home_near(c, 0).start()

    def fold_home(c):
        for part in (0, 1):
            home_near(c, part).wait_recv()
        together(
            local(both_ref.at[c % 2, 0], in_s.at[0], fold_sem.at[0]),
            local(near_in.at[c % 2], in_s.at[1], fold_sem.at[1]),
        )

        @pl.loop(0, rows // 16)
        def _(i):
            at = pl.ds(pl.multiple_of(i * 16, 16), 16)
            in_s[0, at, :] = low(wide(in_s[0, at, :]) + wide(in_s[1, at, :]))

        for k in others:
            for part in (0, 1):
                home_far(c, k, part).wait_recv()
            together(local(far_in.at[c % 2, k - 1], in_s.at[1], fold_sem.at[1]))

            @pl.loop(0, rows // 16)
            def _(i):
                at = pl.ds(pl.multiple_of(i * 16, 16), 16)
                in_s[0, at, :] = low(wide(in_s[0, at, :]) + wide(in_s[1, at, :]))

        together(local(in_s.at[0], ring_out.at[c], fold_sem.at[0]))

    def drain_sum(c):
        for q in range(half):
            swap_copy(c, q).wait_send()
        for k in others:
            up_copy(c, k).wait_send()
            down_copy(c, k).wait_send()
            for part in (0, 1):
                home_far(c, k, part).wait_send()
        for part in (0, 1):
            home_near(c, part).wait_send()

    def fetch(c, at):
        q, side, slot = at // 2, at % 2, at % 2
        r = side * half + q

        @pl.when(side == 1)
        def _():
            core_copy(c, q).wait_recv()

        rows_at = pl.ds(pl.multiple_of(((z + c) % chunks) * rows, rows), rows)
        @pl.when(r == 0)
        def _():
            local(mine_ref.at[c], in_s.at[slot, :, x_part], x_sem.at[slot]).start()

        @pl.when(r > 0)
        def _():
            source = gather_ref.at[c % ring, jnp.maximum(r - 1, 0)]
            local(source, in_s.at[slot, :, x_part], x_sem.at[slot]).start()

        local(cot_ref.at[r, rows_at], in_s.at[slot, :, y_part], c_sem.at[slot]).start()

    def fetched(slot):
        local(mine_ref.at[0], in_s.at[slot, :, x_part], x_sem.at[slot]).wait()
        local(cot_ref.at[0, pl.ds(0, rows)], in_s.at[slot, :, y_part], c_sem.at[slot]).wait()

    def load(e, slot):
        return local(acc_ref.at[e], acc_s.at[slot], load_sem.at[slot])

    def store(e, slot):
        return local(acc_s.at[slot], acc_ref.at[e], store_sem.at[slot])

    @pl.when((j == 0) & (s == 0))
    def _():
        barrier = pltpu.get_barrier_semaphore()
        peers = [("dp", core_id), ("dp", inner_id)] + [("dp", outer_id(k)) for k in others]
        peers += [("tensor", (z + k) % chunks) for k in range(1, chunks)]
        for axis, where in peers:
            pl.semaphore_signal(
                barrier, inc=1, device_id={axis: where}, device_id_type=pl.DeviceIdType.MESH
            )
        pl.semaphore_wait(barrier, len(peers))
        for k in range(1, chunks):
            ring_copy(k).start()
        together(local(own_ref, in_s.at[0, :, x_part], fold_sem.at[0]))
        together(local(in_s.at[0, :, x_part], mine_ref.at[0], fold_sem.at[0]))
        first_hop(0)
        fetch(0, 0)
        second_hop(0)
        ring_copy(1).wait_recv()
        first_hop(1)

    @pl.when((s == 0) & (j > 0))
    def _():
        load(0, 0).start()

    @pl.when((j == 0) & (s == 4))
    def _():
        third_hop(0)

    @pl.when((s == blocks + 1) & (j + 1 < chunks))
    def _():
        second_hop(j + 1)

    @pl.when((s == blocks + experts) & (j + 1 < chunks))
    def _():
        third_hop(j + 1)

    @pl.when((s == blocks + 2) & (j >= 1))
    def _():
        fold_halves(j - 1)

    @pl.when((s == blocks + 2) & (j + 2 < chunks))
    def _():
        ring_copy(j + 2).wait_recv()
        first_hop(j + 2)

    @pl.when(s == blocks + 3)
    def _():
        drain_gather(j)

    @pl.when((s == blocks + experts + half - 1) & (j >= 1))
    def _():
        fold_home(j - 1)

        @pl.when(j >= 2)
        def _():
            last_copy(j - 1).start()

        drain_sum(j - 1)

    @pl.when(s < blocks)
    def _():
        slot = s % 2

        @pl.when(s + 1 < blocks)
        def _():
            fetch(j, s + 1)

        fetched(slot)
        meta = in_s[slot, :, width:full]
        picks = (dot_nt(pick_ref[...], meta) == 0.0).astype(jnp.bfloat16)
        at = pl.multiple_of(s * slots, slots)
        got = low(dot_nn(picks, in_s[slot, :, :full]))
        cot = low(dot_nn(picks, in_s[slot, :, full:]))
        for e in range(experts):
            part = slice(e * slots, (e + 1) * slots)
            rows_s[e, pl.ds(at, slots), :] = got[part, :width]
            mrow_s[e, pl.ds(at, slots), :] = got[part, width:]
            crow_s[e, pl.ds(at, slots), :] = cot[part]
        meta_s[s] = meta

    @pl.when((s >= blocks) & (s < blocks + experts))
    def _():
        e = s - blocks
        slot = e % 2
        tile = largest_tile(total, 320, 16)
        expert = me * experts + e
        wg = wg_ref[0]
        wu = wu_ref[0]
        wd = wd_ref[0]

        @pl.loop(0, total // tile)
        def _(m):
            ds = pl.ds(pl.multiple_of(m * tile, tile), tile)
            picked_rows = rows_s[e, ds, :]
            gate = dot_nn(picked_rows, wg)
            up = dot_nn(picked_rows, wu)
            grad_act = dot_nt(crow_s[e, ds, :], wd)
            meta = wide(mrow_s[e, ds, :])
            column = lax.broadcasted_iota(jnp.int32, meta.shape, 1)
            wanted = (column == expert) | (column == expert + all_experts)
            weight = jnp.sum(jnp.where(wanted, meta, 0.0), axis=1, keepdims=True)
            sig = jax.nn.sigmoid(gate)
            silu = gate * sig
            act = silu * up
            g_pick = jnp.sum(act * grad_act, axis=1, keepdims=True)
            scaled = weight * grad_act
            aw_s[ds, :] = low(weight * act)
            gg_s[ds, :] = low(scaled * up * sig * (1.0 + gate * (1.0 - sig)))
            gu_s[ds, :] = low(scaled * silu)
            mrow_s[e, ds, :] = low(jnp.where(column == expert, g_pick, 0.0))

        @pl.when(e >= 1)
        def _():
            store(e - 1, 1 - slot).wait()

        @pl.when(j == 0)
        def _():
            acc_s[slot] = jnp.zeros(acc_s.shape[1:], jnp.float32)

        @pl.when(j > 0)
        def _():
            load(e, slot).wait()

            @pl.when(e + 1 < experts)
            def _():
                load(e + 1, 1 - slot).start()

        cols = largest_tile(width, 512, 128)
        for which, (left, right) in enumerate(((gg_s, rows_s), (gu_s, rows_s), (aw_s, crow_s))):
            turn_s[...] = left[...].T

            @pl.loop(0, width // cols)
            def _(n):
                ds = pl.ds(pl.multiple_of(n * cols, cols), cols)
                add = dot_nn(turn_s[...], right[e, :, ds])
                acc_s[slot, which, :, ds] = acc_s[slot, which, :, ds] + add

        store(e, slot).start()

        @pl.loop(0, total // tile)
        def _(m):
            ds = pl.ds(pl.multiple_of(m * tile, tile), tile)
            crow_s[e, ds, :] = low(dot_nn(aw_s[ds, :], wd))
            rows_s[e, ds, :] = low(dot_nt(gg_s[ds, :], wg) + dot_nt(gu_s[ds, :], wu))

    first = blocks + experts

    def written(c, o):
        q, slot = half - 1 - o % half, o % 2

        @pl.when(o < half)
        def _():
            local(out_s.at[slot], other_ref.at[c % 2, q], out_sem.at[slot]).wait()
            swap_copy(c, q).start()

        @pl.when(o >= half)
        def _():
            local(out_s.at[slot], both_ref.at[c % 2, q], out_sem.at[slot]).wait()

        for k in others:

            @pl.when((o >= half) & (q == 2 * k + 1))
            def _():
                up_copy(c, k).start()
                down_copy(c, k).start()

            @pl.when((o >= half) & (q == 2 * k))
            def _():
                home_far(c, k, 0).start()

        @pl.when((o >= half) & (q == 1))
        def _():
            home_near(c, 1).start()

    @pl.when(s >= first)
    def _():
        o = s - first
        slot = o % 2
        q = half - 1 - o % half
        side = 1 - o // half
        place = 2 * q + side
        at = pl.multiple_of(place * slots, slots)

        @pl.when(o >= 1)
        def _():
            written(j, o - 1)

        @pl.when((o >= half - 1) & (o < 2 * half - 1))
        def _():
            coming = half - 1 - (o + 1) % half
            swap_copy(j, coming).wait_recv()
            local(core_in.at[j % 2, coming], in_s.at[1 - slot], x_sem.at[1 - slot]).start()

        @pl.when(o >= half)
        def _():
            local(core_in.at[j % 2, q], in_s.at[slot], x_sem.at[slot]).wait()

        @pl.when(o < half)
        def _():
            in_s[slot] = jnp.zeros((rows, span), jnp.bfloat16)

        picks = (dot_nt(meta_s[place], pick_ref[...]) == 0.0).astype(jnp.bfloat16)
        flat = (experts * slots, width)
        g = dot_nn(picks, rows_s[:, pl.ds(at, slots), :].reshape(flat))
        out_s[slot, :, :width] = low(g + wide(in_s[slot, :, :width]))
        flat = (experts * slots, extra)
        p = dot_nn(picks, mrow_s[:, pl.ds(at, slots), :].reshape(flat))
        out_s[slot, :, width:full] = low(p + wide(in_s[slot, :, width:full]))
        flat = (experts * slots, width)
        y = dot_nn(picks, crow_s[:, pl.ds(at, slots), :].reshape(flat))
        out_s[slot, :, full:] = low(y + wide(in_s[slot, :, full:]))

        @pl.when(o < half)
        def _():
            local(out_s.at[slot], other_ref.at[j % 2, q], out_sem.at[slot]).start()

        @pl.when(o >= half)
        def _():
            local(out_s.at[slot], both_ref.at[j % 2, q], out_sem.at[slot]).start()

        @pl.when(s == steps - 1)
        def _():
            written(j, o)
            store(experts - 1, (experts - 1) % 2).wait()

        @pl.when((s == steps - 1) & (j + 1 < chunks))
        def _():
            fetch(j + 1, 0)

    @pl.when((s == steps - 1) & (j == chunks - 1))
    def _():
        fold_halves(chunks - 1)
        fold_home(chunks - 1)
        last_copy(chunks - 1).start()
        drain_sum(chunks - 1)
        together(local(ring_out.at[0], in_s.at[0], fold_sem.at[0]))
        for k in range(1, chunks):
            last_copy(k).wait_recv()
            together(local(ring_in.at[k], in_s.at[1], fold_sem.at[1]))

            @pl.loop(0, rows // 16)
            def _(i):
                at = pl.ds(pl.multiple_of(i * 16, 16), 16)
                in_s[0, at, :] = low(wide(in_s[0, at, :]) + wide(in_s[1, at, :]))

        together(local(in_s.at[0], final_ref, fold_sem.at[0]))
        for k in range(1, chunks):
            last_copy(k).wait_send()
            ring_copy(k).wait_send()


def moe(own, cot, picks, wg, wu, wd, outer, chunks, slots, all_experts):
    rows, full = own.shape
    width = cot.shape[2]
    extra = full - width
    span = full + width
    experts, _, hidden = wg.shape
    blocks, half, cut = 4 * outer, 2 * outer, rows // 2
    total = blocks * slots
    sizes = (outer, chunks, experts, slots, rows, width, extra, all_experts)

    def expert_at(j, s):
        return (jnp.clip(s - blocks, 0, experts - 1), 0, 0)

    anywhere = pl.BlockSpec(memory_space=pl.ANY)
    in_specs = [
        anywhere,
        anywhere,
        pl.BlockSpec(picks.shape, lambda j, s: (0, 0)),
        pl.BlockSpec((1, width, hidden), expert_at),
        pl.BlockSpec((1, width, hidden), expert_at),
        pl.BlockSpec((1, hidden, width), expert_at),
    ]
    bf16 = jnp.bfloat16
    shapes = [
        ((rows, span), bf16),
        ((experts, 3, hidden, width), jnp.float32),
        ((chunks, rows, full), bf16),
        ((chunks if chunks <= 4 else 3, blocks - 1, rows, full), bf16),
        ((2, half, rows, span), bf16),
        ((2, half, rows, span), bf16),
        ((2, half, rows, span), bf16),
        ((2, outer - 1, cut, span), bf16),
        ((2, outer - 1, cut, span), bf16),
        ((2, rows, span), bf16),
        ((2, outer - 1, rows, span), bf16),
        ((chunks, rows, span), bf16),
        ((chunks, rows, span), bf16),
    ]
    dma = pltpu.SemaphoreType.DMA
    gathers, sums = 5 * outer - 2, 6 * outer - 2
    scratch = [
        pltpu.VMEM((2, rows, span), bf16),
        pltpu.VMEM((2, rows, span), bf16),
        pltpu.VMEM((experts, total, width), bf16),
        pltpu.VMEM((experts, total, width), bf16),
        pltpu.VMEM((experts, total, extra), bf16),
        pltpu.VMEM((blocks, rows, extra), bf16),
        pltpu.VMEM((total, hidden), bf16),
        pltpu.VMEM((total, hidden), bf16),
        pltpu.VMEM((total, hidden), bf16),
        pltpu.VMEM((hidden, total), bf16),
        pltpu.VMEM((2, 3, hidden, width), jnp.float32),
        dma((2,)),
        dma((2,)),
        dma((2,)),
        dma((2,)),
        dma((2,)),
        dma((4,)),
        dma((chunks, gathers)),
        dma((chunks, gathers)),
        dma((chunks, sums)),
        dma((chunks, sums)),
        dma((chunks,)),
        dma((chunks,)),
        dma((chunks,)),
        dma((chunks,)),
    ]
    flops = 2 * chunks * experts * total * width * (hidden * 9 + 4 * rows)
    results = pl.pallas_call(
        functools.partial(moe_kernel, sizes),
        grid=(chunks, 2 * blocks + experts),
        in_specs=in_specs,
        out_specs=[anywhere] * len(shapes),
        out_shape=[jax.ShapeDtypeStruct(*shape) for shape in shapes],
        scratch_shapes=scratch,
        compiler_params=pltpu.CompilerParams(
            dimension_semantics=("arbitrary", "arbitrary"),
            vmem_limit_bytes=66_500_000,
            collective_id=0,
            has_side_effects=True,
        ),
        cost_estimate=pl.CostEstimate(
            flops=flops, bytes_accessed=blocks * chunks * rows * full * 8, transcendentals=0
        ),
        name="moe",
    )(own, cot, picks, wg, wu, wd)
    return results[:2]


def wide(values):
    return values.astype(jnp.float32)


def low(values):
    return values.astype(jnp.bfloat16)


def tie(*values):
    return lax.optimization_barrier(values)


def ring_sum(values, count):
    total = wide(values)
    for step in range(1, count):
        pairs = [(i, (i + step) % count) for i in range(count)]
        total = total + wide(lax.ppermute(low(values), "tensor", pairs))
    return total


class Plane:
    def __init__(self, count):
        self.outer = count // 4
        everyone = range(count)
        self.core = [(i, i ^ 1) for i in everyone]
        self.inner = [(i, i ^ 2) for i in everyone]
        self.count = count

    def pull(self, values, k):
        pairs = [((i + 4 * k) % self.count, i) for i in range(self.count)]
        return lax.ppermute(values, "dp", pairs)

    def swap_inner(self, values):
        return lax.ppermute(values, "dp", self.inner)

    def swap_core(self, values):
        return lax.ppermute(values, "dp", self.core)

    def first(self, own):
        return self.swap_inner(own), [self.pull(own, k) for k in range(1, self.outer)]

    def second(self, near, fars):
        half = near.shape[0] // 2
        return [
            jnp.concatenate([self.pull(near[:half], k + 1), self.swap_inner(far[half:])], axis=0)
            for k, far in enumerate(fars)
        ]

    def third(self, own, near, fars, diagonals):
        mine = [own, near]
        for far, diagonal in zip(fars, diagonals):
            mine += [far, diagonal]
        return mine + [self.swap_core(part) for part in mine]


def per_device(
    tokens,
    lengths,
    routes,
    attn_gain,
    w_query,
    w_key,
    w_value,
    w_out,
    q_gain,
    k_gain,
    ffn_gain,
    router_weight,
    w_gate,
    w_up,
    w_down,
    cotangent,
):
    tensor_count = lax.axis_size("tensor")
    data_count = lax.axis_size("dp")
    tensor_rank = lax.axis_index("tensor")
    block_rows = tokens.shape[1]
    width = tokens.shape[2]
    full_length = block_rows * tensor_count
    route_count = routes.shape[2]
    local_experts = w_gate.shape[0]
    all_experts = local_experts * data_count
    head_dim = q_gain.shape[0]
    local_width = w_query.shape[1]
    capacity = max(2, (block_rows * route_count * 5 + 4 * all_experts - 1) // (4 * all_experts))
    query_rows = min(512, full_length)
    scale = head_dim ** (-0.5)
    own_start = tensor_rank * block_rows
    token_values = tokens[0].astype(jnp.float32)
    seq_length = lengths[0]
    own_valid = (own_start + jnp.arange(block_rows) < seq_length).astype(jnp.float32)
    key_valid = jnp.arange(full_length) < seq_length
    normed = rms_scale(token_values, attn_gain).astype(jnp.bfloat16)
    gathered = lax.all_gather(normed, "tensor", axis=0, tiled=True)
    plane = Plane(data_count)
    near, fars = plane.first(cotangent[0])
    gathered, near, fars = tie(gathered, near, fars)
    query_unrotated = jnp.dot(gathered, w_query, preferred_element_type=jnp.float32)
    key_raw = jnp.dot(gathered, w_key, preferred_element_type=jnp.float32)
    value_raw = jnp.dot(gathered, w_value, preferred_element_type=jnp.float32)
    query_low = prepare(query_unrotated, q_gain).astype(jnp.bfloat16)
    key_low = prepare(key_raw, k_gain).astype(jnp.bfloat16)
    value_low = value_raw.astype(jnp.bfloat16).reshape(full_length, -1, head_dim)

    def block_scores(query_block):
        scores = (
            jnp.einsum("qhd,khd->hqk", query_block, key_low, preferred_element_type=jnp.float32)
            * scale
        )
        return jnp.where(key_valid[None, None, :], scores, NEG)

    mixed_parts = []
    log_totals = []
    for start in range(0, full_length, query_rows):
        scores = block_scores(query_low[start : start + query_rows])
        row_peak = jnp.max(scores, axis=-1, keepdims=True)
        powers = jnp.exp(scores - row_peak)
        total = jnp.sum(powers, axis=-1, keepdims=True)
        weights = (powers / total).astype(jnp.bfloat16)
        mixed_parts.append(
            jnp.einsum("hqk,khd->qhd", weights, value_low, preferred_element_type=jnp.float32)
        )
        log_totals.append(row_peak + jnp.log(total))
    attended = (
        jnp.concatenate(mixed_parts, axis=0).reshape(full_length, local_width).astype(jnp.bfloat16)
    )
    diagonals = plane.second(near, fars)
    attended, diagonals = tie(attended, diagonals)
    cot_all = plane.third(cotangent[0], near, fars, diagonals)
    attn_own = lax.psum_scatter(
        jnp.einsum("lh,dh->ld", attended, w_out, preferred_element_type=jnp.float32).astype(
            jnp.bfloat16
        ),
        "tensor",
        scatter_dimension=0,
        tiled=True,
    ).astype(jnp.float32)
    cot_all = jnp.stack(cot_all)
    residual = token_values + own_valid[:, None] * attn_own
    moe_own = rms_scale(residual, ffn_gain).astype(jnp.bfloat16)
    router_logits = jnp.dot(moe_own, router_weight, preferred_element_type=jnp.float32)
    own_probs = jax.nn.softmax(router_logits, axis=-1)
    own_routes = lax.dynamic_slice_in_dim(routes[0], own_start, block_rows, 0)
    onehot = own_routes[:, :, None] == jnp.arange(all_experts)[None, None, :]
    named = jnp.any(onehot, axis=1) & (own_valid[:, None] > 0.0)
    named_low = named.astype(jnp.bfloat16)
    before = jnp.arange(block_rows)[:, None] > jnp.arange(block_rows)[None, :]
    order = jnp.dot(before.astype(jnp.bfloat16), named_low, preferred_element_type=jnp.float32)
    place = jnp.where(named, order, -1.0).astype(jnp.bfloat16)
    weight = jnp.where(named, own_probs, 0.0)
    weight_high = weight.astype(jnp.bfloat16)
    weight_low = (weight - weight_high.astype(jnp.float32)).astype(jnp.bfloat16)
    used = 3 * all_experts + 1
    extra = (used + 127) // 128 * 128
    meta = jnp.concatenate(
        [
            weight_high,
            weight_low,
            place,
            jnp.ones((block_rows, 1), jnp.bfloat16),
            jnp.zeros((block_rows, extra - used), jnp.bfloat16),
        ],
        axis=1,
    )
    slots = (capacity + 15) // 16 * 16
    first_expert = lax.axis_index("dp") * local_experts
    slot_row = jnp.arange(local_experts * slots)[:, None]
    slot_column = jnp.arange(extra)[None, :]
    picks = jnp.where(
        slot_column == 2 * all_experts + first_expert + slot_row // slots,
        1.0,
        jnp.where(slot_column == 3 * all_experts, -(slot_row % slots).astype(jnp.float32), 0.0),
    ).astype(jnp.bfloat16)
    packed = jnp.concatenate([moe_own, meta], axis=1)
    combined, sums = moe(
        packed,
        cot_all,
        picks,
        w_gate,
        w_up,
        w_down,
        data_count // 4,
        tensor_count,
        slots,
        all_experts,
    )
    combined = wide(combined)
    grad_gate = jnp.swapaxes(sums[:, 0], 1, 2)
    grad_up = jnp.swapaxes(sums[:, 1], 1, 2)
    grad_down = sums[:, 2]
    grad_moe = combined[:, :width]
    grad_probs = combined[:, width : width + all_experts]
    output = low(residual + combined[:, width + extra :])
    grad_own = lax.dynamic_slice_in_dim(cotangent[0], own_start, block_rows, 0).astype(jnp.float32)
    grad_logits = (
        own_probs * (grad_probs - jnp.sum(own_probs * grad_probs, axis=-1, keepdims=True))
    ).astype(jnp.bfloat16)
    grad_moe = grad_moe + jnp.einsum(
        "re,de->rd", grad_logits, router_weight, preferred_element_type=jnp.float32
    )
    router_part = jnp.einsum("rd,re->de", moe_own, grad_logits, preferred_element_type=jnp.float32)
    ffn_pull = jax.vjp(rms_scale, residual, ffn_gain)[1]
    grad_res_norm, ffn_part = ffn_pull(grad_moe)
    grad_residual = grad_own + grad_res_norm
    grad_attn = (grad_residual * own_valid[:, None]).astype(jnp.bfloat16)
    grad_attn_all = lax.all_gather(grad_attn, "tensor", axis=0, tiled=True)
    grad_mixed = jnp.dot(grad_attn_all, w_out, preferred_element_type=jnp.float32).astype(
        jnp.bfloat16
    )
    grad_mixed = grad_mixed.reshape(full_length, -1, head_dim)
    out_part = jnp.einsum("ld,lh->dh", grad_attn_all, attended, preferred_element_type=jnp.float32)
    grad_query_parts = []
    grad_keys = jnp.zeros(key_low.shape, jnp.float32)
    grad_values = jnp.zeros(value_low.shape, jnp.float32)
    for order, start in enumerate(range(0, full_length, query_rows)):
        query_block = query_low[start : start + query_rows]
        grad_block = grad_mixed[start : start + query_rows]
        probs_block = jnp.exp(block_scores(query_block) - log_totals[order])
        probs_low = probs_block.astype(jnp.bfloat16)
        grad_values = grad_values + jnp.einsum(
            "hqk,qhd->khd", probs_low, grad_block, preferred_element_type=jnp.float32
        )
        grad_probs_block = jnp.einsum(
            "qhd,khd->hqk", grad_block, value_low, preferred_element_type=jnp.float32
        )
        delta = jnp.sum(probs_block * grad_probs_block, axis=-1, keepdims=True)
        grad_scores = (probs_block * (grad_probs_block - delta)).astype(jnp.bfloat16)
        grad_query_parts.append(
            jnp.einsum("hqk,khd->qhd", grad_scores, key_low, preferred_element_type=jnp.float32)
            * scale
        )
        grad_keys = (
            grad_keys
            + jnp.einsum(
                "hqk,qhd->khd", grad_scores, query_block, preferred_element_type=jnp.float32
            )
            * scale
        )
    grad_queries = jnp.concatenate(grad_query_parts, axis=0)
    query_pull = jax.vjp(prepare, query_unrotated, q_gain)[1]
    grad_query_raw, q_part = query_pull(grad_queries)
    key_pull = jax.vjp(prepare, key_raw, k_gain)[1]
    grad_key_raw, k_part = key_pull(grad_keys)
    grad_q_low = grad_query_raw.astype(jnp.bfloat16)
    grad_k_low = grad_key_raw.astype(jnp.bfloat16)
    grad_v_low = grad_values.reshape(full_length, local_width).astype(jnp.bfloat16)
    query_part = jnp.einsum("ld,lh->dh", gathered, grad_q_low, preferred_element_type=jnp.float32)
    key_part = jnp.einsum("ld,lh->dh", gathered, grad_k_low, preferred_element_type=jnp.float32)
    value_part = jnp.einsum("ld,lh->dh", gathered, grad_v_low, preferred_element_type=jnp.float32)
    from_query = jnp.einsum("lh,dh->ld", grad_q_low, w_query, preferred_element_type=jnp.float32)
    from_key = jnp.einsum("lh,dh->ld", grad_k_low, w_key, preferred_element_type=jnp.float32)
    from_value = jnp.einsum("lh,dh->ld", grad_v_low, w_value, preferred_element_type=jnp.float32)
    early = jnp.concatenate(
        [
            low(out_part),
            low(value_part),
            low(ring_sum(jnp.concatenate([router_part, ffn_part[:, None]], axis=1), tensor_count)),
        ],
        axis=1,
    )
    early = wide(lax.psum_scatter(early, "dp", scatter_dimension=0, tiled=True))
    grad_normed = wide(
        lax.psum_scatter(
            low(from_query + from_key + from_value), "tensor", scatter_dimension=0, tiled=True
        )
    )
    attn_pull = jax.vjp(rms_scale, token_values, attn_gain)[1]
    grad_tok_norm, attn_part = attn_pull(grad_normed)
    grad_tokens = (grad_residual + grad_tok_norm).astype(jnp.bfloat16)
    piece = head_dim // data_count
    gains = jnp.stack([q_part, k_part]).reshape(2, data_count, piece)
    gains = jnp.pad(gains, ((0, 0), (0, 0), (0, width // data_count - piece)))
    small = jnp.concatenate([attn_part[:, None], gains.reshape(2, width).T], axis=1)
    late = jnp.concatenate(
        [low(query_part), low(key_part), low(ring_sum(small, tensor_count))], axis=1
    )
    late = wide(lax.psum_scatter(late, "dp", scatter_dimension=0, tiled=True))
    end = 2 * local_width
    return (
        output[None],
        grad_tokens[None],
        late[:, end],
        late[:, :local_width],
        late[:, local_width:end],
        early[:, local_width:end],
        early[:, :local_width],
        late[:piece, end + 1],
        late[:piece, end + 2],
        early[:, end + all_experts],
        early[:, end : end + all_experts],
        grad_gate,
        grad_up,
        grad_down,
    )


def solution(mesh):
    return jax.shard_map(
        per_device,
        mesh=mesh,
        in_specs=(
            P("dp", "tensor", None),
            P("dp"),
            P("dp", None, None),
            P(),
            P(None, "tensor"),
            P(None, "tensor"),
            P(None, "tensor"),
            P(None, "tensor"),
            P(),
            P(),
            P(),
            P(),
            P("dp", None, "tensor"),
            P("dp", None, "tensor"),
            P("dp", "tensor", None),
            P("dp", None, None),
        ),
        out_specs=(
            P("dp", "tensor", None),
            P("dp", "tensor", None),
            P("dp"),
            P("dp", "tensor"),
            P("dp", "tensor"),
            P("dp", "tensor"),
            P("dp", "tensor"),
            P("dp"),
            P("dp"),
            P("dp"),
            P("dp", None),
            P("dp", None, "tensor"),
            P("dp", None, "tensor"),
            P("dp", "tensor", None),
        ),
        check_vma=False,
    )
```

time: 1590 us -> 1210 us (0.76)
  waiting for transfers between devices: 842 us -> 330 us
  Pallas kernels: 290 us -> 570 us
  other arithmetic: 132 us -> 63.9 us
  starting transfers between devices: 66.4 us -> 18.7 us
  local copies, waits for them, and re-layouts: 128 us -> 103 us
    ppermute x18 -> x2, waiting for transfers between devices: 324 us -> 8.44 us  [swap_inner(): return lax.ppermute(values, 'dp', self.inner)]
    pallas_call x4 -> x1, Pallas kernels: 290 us -> 570 us  [moe(): pl.pallas_call(functools.partial(moe_kernel, sizes), grid=(chunks, 2 * bl...]
    ppermute x25 -> x0, waiting for transfers between devices: 216 us -> none  [the longest x3 96.4 us: per_device(): lax.ppermute(packed, 'tensor', shift_in[step])]
    all_gather x1, waiting for transfers between devices: 81 us -> 0.01 us  [per_device(): gathered = lax.all_gather(normed, 'tensor', axis=0, tiled=True)]
    convert_element_type x26 -> x4, other arithmetic: 71.4 us -> 0.17 us  [low(): return values.astype(jnp.bfloat16)]
    ppermute x2, waiting for transfers between devices: 31.9 us -> 88 us  [pull(): return lax.ppermute(values, 'dp', pairs)]
    reduce_scatter x1, waiting for transfers between devices: 0.02 us -> 40.5 us  [per_device(): late = wide(lax.psum_scatter(late, 'dp', scatter_dimension=0, tiled=True))]
    ppermute x25 -> x0, starting transfers between devices: 32.4 us -> none  [the longest x16 18.3 us: push(): return lax.ppermute(values, 'dp', pairs)]
  transfers between devices with their start and end apart: 73 -> 20, of which waited for: 33 -> 11; matrix products, arithmetic and copies ran while one was open for 13% -> 12% of each run, Pallas kernels for 18% -> 0%
where the time goes in v2:
time: 1210 us; the launch traced here: 1200 us
  Pallas kernels  570 us (47%)
  waiting for transfers between devices  330 us (27%)
  local copies, waits for them, and re-layouts  103 us (9%)
  matrix products  96 us (8%)
  other arithmetic  63.9 us (5%)
  starting transfers between devices  18.7 us (2%)
  between operations  16.4 us (1%)
    pallas_call x1, Pallas kernels, moe(): pl.pallas_call(functools.partial(moe_kernel, sizes), grid=(chunks, 2 * bl...  570 us
    ppermute x2, waiting for transfers between devices, pull(): return lax.ppermute(values, 'dp', pairs)  88 us
    all_gather x1, waiting for transfers between devices, per_device(): grad_attn_all = lax.all_gather(grad_attn, 'tensor', axis=0, tiled=True)  81.4 us
    unnamed x182, local copies, waits for them, and re-layouts  58.6 us
    reduce_scatter x1, waiting for transfers between devices, per_device(): lax.psum_scatter(jnp.einsum('lh,dh->ld', attended, w_out, preferred_eleme...  42 us
    reduce_scatter x1, waiting for transfers between devices, per_device(): late = wide(lax.psum_scatter(late, 'dp', scatter_dimension=0, tiled=True))  40.5 us
    reduce_scatter x1, waiting for transfers between devices, per_device(): lax.psum_scatter(low(from_query + from_key + from_value), 'tensor', scatt...  38.3 us
    ppermute x6, waiting for transfers between devices, ring_sum(): total = total + wide(lax.ppermute(low(values), 'tensor', pairs))  25.4 us
  transfers between devices with their start and end apart: 20, of which 11 were waited for; matrix products, arithmetic and copies ran while one was open for 12% of the time, Pallas kernels for 0%

profile of v2, /device:TPU:0, one launch (start us, length us, event | category | flops | bytes accessed | tf_op | source)
XLA Modules:
  0.0 1197.5 jit_solution(1261346875796388965)
XLA Ops:
  19.6 86.8 %collective-permute-done.1 = bf16[1024,2048]{1,0:T(8,128)(2,1)} collective-permute-done((bf16[1024,2048]{1,0:T(8,128)(2,1)}, bf16[1024,2048]{1,0:T(8,128)(2,1)}, u32[]{:S(2)}, u32[]{:S(2)}) %collective-permute-start.1) | collective-permute-done | bytes 4194336 | tf_op jit(solution)/shard_map/ppermute | solution.py:695
  124.4 6.6 multiply_reduce_fusion.10
  154.1 7.0 collective-permute-done.3
  162.2 4.9 pad_maximum_fusion.2
  167.1 4.4 convolution_convert_fusion
  173.5 4.9 constant_dynamic-update-slice_fusion
  179.7 4.8 bitcast_dynamic-update-slice_fusion.6
  184.4 4.8 bitcast_dynamic-update-slice_fusion.5
  191.5 4.8 bitcast_dynamic-update-slice_fusion.3
  196.4 4.9 bitcast_dynamic-update-slice_fusion.2
  205.8 42.0 %reduce-scatter.5.cloned.1.call-done = bf16[256,2048]{1,0:T(8,128)(2,1)} async-done(((bf16[1024,2048]{1,0:T(8,128)(2,1)}), bf16[256,2048]{1,0:T(8,128)(2,1)}) %reduce-scatter.5.cloned.1.call-update) | async-done | bytes 1048592 | tf_op jit(solution)/shard_map/reduce_scatter | solution.py:794
  253.5 569.8 %moe.1 = (bf16[256,4224]{1,0:T(8,128)(2,1)}, f32[4,3,256,2048]{3,2,1,0:T(8,128)}, bf16[4,256,2176]{2,1,0:T(8,128)(2,1)}, bf16[4,7,256,2176]{3,2,1,0:T(8,128)(2,1...) custom-call(bf16[256,2176]{1,0:T(8,128)(2,1)} %concatenate.38.own_re, ...), custom_call_target="tpu_custom_call" | custom-call | flops 139586437120 | bytes 142606336 | tf_op jit(solution)/shard_map/moe/pallas_call | solution.py:644
  832.3 81.4 %all-gather.5.cloned.1.call-done = bf16[1024,2048]{1,0:T(8,128)(2,1)} async-done(((bf16[256,2048]{1,0:T(8,128)(2,1)}), bf16[1024,2048]{1,0:T(8,128)(2,1)}) %all-gather.5.cloned.1.call-update) | async-done | bytes 4194320 | tf_op jit(solution)/shard_map/all_gather | solution.py:870
  913.7 4.7 convolution_convert_fusion.5
  918.5 5.6 fusion.79
  924.1 7.6 fusion.4
  931.7 10.2 multiply_reduce_fusion.1
  941.9 8.6 multiply_convert_fusion.1
  976.4 4.1 fusion.81
  982.9 5.7 add_convert_fusion
  994.4 10.3 collective-permute-done.13
  1004.7 15.1 %collective-permute-done.12 = bf16[2048,33]{0,1:T(8,128)(2,1)S(1)} collective-permute-done((bf16[2048,33]{0,1:T(8,128)(2,1)S(1)}, bf16[2048,33]{0,1:T(8,128)(2,1)S(1)}, u32[]{:S(2)}, u32[]{:S(2)}) %collective-permute-start.12) | collective-permute-done | bytes 135200 | tf_op jit(solution)/shard_map/ppermute | solution.py:681
  1020.0 4.7 convolution_convert_fusion.1
  1029.7 5.0 convolution_convert_fusion.4
  1034.7 38.3 %reduce-scatter.7.cloned.1.call-done = bf16[256,2048]{1,0:T(8,128)(2,1)} async-done(((bf16[1024,2048]{1,0:T(8,128)(2,1)}), bf16[256,2048]{1,0:T(8,128)(2,1)}) %reduce-scatter.7.cloned.1.call-update) | async-done | bytes 1048592 | tf_op jit(solution)/shard_map/reduce_scatter | solution.py:927
  1083.0 4.9 convolution_convert_fusion.3
  1090.4 18.5 %slice_bitcast_fusion = (f32[4,256,2048]{2,1,0:T(8,128)}, f32[4,2048,256]{1,2,0:T(8,128)}, f32[4,2048,256]{1,2,0:T(8,128)}) fusion(f32[4,3,256,2048]{3,2,1,0:T(8,128)} %get-tuple-element.27), kind=kLoop, calls=%fused_computation | loop fusion | bytes 50331648 | tf_op jit(solution)/shard_map/squeeze | solution.py:854
  1108.9 8.7 copy.142
  1117.6 8.7 copy.141
  1126.2 5.9 reduce-scatter.11.cloned.1.call-done
  1140.8 4.8 fusion.36
  1145.6 40.5 %reduce-scatter.9.cloned.1.call-done = bf16[256,1027]{0,1:T(8,128)(2,1)} async-done(((bf16[2048,1027]{0,1:T(8,128)(2,1)}), bf16[256,1027]{0,1:T(8,128)(2,1)}) %reduce-scatter.9.cloned.1.call-update) | async-done | bytes 525840 | tf_op jit(solution)/shard_map/reduce_scatter | solution.py:941
  (303 shorter events, 142.5 us)
Async XLA Ops:
  7.2 243.1 %copy-start = (bf16[2048,32]{0,1:T(8,128)(2,1)S(1)}, bf16[2048,32]{0,1:T(8,128)(2,1)}, u32[]{:S(2)}) copy-start(bf16[2048,32]{0,1:T(8,128)(2,1)} %param.27) | copy-start | bytes 393220
  7.2 100.7 %all-gather.3.cloned.1.call-start = ((), (), s32[]{:S(2)}) async-start(), calls=%async_computation.4 | async-start | bytes 5242880 | tf_op jit(solution)/shard_map/all_gather | solution.py:758
  12.4 235.4 %reduce-scatter.5.cloned.1.call-start = ((), (), s32[]{:S(2)}) async-start(), calls=%async_computation.5 | async-start | bytes 5242880 | tf_op jit(solution)/shard_map/reduce_scatter | solution.py:794
  12.5 94.0 %collective-permute-start.1 = (bf16[1024,2048]{1,0:T(8,128)(2,1)}, bf16[1024,2048]{1,0:T(8,128)(2,1)}, u32[]{:S(2)}, u32[]{:S(2)}) collective-permute-start(bf16[1024,2048]{1,0:T(8,128)(2,1)} %bitcast.150), channel_id=1, source_target_pairs={{16,0},{20,4},{24,8},{28,12},{0,16},{4,20},{8,24},{12,28},{17,1},{... | collective-permute-start | bytes 12582920 | tf_op jit(solution)/shard_map/ppermute | solution.py:695
  15.5 92.3 %collective-permute-start = (bf16[1024,2048]{1,0:T(8,128)(2,1)}, bf16[1024,2048]{1,0:T(8,128)(2,1)}, u32[]{:S(2)}, u32[]{:S(2)}) collective-permute-start(bf16[1024,2048]{1,0:T(8,128)(2,1)} %bitcast.151), channel_id=1, source_target_pairs={{0,8},{4,12},{8,0},{12,4},{16,24},{20,28},{24,16},{28,20},{1,9},{5... | collective-permute-start | bytes 12582920 | tf_op jit(solution)/shard_map/ppermute | solution.py:698
  17.7 133.4 %copy-start.61 = (pred[1024]{0:T(1024)(128)(4,1)}, pred[1024]{0:T(1024)(128)(4,1)S(1)}, u32[]{:S(2)}) copy-start(pred[1024]{0:T(1024)(128)(4,1)S(1)} %iota_compare_fusion.5) | copy-start | bytes 3076
  19.6 117.1 %copy-start.27 = (f32[1024,64]{1,0:T(8,128)}, f32[1024,64]{1,0:T(8,128)S(1)}, u32[]{:S(2)}) copy-start(f32[1024,64]{1,0:T(8,128)S(1)} %get-tuple-element.125) | copy-start | bytes 786436
  19.6 117.1 %copy-start.29 = (f32[1024,64]{1,0:T(8,128)}, f32[1024,64]{1,0:T(8,128)S(1)}, u32[]{:S(2)}) copy-start(f32[1024,64]{1,0:T(8,128)S(1)} %get-tuple-element.126) | copy-start | bytes 786436
  114.5 46.6 %collective-permute-start.3 = (bf16[512,2048]{1,0:T(8,128)(2,1)}, bf16[512,2048]{1,0:T(8,128)(2,1)}, u32[]{:S(2)}, u32[]{:S(2)}) collective-permute-start(bf16[512,2048]{1,0:T(8,128)(2,1)} %slice.90), channel_id=1, source_target_pairs={{0,8},{4,12},{8,0},{12,4},{16,24},{20,28},{24,16},{28,20},{1,9},{5... | collective-permute-start | bytes 6291464 | tf_op jit(solution)/shard_map/ppermute | solution.py:698
  116.0 46.3 %collective-permute-start.2 = (bf16[512,2048]{1,0:T(8,128)(2,1)}, bf16[512,2048]{1,0:T(8,128)(2,1)}, u32[]{:S(2)}, u32[]{:S(2)}) collective-permute-start(bf16[512,2048]{1,0:T(8,128)(2,1)} %slice.89), channel_id=1, source_target_pairs={{16,0},{20,4},{24,8},{28,12},{0,16},{4,20},{8,24},{12,28},{17,1},{... | collective-permute-start | bytes 6291464 | tf_op jit(solution)/shard_map/ppermute | solution.py:695
  171.5 742.2 %all-gather.5.cloned.1.call-start = ((), (), s32[]{:S(2)}) async-start(), calls=%async_computation.6 | async-start | bytes 5242880 | tf_op jit(solution)/shard_map/all_gather | solution.py:870
  171.6 19.9 %collective-permute-start.4 = (bf16[1024,2048]{1,0:T(8,128)(2,1)}, bf16[1024,2048]{1,0:T(8,128)(2,1)}, u32[]{:S(2)}, u32[]{:S(2)}) collective-permute-start(bf16[1024,2048]{1,0:T(8,128)(2,1)} %bitcast.152), channel_id=1, source_target_pairs={{0,4},{4,0},{8,12},{12,8},{16,20},{20,16},{24,28},{28,24},{1,5},{5... | collective-permute-start | bytes 12582920 | tf_op jit(solution)/shard_map/ppermute | solution.py:701
  171.7 24.7 %collective-permute-start.5 = (bf16[1024,2048]{1,0:T(8,128)(2,1)}, bf16[1024,2048]{1,0:T(8,128)(2,1)}, u32[]{:S(2)}, u32[]{:S(2)}) collective-permute-start(bf16[1024,2048]{1,0:T(8,128)(2,1)} %collective-permute-done), channel_id=1, source_target_pairs={{0,4},{4,0},{8,12},{12,8},{16,20},{20,16},{24,28},{28,24},{1,5},{5... | collective-permute-start | bytes 12582920 | tf_op jit(solution)/shard_map/ppermute | solution.py:701
  173.1 28.1 %collective-permute-start.6 = (bf16[1024,2048]{1,0:T(8,128)(2,1)}, bf16[1024,2048]{1,0:T(8,128)(2,1)S(1)}, u32[]{:S(2)}, u32[]{:S(2)}) collective-permute-start(bf16[1024,2048]{1,0:T(8,128)(2,1)} %collective-permute-done.1), channel_id=1, source_target_pairs={{0,4},{4,0},{8,12},{12,8},{16,20},{20,16},{24,28},{28,24},{1,5},{5... | collective-permute-start | bytes 12582920 | tf_op jit(solution)/shard_map/ppermute | solution.py:701
  178.4 25.2 %collective-permute-start.7 = (bf16[1024,2048]{1,0:T(8,128)(2,1)S(1)}, bf16[1024,2048]{1,0:T(8,128)(2,1)S(1)}, u32[]{:S(2)}, u32[]{:S(2)}) collective-permute-start(bf16[1024,2048]{1,0:T(8,128)(2,1)S(1)} %copy-done.11), channel_id=1, source_target_pairs={{0,4},{4,0},{8,12},{12,8},{16,20},{20,16},{24,28},{28,24},{1,5},{5... | collective-permute-start | bytes 12582920 | tf_op jit(solution)/shard_map/ppermute | solution.py:701
  203.6 44.3 %copy-start.3 = (bf16[1,256,2048]{2,1,0:T(8,128)(2,1)S(1)}, bf16[1,256,2048]{2,1,0:T(8,128)(2,1)}, u32[]{:S(2)}) copy-start(bf16[1,256,2048]{2,1,0:T(8,128)(2,1)} %param.16) | copy-start | bytes 3145732
  205.8 43.9 %copy-start.52 = (f32[2048]{0:T(1024)S(1)}, f32[2048]{0:T(1024)}, u32[]{:S(2)}) copy-start(f32[2048]{0:T(1024)} %param.26) | copy-start | bytes 24580
  828.7 85.0 %copy-start.76 = (bf16[2048,512]{1,0:T(8,128)(2,1)S(1)}, bf16[2048,512]{1,0:T(8,128)(2,1)}, u32[]{:S(2)}) copy-start(bf16[2048,512]{1,0:T(8,128)(2,1)} %param.23) | copy-start | bytes 6291460
  832.2 240.8 %reduce-scatter.7.cloned.1.call-start = ((), (), s32[]{:S(2)}) async-start(), calls=%async_computation.7 | async-start | bytes 5242880 | tf_op jit(solution)/shard_map/reduce_scatter | solution.py:927
  988.7 31.3 %copy-start.37 = (bf16[4,128,1024]{2,1,0:T(8,128)(2,1)S(1)}, bf16[4,128,1024]{2,1,0:T(8,128)(2,1)}, u32[]{:S(2)}) copy-start(bf16[4,128,1024]{2,1,0:T(8,128)(2,1)} %add_convert_fusion.1) | copy-start | bytes 3145732
  988.7 143.4 %reduce-scatter.11.cloned.1.call-start = ((), (), s32[]{:S(2)}) async-start(), calls=%async_computation.9 | async-start | bytes 4902912 | tf_op jit(solution)/shard_map/reduce_scatter | solution.py:925
  991.3 13.5 %collective-permute-start.13 = (bf16[2048,33]{0,1:T(8,128)(2,1)S(1)}, bf16[2048,33]{0,1:T(8,128)(2,1)S(1)}, u32[]{:S(2)}, u32[]{:S(2)}) collective-permute-start(bf16[2048,33]{0,1:T(8,128)(2,1)S(1)} %fusion.38), channel_id=1, source_target_pairs={{0,3},{1,0},{2,1},{3,2},{4,7},{5,4},{6,5},{7,6},{8,11},{9,8},{10,9... | collective-permute-start | bytes 405512 | tf_op jit(solution)/shard_map/ppermute | solution.py:681
  991.9 27.9 %collective-permute-start.12 = (bf16[2048,33]{0,1:T(8,128)(2,1)S(1)}, bf16[2048,33]{0,1:T(8,128)(2,1)S(1)}, u32[]{:S(2)}, u32[]{:S(2)}) collective-permute-start(bf16[2048,33]{0,1:T(8,128)(2,1)S(1)} %fusion.38), channel_id=1, source_target_pairs={{0,2},{1,3},{2,0},{3,1},{4,6},{5,7},{6,4},{7,5},{8,10},{9,11},{10,... | collective-permute-start | bytes 405512 | tf_op jit(solution)/shard_map/ppermute | solution.py:681
  992.3 27.5 %collective-permute-start.11 = (bf16[2048,33]{0,1:T(8,128)(2,1)S(1)}, bf16[2048,33]{0,1:T(8,128)(2,1)S(1)}, u32[]{:S(2)}, u32[]{:S(2)}) collective-permute-start(bf16[2048,33]{0,1:T(8,128)(2,1)S(1)} %fusion.38), channel_id=1, source_target_pairs={{0,1},{1,2},{2,3},{3,0},{4,5},{5,6},{6,7},{7,4},{8,9},{9,10},{10,1... | collective-permute-start | bytes 405512 | tf_op jit(solution)/shard_map/ppermute | solution.py:681
  1029.4 156.7 %reduce-scatter.9.cloned.1.call-start = ((), (), s32[]{:S(2)}) async-start(), calls=%async_computation.8 | async-start | bytes 4755456 | tf_op jit(solution)/shard_map/reduce_scatter | solution.py:941
  1029.7 43.3 %copy-start.5 = (bf16[1,256,2048]{2,1,0:T(8,128)(2,1)S(1)}, bf16[1,256,2048]{2,1,0:T(8,128)(2,1)}, u32[]{:S(2)}) copy-start(bf16[1,256,2048]{2,1,0:T(8,128)(2,1)} %param.16) | copy-start | bytes 3145732
  1029.7 43.3 %copy-start.51 = (f32[2048]{0:T(1024)S(1)}, f32[2048]{0:T(1024)}, u32[]{:S(2)}) copy-start(f32[2048]{0:T(1024)} %param.19) | copy-start | bytes 24580
  1029.7 43.3 %copy-start.64 = (f32[256]{0:T(256)S(1)}, f32[256]{0:T(256)}, u32[]{:S(2)}) copy-start(f32[256]{0:T(256)} %copy-done.63) | copy-start | bytes 3076
  1075.4 12.5 %collective-permute-start.10 = (bf16[2048,3]{0,1:T(4,128)(2,1)S(1)}, bf16[2048,3]{0,1:T(4,128)(2,1)S(1)}, u32[]{:S(2)}, u32[]{:S(2)}) collective-permute-start(bf16[2048,3]{0,1:T(4,128)(2,1)S(1)} %fusion.44), channel_id=1, source_target_pairs={{0,3},{1,0},{2,1},{3,2},{4,7},{5,4},{6,5},{7,6},{8,11},{9,8},{10,9... | collective-permute-start | bytes 36872 | tf_op jit(solution)/shard_map/ppermute | solution.py:681
  1078.6 9.3 collective-permute-start.9
  1080.8 7.1 collective-permute-start.8
  1126.2 14.6 %copy-start.34 = (bf16[256,2048]{1,0:T(8,128)(2,1)S(1)}, bf16[256,2048]{1,0:T(8,128)(2,1)}, u32[]{:S(2)}) copy-start(bf16[256,2048]{1,0:T(8,128)(2,1)} %reduce-scatter.7.cloned.1.call-done) | copy-start | bytes 3145732
  (72 other events, 327.2 us)
Sparse Core Ops, SparseCore 0:
  12.5 83.4 all-gather.2
  171.7 76.1 reduce-scatter.4
  832.3 81.3 all-gather.4
  988.8 84.1 reduce-scatter.6
  1076.3 55.7 reduce-scatter.10
  1135.4 50.6 reduce-scatter.8

commit v3 on v2

--- a/solution.py
+++ b/solution.py
@@ -55,7 +55,16 @@
 def moe_kernel(
     sizes,
     own_ref,
-    cot_ref,
+    *others_refs,
+):
+    blocks = 4 * sizes[0]
+    moe_body(sizes, own_ref, others_refs[:blocks], *others_refs[blocks:])
+
+
+def moe_body(
+    sizes,
+    own_ref,
+    cot_refs,
     pick_ref,
     wg_ref,
     wu_ref,
@@ -310,11 +319,16 @@
             source = gather_ref.at[c % ring, jnp.maximum(r - 1, 0)]
             local(source, in_s.at[slot, :, x_part], x_sem.at[slot]).start()
 
-        local(cot_ref.at[r, rows_at], in_s.at[slot, :, y_part], c_sem.at[slot]).start()
+        for place, cot_ref in enumerate(cot_refs):
+
+            @pl.when(r == place)
+            def _():
+                local(cot_ref.at[rows_at], in_s.at[slot, :, y_part], c_sem.at[slot]).start()
+
 
     def fetched(slot):
         local(mine_ref.at[0], in_s.at[slot, :, x_part], x_sem.at[slot]).wait()
-        local(cot_ref.at[0, pl.ds(0, rows)], in_s.at[slot, :, y_part], c_sem.at[slot]).wait()
+        local(cot_refs[0].at[pl.ds(0, rows)], in_s.at[slot, :, y_part], c_sem.at[slot]).wait()
 
     def load(e, slot):
         return local(acc_ref.at[e], acc_s.at[slot], load_sem.at[slot])
@@ -575,7 +589,7 @@
 
 def moe(own, cot, picks, wg, wu, wd, outer, chunks, slots, all_experts):
     rows, full = own.shape
-    width = cot.shape[2]
+    width = cot[0].shape[1]
     extra = full - width
     span = full + width
     experts, _, hidden = wg.shape
@@ -588,8 +602,7 @@
 
     anywhere = pl.BlockSpec(memory_space=pl.ANY)
     in_specs = [
-        anywhere,
-        anywhere,
+        *[anywhere] * (1 + len(cot)),
         pl.BlockSpec(picks.shape, lambda j, s: (0, 0)),
         pl.BlockSpec((1, width, hidden), expert_at),
         pl.BlockSpec((1, width, hidden), expert_at),
@@ -658,7 +671,7 @@
             flops=flops, bytes_accessed=blocks * chunks * rows * full * 8, transcendentals=0
         ),
         name="moe",
-    )(own, cot, picks, wg, wu, wd)
+    )(own, *cot, picks, wg, wu, wd)
     return results[:2]
 
 
@@ -675,11 +688,15 @@
 
 
 def ring_sum(values, count):
-    total = wide(values)
+    total = values
     for step in range(1, count):
         pairs = [(i, (i + step) % count) for i in range(count)]
-        total = total + wide(lax.ppermute(low(values), "tensor", pairs))
+        total = total + lax.ppermute(values, "tensor", pairs)
     return total
+
+
+def pick(values, at, axis):
+    return lax.dynamic_index_in_dim(values, at, axis, keepdims=False)
 
 
 class Plane:
@@ -699,6 +716,32 @@
 
     def swap_core(self, values):
         return lax.ppermute(values, "dp", self.core)
+
+    def push(self, values, k):
+        pairs = [(i, (i + 4 * k) % self.count) for i in range(self.count)]
+        return lax.ppermute(values, "dp", pairs)
+
+    def fold_inner(self, parts, b, axis, kind):
+        given = self.swap_inner(pick(parts, 1 - b, axis).astype(kind))
+        return wide(pick(parts, b, axis)) + wide(given)
+
+    def fold_outer(self, parts, a, kind):
+        total = wide(pick(parts, a, 0))
+        for k in range(1, self.outer):
+            given = pick(parts, (a + k) % self.outer, 0).astype(kind)
+            total = total + wide(self.push(given, k))
+        return total
+
+    def scatter(self, values, inner_first):
+        kind = values.dtype
+        index = lax.axis_index("dp")
+        core, b, a = index % 2, index // 2 % 2, index // 4
+        parts = values.reshape(self.outer, 2, 2, values.shape[0] // self.count, values.shape[1])
+        given = self.swap_core(pick(parts, 1 - core, 2))
+        parts = (wide(pick(parts, core, 2)) + wide(given)).astype(kind)
+        if inner_first:
+            return self.fold_outer(self.fold_inner(parts, b, 1, kind).astype(kind), a, kind)
+        return self.fold_inner(self.fold_outer(parts, a, kind).astype(kind), b, 0, kind)
 
     def first(self, own):
         return self.swap_inner(own), [self.pull(own, k) for k in range(1, self.outer)]
@@ -758,7 +801,11 @@
     gathered = lax.all_gather(normed, "tensor", axis=0, tiled=True)
     plane = Plane(data_count)
     near, fars = plane.first(cotangent[0])
-    gathered, near, fars = tie(gathered, near, fars)
+    core = lax.axis_index("dp") % 2
+    depth = width // 2
+    out_half = lax.dynamic_slice_in_dim(w_out, core * depth, depth, 0)
+    gathered, near, fars, out_half = tie(gathered, near, fars, out_half)
+    out_mine = lax.all_gather(out_half, "tensor", axis=0)
     query_unrotated = jnp.dot(gathered, w_query, preferred_element_type=jnp.float32)
     key_raw = jnp.dot(gathered, w_key, preferred_element_type=jnp.float32)
     value_raw = jnp.dot(gathered, w_value, preferred_element_type=jnp.float32)
@@ -791,15 +838,21 @@
     diagonals = plane.second(near, fars)
     attended, diagonals = tie(attended, diagonals)
     cot_all = plane.third(cotangent[0], near, fars, diagonals)
-    attn_own = lax.psum_scatter(
-        jnp.einsum("lh,dh->ld", attended, w_out, preferred_element_type=jnp.float32).astype(
-            jnp.bfloat16
-        ),
-        "tensor",
-        scatter_dimension=0,
-        tiled=True,
-    ).astype(jnp.float32)
-    cot_all = jnp.stack(cot_all)
+    out_other = plane.swap_core(out_mine)
+    heads_own = lax.all_to_all(
+        attended.reshape(tensor_count, block_rows, local_width), "tensor", 0, 0
+    )
+    heads_own = heads_own.reshape(tensor_count, block_rows, local_width)
+
+    def from_heads(out_weight):
+        return sum(dot_nt(heads_own[t], out_weight[t]) for t in range(tensor_count))
+
+    attn_mine, attn_other = from_heads(out_mine), from_heads(out_other)
+    attn_own = jnp.where(
+        core == 0,
+        jnp.concatenate([attn_mine, attn_other], axis=1),
+        jnp.concatenate([attn_other, attn_mine], axis=1),
+    )
     residual = token_values + own_valid[:, None] * attn_own
     moe_own = rms_scale(residual, ffn_gain).astype(jnp.bfloat16)
     router_logits = jnp.dot(moe_own, router_weight, preferred_element_type=jnp.float32)
@@ -867,10 +920,17 @@
     grad_res_norm, ffn_part = ffn_pull(grad_moe)
     grad_residual = grad_own + grad_res_norm
     grad_attn = (grad_residual * own_valid[:, None]).astype(jnp.bfloat16)
+    attn_lower = lax.dynamic_slice_in_dim(grad_attn, core * depth, depth, 1)
+    attn_upper = lax.dynamic_slice_in_dim(grad_attn, depth - core * depth, depth, 1)
+    grad_heads = jnp.stack(
+        [
+            low(dot_nn(attn_lower, out_mine[t]) + dot_nn(attn_upper, out_other[t]))
+            for t in range(tensor_count)
+        ]
+    )
+    grad_mixed = lax.all_to_all(grad_heads, "tensor", 0, 0)
+    grad_mixed, grad_attn = tie(grad_mixed, grad_attn)
     grad_attn_all = lax.all_gather(grad_attn, "tensor", axis=0, tiled=True)
-    grad_mixed = jnp.dot(grad_attn_all, w_out, preferred_element_type=jnp.float32).astype(
-        jnp.bfloat16
-    )
     grad_mixed = grad_mixed.reshape(full_length, -1, head_dim)
     out_part = jnp.einsum("ld,lh->dh", grad_attn_all, attended, preferred_element_type=jnp.float32)
     grad_query_parts = []
@@ -914,15 +974,6 @@
     from_query = jnp.einsum("lh,dh->ld", grad_q_low, w_query, preferred_element_type=jnp.float32)
     from_key = jnp.einsum("lh,dh->ld", grad_k_low, w_key, preferred_element_type=jnp.float32)
     from_value = jnp.einsum("lh,dh->ld", grad_v_low, w_value, preferred_element_type=jnp.float32)
-    early = jnp.concatenate(
-        [
-            low(out_part),
-            low(value_part),
-            low(ring_sum(jnp.concatenate([router_part, ffn_part[:, None]], axis=1), tensor_count)),
-        ],
-        axis=1,
-    )
-    early = wide(lax.psum_scatter(early, "dp", scatter_dimension=0, tiled=True))
     grad_normed = wide(
         lax.psum_scatter(
             low(from_query + from_key + from_value), "tensor", scatter_dimension=0, tiled=True
@@ -931,27 +982,28 @@
     attn_pull = jax.vjp(rms_scale, token_values, attn_gain)[1]
     grad_tok_norm, attn_part = attn_pull(grad_normed)
     grad_tokens = (grad_residual + grad_tok_norm).astype(jnp.bfloat16)
-    piece = head_dim // data_count
-    gains = jnp.stack([q_part, k_part]).reshape(2, data_count, piece)
-    gains = jnp.pad(gains, ((0, 0), (0, 0), (0, width // data_count - piece)))
-    small = jnp.concatenate([attn_part[:, None], gains.reshape(2, width).T], axis=1)
-    late = jnp.concatenate(
-        [low(query_part), low(key_part), low(ring_sum(small, tensor_count))], axis=1
-    )
-    late = wide(lax.psum_scatter(late, "dp", scatter_dimension=0, tiled=True))
-    end = 2 * local_width
+    grad_out = plane.scatter(low(out_part), True)
+    grad_value = plane.scatter(low(value_part), False)
+    grad_query = plane.scatter(low(query_part), True)
+    grad_key = plane.scatter(low(key_part), False)
+    routing = plane.scatter(jnp.concatenate([router_part, ffn_part[:, None]], axis=1), False)
+    routing = ring_sum(routing, tensor_count)
+    parts = [v.reshape(data_count, -1) for v in (attn_part, q_part, k_part)]
+    gains = ring_sum(plane.scatter(jnp.concatenate(parts, axis=1), True), tensor_count)[0]
+    piece = width // data_count
+    last = piece + head_dim // data_count
     return (
         output[None],
         grad_tokens[None],
-        late[:, end],
-        late[:, :local_width],
-        late[:, local_width:end],
-        early[:, local_width:end],
-        early[:, :local_width],
-        late[:piece, end + 1],
-        late[:piece, end + 2],
-        early[:, end + all_experts],
-        early[:, end : end + all_experts],
+        gains[:piece],
+        grad_query,
+        grad_key,
+        grad_value,
+        grad_out,
+        gains[piece:last],
+        gains[last:],
+        routing[:, all_experts],
+        routing[:, :all_experts],
         grad_gate,
         grad_up,
         grad_down,

time: 1210 us -> 1110 us (0.917)
  waiting for transfers between devices: 330 us -> 201 us
  starting transfers between devices: 18.7 us -> 38.3 us
  matrix products: 96 us -> 114 us
    ppermute x2 -> x8, waiting for transfers between devices: 8.44 us -> 99.3 us  [swap_inner(): return lax.ppermute(values, 'dp', self.inner)]
    reduce_scatter x3 -> x0, waiting for transfers between devices: 88.4 us -> none  [the longest x1 42 us: per_device(): lax.psum_scatter(jnp.einsum('lh,dh->ld', attended, w_out, preferred_eleme...]
    ppermute x2, waiting for transfers between devices: 88 us -> 1.46 us  [pull(): return lax.ppermute(values, 'dp', pairs)]
    all_gather x1, waiting for transfers between devices: 81.4 us -> 0.01 us  [per_device(): grad_attn_all = lax.all_gather(grad_attn, 'tensor', axis=0, tiled=True)]
    all_gather x0 -> x1, waiting for transfers between devices: none -> 39 us  [per_device(): out_mine = lax.all_gather(out_half, 'tensor', axis=0)]
    all_to_all x0 -> x2, waiting for transfers between devices: none -> 38.2 us  [the longest x1 23.4 us: per_device(): lax.all_to_all(attended.reshape(tensor_count, block_rows, local_width), '...]
    reduce_scatter x1, waiting for transfers between devices: 38.3 us -> 1.21 us  [per_device(): lax.psum_scatter(low(from_query + from_key + from_value), 'tensor', scatt...]
    unnamed x182 -> x196, local copies, waits for them, and re-layouts: 58.6 us -> 32.1 us
  transfers between devices with their start and end apart: 20 -> 39, of which waited for: 11 -> 16; matrix products, arithmetic and copies ran while one was open for 12% -> 22% of each run, Pallas kernels for 0% -> 0%
where the time goes in v3:
time: 1110 us; the launch traced here: 1100 us
  Pallas kernels  568 us (51%)
  waiting for transfers between devices  201 us (18%)
  matrix products  114 us (10%)
  local copies, waits for them, and re-layouts  91 us (8%)
  other arithmetic  72 us (6%)
  starting transfers between devices  38.3 us (3%)
  between operations  16.4 us (1%)
    pallas_call x1, Pallas kernels, moe(): pl.pallas_call(functools.partial(moe_kernel, sizes), grid=(chunks, 2 * bl...  568 us
    ppermute x8, waiting for transfers between devices, swap_inner(): return lax.ppermute(values, 'dp', self.inner)  99.3 us
    all_gather x1, waiting for transfers between devices, per_device(): out_mine = lax.all_gather(out_half, 'tensor', axis=0)  39 us
    unnamed x196, local copies, waits for them, and re-layouts  32.1 us
    all_to_all x1, waiting for transfers between devices, per_device(): lax.all_to_all(attended.reshape(tensor_count, block_rows, local_width), '...  23.4 us
  transfers between devices with their start and end apart: 39, of which 16 were waited for; matrix products, arithmetic and copies ran while one was open for 22% of the time, Pallas kernels for 0%

profile of v3, /device:TPU:0, one launch (start us, length us, event | category | flops | bytes accessed | tf_op | source)
XLA Modules:
  0.0 1101.2 jit_solution(17419886869469087884)
XLA Ops:
  20.8 85.7 %collective-permute-done.others_refs_1_ = bf16[1024,2048]{1,0:T(8,128)(2,1)} collective-permute-done((bf16[1024,2048]{1,0:T(8,128)(2,1)}, bf16[1024,2048]{1,0:T(8,128)(2,1)}, u32[]{:S(2)}, u32[]{:S(2)}) %collective-permute-start) | collective-permute-done | bytes 4194336 | tf_op jit(solution)/shard_map/ppermute | solution.py:715
  108.0 5.4 multiply_reduce_fusion.10
  113.5 3.8 multiply_reduce_fusion.9
  121.2 3.9 slice.135
  142.5 4.0 fusion
  150.2 39.0 %all-gather.9.cloned.1.call-done = bf16[4096,512]{1,0:T(8,128)(2,1)} async-done(((bf16[1024,512]{1,0:T(8,128)(2,1)}), bf16[4096,512]{1,0:T(8,128)(2,1)}) %all-gather.9.cloned.1.call-update) | async-done | bytes 4194320 | tf_op jit(solution)/shard_map/all_gather | solution.py:808
  189.2 4.8 fusion.39
  194.2 5.2 pad_maximum_fusion.others_refs_3_
  200.7 3.5 all-to-all-start
  207.4 23.4 %all-to-all-done = bf16[4,256,512]{2,1,0:T(8,128)(2,1)S(1)} async-done(((bf16[4,256,512]{2,1,0:T(8,128)(2,1)}), bf16[4,256,512]{2,1,0:T(8,128)(2,1)S(1)}, u32[]{:S(2)}, u32[]{:S(2)}) %all-to-all-start) | async-done | bytes 1048608 | tf_op jit(solution)/shard_map/all_to_all | solution.py:842
  246.8 568.5 %moe.1 = (bf16[256,4224]{1,0:T(8,128)(2,1)}, f32[4,3,256,2048]{3,2,1,0:T(8,128)}, bf16[4,256,2176]{2,1,0:T(8,128)(2,1)}, bf16[4,7,256,2176]{3,2,1,0:T(8,128)(2,1...) custom-call(bf16[256,2176]{1,0:T(8,128)(2,1)} %concatenate.49.own_re, ...), custom_call_target="tpu_custom_call" | custom-call | flops 139586437120 | bytes 142606336 | tf_op jit(solution)/shard_map/moe/pallas_call | solution.py:657
  835.1 4.9 all-to-all-start.1
  851.3 14.7 %all-to-all-done.1 = bf16[4,256,512]{2,1,0:T(8,128)(2,1)} async-done(((bf16[4,256,512]{2,1,0:T(8,128)(2,1)}), bf16[4,256,512]{2,1,0:T(8,128)(2,1)}, u32[]{:S(2)}, u32[]{:S(2)}) %all-to-all-start.1) | async-done | bytes 1048608 | tf_op jit(solution)/shard_map/all_to_all | solution.py:931
  872.3 5.7 fusion.141
  882.1 10.9 multiply_reduce_fusion.1
  893.0 10.2 multiply_convert_fusion.1
  909.3 4.2 fusion.133
  915.7 3.8 multiply_add_fusion.1
  924.7 3.9 multiply_reduce_fusion.3
  932.7 4.5 fusion.142
  937.2 5.8 fusion.143
  948.7 8.1 add_convert_fusion
  956.8 17.8 %slice_bitcast_fusion = (f32[4,256,2048]{2,1,0:T(8,128)}, f32[4,2048,256]{1,2,0:T(8,128)}, f32[4,2048,256]{1,2,0:T(8,128)}) fusion(f32[4,3,256,2048]{3,2,1,0:T(8,128)} %get-tuple-element.33), kind=kLoop, calls=%fused_computation | loop fusion | bytes 50331648 | tf_op jit(solution)/shard_map/squeeze | solution.py:907
  974.6 8.7 copy.176
  983.3 8.8 copy.177
  994.3 5.2 convolution_convert_fusion.3
  1023.6 4.7 convolution_convert_fusion
  1036.9 8.3 collective-permute-done.22
  1051.7 4.0 collective-permute-done.23
  1056.5 7.9 collective-permute-done.25
  1073.3 5.7 collective-permute-done.26
  1088.9 4.4 fusion.51
  (406 shorter events, 185.7 us)
Async XLA Ops:
  7.2 100.8 %all-gather.5.cloned.1.call-start = ((), (), s32[]{:S(2)}) async-start(), calls=%async_computation.3 | async-start | bytes 5242880 | tf_op jit(solution)/shard_map/all_gather | solution.py:801
  12.6 176.7 %all-gather.9.cloned.1.call-start = ((), (), s32[]{:S(2)}) async-start(), calls=%async_computation.6 | async-start | bytes 5242880 | tf_op jit(solution)/shard_map/all_gather | solution.py:808
  12.6 93.9 %collective-permute-start = (bf16[1024,2048]{1,0:T(8,128)(2,1)}, bf16[1024,2048]{1,0:T(8,128)(2,1)}, u32[]{:S(2)}, u32[]{:S(2)}) collective-permute-start(bf16[1024,2048]{1,0:T(8,128)(2,1)} %bitcast.291), channel_id=1, source_target_pairs={{0,8},{4,12},{8,0},{12,4},{16,24},{20,28},{24,16},{28,20},{1,9},{5... | collective-permute-start | bytes 12582920 | tf_op jit(solution)/shard_map/ppermute | solution.py:715
  15.6 92.3 %collective-permute-start.1 = (bf16[1024,2048]{1,0:T(8,128)(2,1)}, bf16[1024,2048]{1,0:T(8,128)(2,1)}, u32[]{:S(2)}, u32[]{:S(2)}) collective-permute-start(bf16[1024,2048]{1,0:T(8,128)(2,1)} %bitcast.292), channel_id=1, source_target_pairs={{16,0},{20,4},{24,8},{28,12},{0,16},{4,20},{8,24},{12,28},{17,1},{... | collective-permute-start | bytes 12582920 | tf_op jit(solution)/shard_map/ppermute | solution.py:712
  125.1 69.1 %collective-permute-start.3 = (bf16[512,2048]{1,0:T(8,128)(2,1)}, bf16[512,2048]{1,0:T(8,128)(2,1)}, u32[]{:S(2)}, u32[]{:S(2)}) collective-permute-start(bf16[512,2048]{1,0:T(8,128)(2,1)} %slice.135), channel_id=1, source_target_pairs={{0,8},{4,12},{8,0},{12,4},{16,24},{20,28},{24,16},{28,20},{1,9},{5... | collective-permute-start | bytes 6291464 | tf_op jit(solution)/shard_map/ppermute | solution.py:715
  128.9 65.3 %collective-permute-start.2 = (bf16[512,2048]{1,0:T(8,128)(2,1)}, bf16[512,2048]{1,0:T(8,128)(2,1)}, u32[]{:S(2)}, u32[]{:S(2)}) collective-permute-start(bf16[512,2048]{1,0:T(8,128)(2,1)} %slice.134), channel_id=1, source_target_pairs={{16,0},{20,4},{24,8},{28,12},{0,16},{4,20},{8,24},{12,28},{17,1},{... | collective-permute-start | bytes 6291464 | tf_op jit(solution)/shard_map/ppermute | solution.py:712
  189.2 46.2 %collective-permute-start.4 = (bf16[4,1024,512]{2,1,0:T(8,128)(2,1)}, bf16[4,1024,512]{2,1,0:T(8,128)(2,1)}, u32[]{:S(2)}, u32[]{:S(2)}) collective-permute-start(bf16[4,1024,512]{2,1,0:T(8,128)(2,1)} %bitcast.272), channel_id=1, source_target_pairs={{0,4},{4,0},{8,12},{12,8},{16,20},{20,16},{24,28},{28,24},{1,5},{5... | collective-permute-start | bytes 12582920 | tf_op jit(solution)/shard_map/ppermute | solution.py:718
  200.7 30.2 %all-to-all-start = ((bf16[4,256,512]{2,1,0:T(8,128)(2,1)}), bf16[4,256,512]{2,1,0:T(8,128)(2,1)S(1)}, u32[]{:S(2)}, u32[]{:S(2)}) async-start(bf16[4,256,512]{2,1,0:T(8,128)(2,1)} %bitcast.10), calls=%async_computation | async-start | bytes 2097152 | tf_op jit(solution)/shard_map/all_to_all | solution.py:842
  204.2 42.5 %collective-permute-start.5 = (bf16[1024,2048]{1,0:T(8,128)(2,1)}, bf16[1024,2048]{1,0:T(8,128)(2,1)}, u32[]{:S(2)}, u32[]{:S(2)}) collective-permute-start(bf16[1024,2048]{1,0:T(8,128)(2,1)} %bitcast.293), channel_id=1, source_target_pairs={{0,4},{4,0},{8,12},{12,8},{16,20},{20,16},{24,28},{28,24},{1,5},{5... | collective-permute-start | bytes 12582920 | tf_op jit(solution)/shard_map/ppermute | solution.py:718
  206.8 39.9 %collective-permute-start.6 = (bf16[1024,2048]{1,0:T(8,128)(2,1)}, bf16[1024,2048]{1,0:T(8,128)(2,1)}, u32[]{:S(2)}, u32[]{:S(2)}) collective-permute-start(bf16[1024,2048]{1,0:T(8,128)(2,1)} %collective-permute-done.others_refs_1_), channel_id=1, source_target_pairs={{0,4},{4,0},{8,12},{12,8},{16,20},{20,16},{24,28},{28,24},{1,5},{5... | collective-permute-start | bytes 12582920 | tf_op jit(solution)/shard_map/ppermute | solution.py:718
  206.9 39.8 %collective-permute-start.7 = (bf16[1024,2048]{1,0:T(8,128)(2,1)}, bf16[1024,2048]{1,0:T(8,128)(2,1)}, u32[]{:S(2)}, u32[]{:S(2)}) collective-permute-start(bf16[1024,2048]{1,0:T(8,128)(2,1)} %collective-permute-done.1.others_refs_2_), channel_id=1, source_target_pairs={{0,4},{4,0},{8,12},{12,8},{16,20},{20,16},{24,28},{28,24},{1,5},{5... | collective-permute-start | bytes 12582920 | tf_op jit(solution)/shard_map/ppermute | solution.py:718
  207.3 39.4 %collective-permute-start.8 = (bf16[1024,2048]{1,0:T(8,128)(2,1)}, bf16[1024,2048]{1,0:T(8,128)(2,1)}, u32[]{:S(2)}, u32[]{:S(2)}) collective-permute-start(bf16[1024,2048]{1,0:T(8,128)(2,1)} %pad_maximum_fusion.others_refs_3_), channel_id=1, source_target_pairs={{0,4},{4,0},{8,12},{12,8},{16,20},{20,16},{24,28},{28,24},{1,5},{5... | collective-permute-start | bytes 12582920 | tf_op jit(solution)/shard_map/ppermute | solution.py:718
  835.1 30.9 %all-to-all-start.1 = ((bf16[4,256,512]{2,1,0:T(8,128)(2,1)}), bf16[4,256,512]{2,1,0:T(8,128)(2,1)}, u32[]{:S(2)}, u32[]{:S(2)}) async-start(bf16[4,256,512]{2,1,0:T(8,128)(2,1)} %pad_maximum_fusion.4), calls=%async_computation.1 | async-start | bytes 2097152 | tf_op jit(solution)/shard_map/all_to_all | solution.py:931
  840.0 183.6 %all-gather.7.cloned.1.call-start = ((), (), s32[]{:S(2)}) async-start(), calls=%async_computation.5 | async-start | bytes 5242880 | tf_op jit(solution)/shard_map/all_gather | solution.py:933
  850.4 141.7 %collective-permute-start.29 = (f32[256,33]{0,1:T(8,128)S(1)}, f32[256,33]{0,1:T(8,128)S(1)}, u32[]{:S(2)}, u32[]{:S(2)}) collective-permute-start(f32[256,33]{0,1:T(8,128)S(1)} %dynamic-slice_bitcast_fusion.11), channel_id=1, source_target_pairs={{0,8},{4,12},{8,0},{12,4},{16,24},{20,28},{24,16},{28,20},{1,9},{5... | collective-permute-start | bytes 101384 | tf_op jit(solution)/shard_map/ppermute | solution.py:715
  909.2 157.4 %reduce-scatter.2.cloned.1.call-start = ((), (), s32[]{:S(2)}) async-start(), calls=%async_computation.4 | async-start | bytes 5242880 | tf_op jit(solution)/shard_map/reduce_scatter | solution.py:978
  992.1 19.8 %collective-permute-start.32 = (f32[256,33]{0,1:T(8,128)S(1)}, f32[256,33]{0,1:T(8,128)S(1)}, u32[]{:S(2)}, u32[]{:S(2)}) collective-permute-start(f32[256,33]{0,1:T(8,128)S(1)} %bitcast_add_fusion.1), channel_id=1, source_target_pairs={{0,3},{1,0},{2,1},{3,2},{4,7},{5,4},{6,5},{7,6},{8,11},{9,8},{10,9... | collective-permute-start | bytes 101384 | tf_op jit(solution)/shard_map/ppermute | solution.py:694
  993.4 18.7 %collective-permute-start.31 = (f32[256,33]{0,1:T(8,128)S(1)}, f32[256,33]{0,1:T(8,128)S(1)}, u32[]{:S(2)}, u32[]{:S(2)}) collective-permute-start(f32[256,33]{0,1:T(8,128)S(1)} %bitcast_add_fusion.1), channel_id=1, source_target_pairs={{0,2},{1,3},{2,0},{3,1},{4,6},{5,7},{6,4},{7,5},{8,10},{9,11},{10,... | collective-permute-start | bytes 101384 | tf_op jit(solution)/shard_map/ppermute | solution.py:694
  993.4 18.7 %collective-permute-start.30 = (f32[256,33]{0,1:T(8,128)S(1)}, f32[256,33]{0,1:T(8,128)S(1)}, u32[]{:S(2)}, u32[]{:S(2)}) collective-permute-start(f32[256,33]{0,1:T(8,128)S(1)} %bitcast_add_fusion.1), channel_id=1, source_target_pairs={{0,1},{1,2},{2,3},{3,0},{4,5},{5,6},{6,7},{7,4},{8,9},{9,10},{10,1... | collective-permute-start | bytes 101384 | tf_op jit(solution)/shard_map/ppermute | solution.py:694
  1000.7 12.8 %collective-permute-start.15 = (bf16[2,2,256,512]{3,2,0,1:T(8,128)(2,1)}, bf16[2,2,256,512]{3,2,0,1:T(8,128)(2,1)}, u32[]{:S(2)}, u32[]{:S(2)}) collective-permute-start(bf16[2,2,256,512]{3,2,0,1:T(8,128)(2,1)} %bitcast.260), channel_id=1, source_target_pairs={{0,4},{4,0},{8,12},{12,8},{16,20},{20,16},{24,28},{28,24},{1,5},{5... | collective-permute-start | bytes 3145736 | tf_op jit(solution)/shard_map/ppermute | solution.py:718
  1006.6 9.6 collective-permute-start.18
  1016.0 14.5 %collective-permute-start.16 = (bf16[2,256,512]{2,1,0:T(8,128)(2,1)}, bf16[2,256,512]{2,1,0:T(8,128)(2,1)}, u32[]{:S(2)}, u32[]{:S(2)}) collective-permute-start(bf16[2,256,512]{2,1,0:T(8,128)(2,1)} %dynamic-slice_bitcast_fusion.5), channel_id=1, source_target_pairs={{0,8},{4,12},{8,0},{12,4},{16,24},{20,28},{24,16},{28,20},{1,9},{5... | collective-permute-start | bytes 1572872 | tf_op jit(solution)/shard_map/ppermute | solution.py:715
  1018.8 15.1 %collective-permute-start.19 = (bf16[2,256,512]{2,1,0:T(8,128)(2,1)}, bf16[2,256,512]{2,1,0:T(8,128)(2,1)}, u32[]{:S(2)}, u32[]{:S(2)}) collective-permute-start(bf16[2,256,512]{2,1,0:T(8,128)(2,1)} %dynamic-slice_bitcast_fusion.4), channel_id=1, source_target_pairs={{0,16},{4,20},{8,24},{12,28},{16,0},{20,4},{24,8},{28,12},{1,17},{... | collective-permute-start | bytes 1572872 | tf_op jit(solution)/shard_map/ppermute | solution.py:722
  1023.0 22.1 %collective-permute-start.22 = (bf16[2,256,512]{2,1,0:T(8,128)(2,1)}, bf16[2,256,512]{2,1,0:T(8,128)(2,1)}, u32[]{:S(2)}, u32[]{:S(2)}) collective-permute-start(bf16[2,256,512]{2,1,0:T(8,128)(2,1)} %dynamic-slice_bitcast_fusion.3), channel_id=1, source_target_pairs={{0,16},{4,20},{8,24},{12,28},{16,0},{20,4},{24,8},{28,12},{1,17},{... | collective-permute-start | bytes 1572872 | tf_op jit(solution)/shard_map/ppermute | solution.py:722
  1028.7 19.4 %collective-permute-start.24 = (bf16[2,2,256,512]{3,2,0,1:T(8,128)(2,1)S(1)}, bf16[2,2,256,512]{3,2,0,1:T(8,128)(2,1)S(1)}, u32[]{:S(2)}, u32[]{:S(2)}) collective-permute-start(bf16[2,2,256,512]{3,2,0,1:T(8,128)(2,1)S(1)} %bitcast.290), channel_id=1, source_target_pairs={{0,4},{4,0},{8,12},{12,8},{16,20},{20,16},{24,28},{28,24},{1,5},{5... | collective-permute-start | bytes 3145736 | tf_op jit(solution)/shard_map/ppermute | solution.py:718
  1031.7 18.2 %collective-permute-start.17 = (bf16[256,512]{1,0:T(8,128)(2,1)S(1)}, bf16[256,512]{1,0:T(8,128)(2,1)S(1)}, u32[]{:S(2)}, u32[]{:S(2)}) collective-permute-start(bf16[256,512]{1,0:T(8,128)(2,1)S(1)} %dynamic-slice_bitcast_fusion.9), channel_id=1, source_target_pairs={{0,16},{4,20},{8,24},{12,28},{16,0},{20,4},{24,8},{28,12},{1,17},{... | collective-permute-start | bytes 786440 | tf_op jit(solution)/shard_map/ppermute | solution.py:722
  1035.2 15.6 %collective-permute-start.20 = (bf16[256,512]{1,0:T(8,128)(2,1)S(1)}, bf16[256,512]{1,0:T(8,128)(2,1)S(1)}, u32[]{:S(2)}, u32[]{:S(2)}) collective-permute-start(bf16[256,512]{1,0:T(8,128)(2,1)S(1)} %dynamic-slice_bitcast_fusion.8), channel_id=1, source_target_pairs={{0,8},{4,12},{8,0},{12,4},{16,24},{20,28},{24,16},{28,20},{1,9},{5... | collective-permute-start | bytes 786440 | tf_op jit(solution)/shard_map/ppermute | solution.py:715
  1046.4 9.2 collective-permute-start.23
  1048.5 15.9 %collective-permute-start.25 = (bf16[2,256,512]{2,1,0:T(8,128)(2,1)S(1)}, bf16[2,256,512]{2,1,0:T(8,128)(2,1)S(1)}, u32[]{:S(2)}, u32[]{:S(2)}) collective-permute-start(bf16[2,256,512]{2,1,0:T(8,128)(2,1)S(1)} %dynamic-slice_bitcast_fusion.2), channel_id=1, source_target_pairs={{0,8},{4,12},{8,0},{12,4},{16,24},{20,28},{24,16},{28,20},{1,9},{5... | collective-permute-start | bytes 1572872 | tf_op jit(solution)/shard_map/ppermute | solution.py:715
  1070.2 8.8 collective-permute-start.26
  1071.7 9.0 collective-permute-start.10
  1084.4 8.9 collective-permute-start.14
  (104 other events, 1290.5 us)
Sparse Core Ops, SparseCore 0:
  12.7 83.4 all-gather.4
  108.1 81.0 all-gather.8
  909.3 78.8 all-gather.6
  990.4 76.1 reduce-scatter.1

commit v4 on v3

--- a/solution.py
+++ b/solution.py
@@ -838,10 +838,11 @@
     diagonals = plane.second(near, fars)
     attended, diagonals = tie(attended, diagonals)
     cot_all = plane.third(cotangent[0], near, fars, diagonals)
-    out_other = plane.swap_core(out_mine)
     heads_own = lax.all_to_all(
         attended.reshape(tensor_count, block_rows, local_width), "tensor", 0, 0
     )
+    heads_own, out_mine = tie(heads_own, out_mine)
+    out_other = plane.swap_core(out_mine)
     heads_own = heads_own.reshape(tensor_count, block_rows, local_width)
 
     def from_heads(out_weight):
@@ -902,9 +903,6 @@
         all_experts,
     )
     combined = wide(combined)
-    grad_gate = jnp.swapaxes(sums[:, 0], 1, 2)
-    grad_up = jnp.swapaxes(sums[:, 1], 1, 2)
-    grad_down = sums[:, 2]
     grad_moe = combined[:, :width]
     grad_probs = combined[:, width : width + all_experts]
     output = low(residual + combined[:, width + extra :])
@@ -932,7 +930,6 @@
     grad_mixed, grad_attn = tie(grad_mixed, grad_attn)
     grad_attn_all = lax.all_gather(grad_attn, "tensor", axis=0, tiled=True)
     grad_mixed = grad_mixed.reshape(full_length, -1, head_dim)
-    out_part = jnp.einsum("ld,lh->dh", grad_attn_all, attended, preferred_element_type=jnp.float32)
     grad_query_parts = []
     grad_keys = jnp.zeros(key_low.shape, jnp.float32)
     grad_values = jnp.zeros(value_low.shape, jnp.float32)
@@ -974,11 +971,16 @@
     from_query = jnp.einsum("lh,dh->ld", grad_q_low, w_query, preferred_element_type=jnp.float32)
     from_key = jnp.einsum("lh,dh->ld", grad_k_low, w_key, preferred_element_type=jnp.float32)
     from_value = jnp.einsum("lh,dh->ld", grad_v_low, w_value, preferred_element_type=jnp.float32)
+    grad_gathered, grad_attn_all, sums, router_part = tie(
+        low(from_query + from_key + from_value), grad_attn_all, sums, router_part
+    )
     grad_normed = wide(
-        lax.psum_scatter(
-            low(from_query + from_key + from_value), "tensor", scatter_dimension=0, tiled=True
-        )
-    )
+        lax.psum_scatter(grad_gathered, "tensor", scatter_dimension=0, tiled=True)
+    )
+    grad_gate = jnp.swapaxes(sums[:, 0], 1, 2)
+    grad_up = jnp.swapaxes(sums[:, 1], 1, 2)
+    grad_down = sums[:, 2]
+    out_part = jnp.einsum("ld,lh->dh", grad_attn_all, attended, preferred_element_type=jnp.float32)
     attn_pull = jax.vjp(rms_scale, token_values, attn_gain)[1]
     grad_tok_norm, attn_part = attn_pull(grad_normed)
     grad_tokens = (grad_residual + grad_tok_norm).astype(jnp.bfloat16)
@@ -989,7 +991,8 @@
     routing = plane.scatter(jnp.concatenate([router_part, ffn_part[:, None]], axis=1), False)
     routing = ring_sum(routing, tensor_count)
     parts = [v.reshape(data_count, -1) for v in (attn_part, q_part, k_part)]
-    gains = ring_sum(plane.scatter(jnp.concatenate(parts, axis=1), True), tensor_count)[0]
+    gains = jnp.repeat(jnp.concatenate(parts, axis=1), tensor_count, axis=0)
+    gains = jnp.sum(lax.all_to_all(gains, ("dp", "tensor"), 0, 0, tiled=True), axis=0)
     piece = width // data_count
     last = piece + head_dim // data_count
     return (

time: 1110 us -> 1070 us (0.964)
  blocking collectives: 0 us -> 43.4 us
  waiting for transfers between devices: 201 us -> 158 us
  Pallas kernels: 568 us -> 552 us
    ppermute x2, waiting for transfers between devices: 1.46 us -> 86.9 us  [pull(): return lax.ppermute(values, 'dp', pairs)]
    ppermute x8 -> x7, waiting for transfers between devices: 99.3 us -> 16.3 us  [swap_inner(): return lax.ppermute(values, 'dp', self.inner)]
    all_to_all x0 -> x1, blocking collectives: none -> 43.4 us  [per_device(): lax.all_to_all(attended.reshape(tensor_count, block_rows, local_width), '...]
    all_gather x1, waiting for transfers between devices: 39 us -> 0.01 us  [per_device(): out_mine = lax.all_gather(out_half, 'tensor', axis=0)]
    all_to_all x1, waiting for transfers between devices: 23.4 us -> 2.04 us  [per_device(): lax.all_to_all(gains, ('dp', 'tensor'), 0, 0, tiled=True)]
    pallas_call x1, Pallas kernels: 568 us -> 552 us  [moe(): pl.pallas_call(functools.partial(moe_kernel, sizes), grid=(chunks, 2 * bl...]
    ppermute x11 -> x10, waiting for transfers between devices: 1.37 us -> 12.6 us  [swap_core(): return lax.ppermute(values, 'dp', self.core)]
    unnamed x196 -> x188, local copies, waits for them, and re-layouts: 32.1 us -> 30.7 us
  transfers between devices with their start and end apart: 39 -> 33, of which waited for: 16 -> 14; matrix products, arithmetic and copies ran while one was open for 22% -> 20% of each run, Pallas kernels for 0% -> 0%
where the time goes in v4:
time: 1070 us
  Pallas kernels  552 us (52%)
  waiting for transfers between devices  158 us (15%)
  matrix products  103 us (10%)
  local copies, waits for them, and re-layouts  80.9 us (8%)
  other arithmetic  74.7 us (7%)
  blocking collectives  43.4 us (4%)
  starting transfers between devices  36.3 us (3%)
  between operations  16.7 us (2%)
    pallas_call x1, Pallas kernels, moe(): pl.pallas_call(functools.partial(moe_kernel, sizes), grid=(chunks, 2 * bl...  552 us
    ppermute x2, waiting for transfers between devices, pull(): return lax.ppermute(values, 'dp', pairs)  86.9 us
    all_to_all x1, blocking collectives, per_device(): lax.all_to_all(attended.reshape(tensor_count, block_rows, local_width), '...  43.4 us
    unnamed x188, local copies, waits for them, and re-layouts  30.7 us
    all_to_all x1, waiting for transfers between devices, per_device(): grad_mixed = lax.all_to_all(grad_heads, 'tensor', 0, 0)  22.2 us
  transfers between devices with their start and end apart: 33, of which 14 were waited for; matrix products, arithmetic and copies ran while one was open for 20% of the time, Pallas kernels for 0%

profile of v4, /device:TPU:0, one launch (start us, length us, event | category | flops | bytes accessed | tf_op | source)
XLA Modules:
  0.0 1065.4 jit_solution(3159176224933977498)
XLA Ops:
  20.9 85.7 %collective-permute-done.1.others_refs_2_ = bf16[1024,2048]{1,0:T(8,128)(2,1)} collective-permute-done((bf16[1024,2048]{1,0:T(8,128)(2,1)}, bf16[1024,2048]{1,0:T(8,128)(2,1)}, u32[]{:S(2)}, u32[]{:S(2)}) %collective-permute-start.1) | collective-permute-done | bytes 4194336 | tf_op jit(solution)/shard_map/ppermute | solution.py:712
  108.1 3.3 slice.125
  111.4 3.3 slice.126
  121.5 6.6 multiply_reduce_fusion.10
  130.1 3.7 multiply_multiply_fusion
  146.6 4.2 fusion
  156.6 4.7 collective-permute-done.3
  162.5 4.9 pad_maximum_fusion.others_refs_3_
  167.9 43.4 %all_to_all.19 = bf16[4,256,512]{2,1,0:T(8,128)(2,1)S(1)} all-to-all(bf16[4,256,512]{2,1,0:T(8,128)(2,1)S(1)} %bitcast.276), channel_id=1, replica_groups=mesh['dp'=8,'tensor'=4] {'tensor'}, dimensions={0} | all-to-all | bytes 2097152 | tf_op jit(solution)/shard_map/all_to_all | solution.py:841
  230.8 6.0 collective-permute-done.7.others_refs_6_
  236.8 6.0 collective-permute-done.8.others_refs_7_
  242.8 552.4 %moe.1 = (bf16[256,4224]{1,0:T(8,128)(2,1)}, f32[4,3,256,2048]{3,2,1,0:T(8,128)}, bf16[4,256,2176]{2,1,0:T(8,128)(2,1)}, bf16[4,7,256,2176]{3,2,1,0:T(8,128)(2,1...) custom-call(bf16[256,2176]{1,0:T(8,128)(2,1)} %concatenate.44.own_re, ...), custom_call_target="tpu_custom_call" | custom-call | flops 139586437120 | bytes 142606336 | tf_op jit(solution)/shard_map/moe/pallas_call | solution.py:657
  815.1 9.1 all-to-all-start.1
  825.7 22.2 %all-to-all-done.1 = bf16[4,256,512]{2,1,0:T(8,128)(2,1)S(1)} async-done(((bf16[4,256,512]{2,1,0:T(8,128)(2,1)}), bf16[4,256,512]{2,1,0:T(8,128)(2,1)S(1)}, u32[]{:S(2)}, u32[]{:S(2)}) %all-to-all-start.1) | async-done | bytes 1048608 | tf_op jit(solution)/shard_map/all_to_all | solution.py:929
  850.8 4.7 fusion.151
  855.5 5.8 fusion.4
  868.8 9.8 multiply_reduce_fusion.1
  878.6 8.8 multiply_convert_fusion.1
  893.7 3.4 multiply_add_fusion.1
  903.4 4.1 multiply_reduce_fusion.4
  911.0 4.6 convolution_convert_fusion.2
  923.2 5.7 add_convert_fusion
  930.4 4.8 convolution_convert_fusion.3
  948.1 7.8 collective-permute-done.16
  958.4 8.1 collective-permute-done.13
  971.3 4.6 convolution_convert_fusion
  987.4 10.1 collective-permute-done.23
  1002.8 17.7 %slice_bitcast_fusion = (f32[4,256,2048]{2,1,0:T(8,128)}, f32[4,2048,256]{1,2,0:T(8,128)}, f32[4,2048,256]{1,2,0:T(8,128)}) fusion(f32[4,3,256,2048]{3,2,1,0:T(8,128)} %get-tuple-element.45), kind=kLoop, calls=%fused_computation | loop fusion | bytes 50331648 | tf_op jit(solution)/shard_map/squeeze | solution.py:982
  1020.5 8.7 copy.205
  1029.2 8.8 copy.204
  1046.4 3.4 all-to-all-start.2
  1049.9 5.3 fusion.51
  (386 shorter events, 167.2 us)
Async XLA Ops:
  7.2 100.9 %all-gather.5.cloned.1.call-start = ((), (), s32[]{:S(2)}) async-start(), calls=%async_computation.4 | async-start | bytes 5242880 | tf_op jit(solution)/shard_map/all_gather | solution.py:801
  12.6 198.7 %all-gather.9.cloned.1.call-start = ((), (), s32[]{:S(2)}) async-start(), calls=%async_computation.7 | async-start | bytes 5242880 | tf_op jit(solution)/shard_map/all_gather | solution.py:808
  12.6 94.0 %collective-permute-start.1 = (bf16[1024,2048]{1,0:T(8,128)(2,1)}, bf16[1024,2048]{1,0:T(8,128)(2,1)}, u32[]{:S(2)}, u32[]{:S(2)}) collective-permute-start(bf16[1024,2048]{1,0:T(8,128)(2,1)} %bitcast.292), channel_id=1, source_target_pairs={{16,0},{20,4},{24,8},{28,12},{0,16},{4,20},{8,24},{12,28},{17,1},{... | collective-permute-start | bytes 12582920 | tf_op jit(solution)/shard_map/ppermute | solution.py:712
  15.7 92.3 %collective-permute-start = (bf16[1024,2048]{1,0:T(8,128)(2,1)}, bf16[1024,2048]{1,0:T(8,128)(2,1)}, u32[]{:S(2)}, u32[]{:S(2)}) collective-permute-start(bf16[1024,2048]{1,0:T(8,128)(2,1)} %bitcast.293), channel_id=1, source_target_pairs={{0,8},{4,12},{8,0},{12,4},{16,24},{20,28},{24,16},{28,20},{1,9},{5... | collective-permute-start | bytes 12582920 | tf_op jit(solution)/shard_map/ppermute | solution.py:715
  114.7 46.6 %collective-permute-start.3 = (bf16[512,2048]{1,0:T(8,128)(2,1)}, bf16[512,2048]{1,0:T(8,128)(2,1)}, u32[]{:S(2)}, u32[]{:S(2)}) collective-permute-start(bf16[512,2048]{1,0:T(8,128)(2,1)} %slice.126), channel_id=1, source_target_pairs={{0,8},{4,12},{8,0},{12,4},{16,24},{20,28},{24,16},{28,20},{1,9},{5... | collective-permute-start | bytes 6291464 | tf_op jit(solution)/shard_map/ppermute | solution.py:715
  116.2 46.3 %collective-permute-start.2 = (bf16[512,2048]{1,0:T(8,128)(2,1)}, bf16[512,2048]{1,0:T(8,128)(2,1)}, u32[]{:S(2)}, u32[]{:S(2)}) collective-permute-start(bf16[512,2048]{1,0:T(8,128)(2,1)} %slice.125), channel_id=1, source_target_pairs={{16,0},{20,4},{24,8},{28,12},{0,16},{4,20},{8,24},{12,28},{17,1},{... | collective-permute-start | bytes 6291464 | tf_op jit(solution)/shard_map/ppermute | solution.py:712
  211.3 7.5 collective-permute-start.4
  211.3 18.9 %collective-permute-start.5 = (bf16[1024,2048]{1,0:T(8,128)(2,1)}, bf16[1024,2048]{1,0:T(8,128)(2,1)}, u32[]{:S(2)}, u32[]{:S(2)}) collective-permute-start(bf16[1024,2048]{1,0:T(8,128)(2,1)} %bitcast.294), channel_id=1, source_target_pairs={{0,4},{4,0},{8,12},{12,8},{16,20},{20,16},{24,28},{28,24},{1,5},{5... | collective-permute-start | bytes 12582920 | tf_op jit(solution)/shard_map/ppermute | solution.py:718
  213.8 17.0 %collective-permute-start.6 = (bf16[1024,2048]{1,0:T(8,128)(2,1)}, bf16[1024,2048]{1,0:T(8,128)(2,1)}, u32[]{:S(2)}, u32[]{:S(2)}) collective-permute-start(bf16[1024,2048]{1,0:T(8,128)(2,1)} %collective-permute-done.others_refs_1_), channel_id=1, source_target_pairs={{0,4},{4,0},{8,12},{12,8},{16,20},{20,16},{24,28},{28,24},{1,5},{5... | collective-permute-start | bytes 12582920 | tf_op jit(solution)/shard_map/ppermute | solution.py:718
  213.8 23.0 %collective-permute-start.7 = (bf16[1024,2048]{1,0:T(8,128)(2,1)}, bf16[1024,2048]{1,0:T(8,128)(2,1)}, u32[]{:S(2)}, u32[]{:S(2)}) collective-permute-start(bf16[1024,2048]{1,0:T(8,128)(2,1)} %collective-permute-done.1.others_refs_2_), channel_id=1, source_target_pairs={{0,4},{4,0},{8,12},{12,8},{16,20},{20,16},{24,28},{28,24},{1,5},{5... | collective-permute-start | bytes 12582920 | tf_op jit(solution)/shard_map/ppermute | solution.py:718
  214.3 28.5 %collective-permute-start.8 = (bf16[1024,2048]{1,0:T(8,128)(2,1)}, bf16[1024,2048]{1,0:T(8,128)(2,1)}, u32[]{:S(2)}, u32[]{:S(2)}) collective-permute-start(bf16[1024,2048]{1,0:T(8,128)(2,1)} %pad_maximum_fusion.others_refs_3_), channel_id=1, source_target_pairs={{0,4},{4,0},{8,12},{12,8},{16,20},{20,16},{24,28},{28,24},{1,5},{5... | collective-permute-start | bytes 12582920 | tf_op jit(solution)/shard_map/ppermute | solution.py:718
  815.1 32.7 %all-to-all-start.1 = ((bf16[4,256,512]{2,1,0:T(8,128)(2,1)}), bf16[4,256,512]{2,1,0:T(8,128)(2,1)S(1)}, u32[]{:S(2)}, u32[]{:S(2)}) async-start(bf16[4,256,512]{2,1,0:T(8,128)(2,1)} %pad_maximum_fusion.4), calls=%async_computation.1 | async-start | bytes 2097152 | tf_op jit(solution)/shard_map/all_to_all | solution.py:929
  824.2 105.0 %all-gather.7.cloned.1.call-start = ((), (), s32[]{:S(2)}) async-start(), calls=%async_computation.5 | async-start | bytes 5242880 | tf_op jit(solution)/shard_map/all_gather | solution.py:931
  849.2 192.8 %reduce-scatter.2.cloned.1.call-start = ((), (), s32[]{:S(2)}) async-start(), calls=%async_computation.6 | async-start | bytes 5242880 | tf_op jit(solution)/shard_map/reduce_scatter | solution.py:978
  868.7 70.6 %collective-permute-start.15 = (bf16[2,2,256,512]{3,2,1,0:T(8,128)(2,1)}, bf16[2,2,256,512]{3,2,1,0:T(8,128)(2,1)}, u32[]{:S(2)}, u32[]{:S(2)}) collective-permute-start(bf16[2,2,256,512]{3,2,1,0:T(8,128)(2,1)} %dynamic-slice_bitcast_fusion), channel_id=1, source_target_pairs={{0,4},{4,0},{8,12},{12,8},{16,20},{20,16},{24,28},{28,24},{1,5},{5... | collective-permute-start | bytes 3145736 | tf_op jit(solution)/shard_map/ppermute | solution.py:718
  917.3 25.5 %collective-permute-start.12 = (bf16[2,2,256,512]{3,2,1,0:T(8,128)(2,1)}, bf16[2,2,256,512]{3,2,1,0:T(8,128)(2,1)}, u32[]{:S(2)}, u32[]{:S(2)}) collective-permute-start(bf16[2,2,256,512]{3,2,1,0:T(8,128)(2,1)} %dynamic-slice_bitcast_fusion.1), channel_id=1, source_target_pairs={{0,4},{4,0},{8,12},{12,8},{16,20},{20,16},{24,28},{28,24},{1,5},{5... | collective-permute-start | bytes 3145736 | tf_op jit(solution)/shard_map/ppermute | solution.py:718
  936.5 8.3 collective-permute-start.9
  941.0 14.9 %collective-permute-start.16 = (bf16[2,256,512]{2,1,0:T(8,128)(2,1)S(1)}, bf16[2,256,512]{2,1,0:T(8,128)(2,1)S(1)}, u32[]{:S(2)}, u32[]{:S(2)}) collective-permute-start(bf16[2,256,512]{2,1,0:T(8,128)(2,1)S(1)} %dynamic-slice_bitcast_fusion.3), channel_id=1, source_target_pairs={{0,16},{4,20},{8,24},{12,28},{16,0},{20,4},{24,8},{28,12},{1,17},{... | collective-permute-start | bytes 1572872 | tf_op jit(solution)/shard_map/ppermute | solution.py:722
  944.3 22.2 %collective-permute-start.13 = (bf16[2,256,512]{2,1,0:T(8,128)(2,1)S(1)}, bf16[2,256,512]{2,1,0:T(8,128)(2,1)S(1)}, u32[]{:S(2)}, u32[]{:S(2)}) collective-permute-start(bf16[2,256,512]{2,1,0:T(8,128)(2,1)S(1)} %dynamic-slice_bitcast_fusion.4), channel_id=1, source_target_pairs={{0,16},{4,20},{8,24},{12,28},{16,0},{20,4},{24,8},{28,12},{1,17},{... | collective-permute-start | bytes 1572872 | tf_op jit(solution)/shard_map/ppermute | solution.py:722
  946.4 22.5 %collective-permute-start.10 = (bf16[2,256,512]{2,1,0:T(8,128)(2,1)S(1)}, bf16[2,256,512]{2,1,0:T(8,128)(2,1)S(1)}, u32[]{:S(2)}, u32[]{:S(2)}) collective-permute-start(bf16[2,256,512]{2,1,0:T(8,128)(2,1)S(1)} %dynamic-slice_bitcast_fusion.5), channel_id=1, source_target_pairs={{0,8},{4,12},{8,0},{12,4},{16,24},{20,28},{24,16},{28,20},{1,9},{5... | collective-permute-start | bytes 1572872 | tf_op jit(solution)/shard_map/ppermute | solution.py:715
  956.8 19.9 %collective-permute-start.17 = (bf16[256,512]{1,0:T(8,128)(2,1)}, bf16[256,512]{1,0:T(8,128)(2,1)}, u32[]{:S(2)}, u32[]{:S(2)}) collective-permute-start(bf16[256,512]{1,0:T(8,128)(2,1)} %dynamic-slice_bitcast_fusion.7), channel_id=1, source_target_pairs={{0,8},{4,12},{8,0},{12,4},{16,24},{20,28},{24,16},{28,20},{1,9},{5... | collective-permute-start | bytes 786440 | tf_op jit(solution)/shard_map/ppermute | solution.py:715
  967.4 11.9 %collective-permute-start.14 = (bf16[256,512]{1,0:T(8,128)(2,1)}, bf16[256,512]{1,0:T(8,128)(2,1)}, u32[]{:S(2)}, u32[]{:S(2)}) collective-permute-start(bf16[256,512]{1,0:T(8,128)(2,1)} %dynamic-slice_bitcast_fusion.8), channel_id=1, source_target_pairs={{0,8},{4,12},{8,0},{12,4},{16,24},{20,28},{24,16},{28,20},{1,9},{5... | collective-permute-start | bytes 786440 | tf_op jit(solution)/shard_map/ppermute | solution.py:715
  969.1 16.6 %collective-permute-start.11 = (bf16[256,512]{1,0:T(8,128)(2,1)S(1)}, bf16[256,512]{1,0:T(8,128)(2,1)}, u32[]{:S(2)}, u32[]{:S(2)}) collective-permute-start(bf16[256,512]{1,0:T(8,128)(2,1)S(1)} %dynamic-slice_bitcast_fusion.9), channel_id=1, source_target_pairs={{0,16},{4,20},{8,24},{12,28},{16,0},{20,4},{24,8},{28,12},{1,17},{... | collective-permute-start | bytes 786440 | tf_op jit(solution)/shard_map/ppermute | solution.py:722
  971.2 7.3 collective-permute-start.21
  976.1 7.1 collective-permute-start.18
  983.5 17.7 %collective-permute-start.19 = (bf16[2,256,512]{2,1,0:T(8,128)(2,1)S(1)}, bf16[2,256,512]{2,1,0:T(8,128)(2,1)S(1)}, u32[]{:S(2)}, u32[]{:S(2)}) collective-permute-start(bf16[2,256,512]{2,1,0:T(8,128)(2,1)S(1)} %dynamic-slice_bitcast_fusion.2), channel_id=1, source_target_pairs={{0,8},{4,12},{8,0},{12,4},{16,24},{20,28},{24,16},{28,20},{1,9},{5... | collective-permute-start | bytes 1572872 | tf_op jit(solution)/shard_map/ppermute | solution.py:715
  984.1 13.4 %collective-permute-start.23 = (f32[256,33]{0,1:T(8,128)S(1)}, f32[256,33]{0,1:T(8,128)S(1)}, u32[]{:S(2)}, u32[]{:S(2)}) collective-permute-start(f32[256,33]{0,1:T(8,128)S(1)} %dynamic-slice_bitcast_fusion.10), channel_id=1, source_target_pairs={{0,8},{4,12},{8,0},{12,4},{16,24},{20,28},{24,16},{28,20},{1,9},{5... | collective-permute-start | bytes 101384 | tf_op jit(solution)/shard_map/ppermute | solution.py:715
  998.2 39.7 %collective-permute-start.26 = (f32[256,33]{0,1:T(8,128)}, f32[256,33]{0,1:T(8,128)}, u32[]{:S(2)}, u32[]{:S(2)}) collective-permute-start(f32[256,33]{0,1:T(8,128)} %bitcast_add_fusion.2), channel_id=1, source_target_pairs={{0,3},{1,0},{2,1},{3,2},{4,7},{5,4},{6,5},{7,6},{8,11},{9,8},{10,9... | collective-permute-start | bytes 101384 | tf_op jit(solution)/shard_map/ppermute | solution.py:694
  999.4 38.5 %collective-permute-start.25 = (f32[256,33]{0,1:T(8,128)}, f32[256,33]{0,1:T(8,128)}, u32[]{:S(2)}, u32[]{:S(2)}) collective-permute-start(f32[256,33]{0,1:T(8,128)} %bitcast_add_fusion.2), channel_id=1, source_target_pairs={{0,2},{1,3},{2,0},{3,1},{4,6},{5,7},{6,4},{7,5},{8,10},{9,11},{10,... | collective-permute-start | bytes 101384 | tf_op jit(solution)/shard_map/ppermute | solution.py:694
  999.4 38.5 %collective-permute-start.24 = (f32[256,33]{0,1:T(8,128)}, f32[256,33]{0,1:T(8,128)}, u32[]{:S(2)}, u32[]{:S(2)}) collective-permute-start(f32[256,33]{0,1:T(8,128)} %bitcast_add_fusion.2), channel_id=1, source_target_pairs={{0,1},{1,2},{2,3},{3,0},{4,5},{5,6},{6,7},{7,4},{8,9},{9,10},{10,1... | collective-permute-start | bytes 101384 | tf_op jit(solution)/shard_map/ppermute | solution.py:694
  1002.2 38.0 %collective-permute-start.20 = (bf16[256,512]{1,0:T(8,128)(2,1)S(1)}, bf16[256,512]{1,0:T(8,128)(2,1)}, u32[]{:S(2)}, u32[]{:S(2)}) collective-permute-start(bf16[256,512]{1,0:T(8,128)(2,1)S(1)} %dynamic-slice_bitcast_fusion.6), channel_id=1, source_target_pairs={{0,16},{4,20},{8,24},{12,28},{16,0},{20,4},{24,8},{28,12},{1,17},{... | collective-permute-start | bytes 786440 | tf_op jit(solution)/shard_map/ppermute | solution.py:722
  1046.4 10.8 %all-to-all-start.2 = ((f32[32,1,288]{2,1,0:T(1,128)}), f32[32,1,288]{2,1,0:T(1,128)S(1)}, u32[]{:S(2)}, u32[]{:S(2)}) async-start(f32[32,1,288]{2,1,0:T(1,128)} %all_to_all.14), calls=%async_computation.3 | async-start | bytes 98304 | tf_op jit(solution)/shard_map/all_to_all | solution.py:995
  (93 other events, 2702.9 us)
Sparse Core Ops, SparseCore 0:
  12.7 83.4 all-gather.4
  108.2 99.9 all-gather.8
  849.4 79.7 all-gather.6
  931.3 77.7 reduce-scatter.1

commit v5 on v4

--- a/solution.py
+++ b/solution.py
@@ -162,8 +162,11 @@
     def core_copy(c, q):
         return plane_copy(c, q, half + q, None, 3 * outer - 2 + q, core_id)
 
+    def column(c):
+        return (z + c + 1) % chunks
+
     def ring_copy(k):
-        where = (z - k + chunks) % chunks
+        where = (z - k - 1 + chunks) % chunks
         return remote(own_ref, mine_ref.at[k], ring_send.at[k], ring_recv.at[k], where, "tensor")
 
     others = range(1, outer)
@@ -229,8 +232,8 @@
         return sum_copy(c, both_at(c, 2 * k, rows_at), target, ident, outer_id(k))
 
     def last_copy(c):
-        where = (z + c) % chunks
-        return remote(ring_out.at[c], ring_in.at[c], last_send.at[c], last_recv.at[c], where, "tensor")
+        source, target = ring_out.at[c], ring_in.at[c]
+        return remote(source, target, last_send.at[c], last_recv.at[c], column(c), "tensor")
 
     def local(src, dst, sem):
         return pltpu.make_async_copy(src, dst, sem)
@@ -288,7 +291,6 @@
                 at = pl.ds(pl.multiple_of(i * 16, 16), 16)
                 in_s[0, at, :] = low(wide(in_s[0, at, :]) + wide(in_s[1, at, :]))
 
-        together(local(in_s.at[0], ring_out.at[c], fold_sem.at[0]))
 
     def drain_sum(c):
         for q in range(half):
@@ -309,7 +311,7 @@
         def _():
             core_copy(c, q).wait_recv()
 
-        rows_at = pl.ds(pl.multiple_of(((z + c) % chunks) * rows, rows), rows)
+        rows_at = pl.ds(pl.multiple_of(column(c) * rows, rows), rows)
         @pl.when(r == 0)
         def _():
             local(mine_ref.at[c], in_s.at[slot, :, x_part], x_sem.at[slot]).start()
@@ -346,39 +348,45 @@
                 barrier, inc=1, device_id={axis: where}, device_id_type=pl.DeviceIdType.MESH
             )
         pl.semaphore_wait(barrier, len(peers))
-        for k in range(1, chunks):
+        ring_copy(0).start()
+        together(local(own_ref, in_s.at[0, :, x_part], fold_sem.at[0]))
+        together(local(in_s.at[0, :, x_part], mine_ref.at[chunks - 1], fold_sem.at[0]))
+        ring_copy(0).wait_recv()
+        for k in range(1, chunks - 1):
             ring_copy(k).start()
-        together(local(own_ref, in_s.at[0, :, x_part], fold_sem.at[0]))
-        together(local(in_s.at[0, :, x_part], mine_ref.at[0], fold_sem.at[0]))
         first_hop(0)
         fetch(0, 0)
         second_hop(0)
-        ring_copy(1).wait_recv()
+
+    @pl.when((s == 0) & (j > 0))
+    def _():
+        load(0, 0).start()
+
+    @pl.when((j == 0) & (s == 4))
+    def _():
+        third_hop(0)
+        if chunks > 2:
+            ring_copy(1).wait_recv()
         first_hop(1)
 
-    @pl.when((s == 0) & (j > 0))
-    def _():
-        load(0, 0).start()
-
-    @pl.when((j == 0) & (s == 4))
-    def _():
-        third_hop(0)
-
-    @pl.when((s == blocks + 1) & (j + 1 < chunks))
+    @pl.when((s == blocks + experts) & (j + 1 < chunks))
+    def _():
+        third_hop(j + 1)
+
+    @pl.when((s == blocks + 2) & (j >= 1))
+    def _():
+        fold_halves(j - 1)
+
+    @pl.when((s == blocks + 2) & (j + 1 < chunks))
     def _():
         second_hop(j + 1)
 
-    @pl.when((s == blocks + experts) & (j + 1 < chunks))
-    def _():
-        third_hop(j + 1)
-
-    @pl.when((s == blocks + 2) & (j >= 1))
-    def _():
-        fold_halves(j - 1)
+    @pl.when((s == blocks + 2) & (j + 3 < chunks))
+    def _():
+        ring_copy(j + 2).wait_recv()
 
     @pl.when((s == blocks + 2) & (j + 2 < chunks))
     def _():
-        ring_copy(j + 2).wait_recv()
         first_hop(j + 2)
 
     @pl.when(s == blocks + 3)
@@ -388,11 +396,8 @@
     @pl.when((s == blocks + experts + half - 1) & (j >= 1))
     def _():
         fold_home(j - 1)
-
-        @pl.when(j >= 2)
-        def _():
-            last_copy(j - 1).start()
-
+        together(local(in_s.at[0], ring_out.at[j - 1], fold_sem.at[0]))
+        last_copy(j - 1).start()
         drain_sum(j - 1)
 
     @pl.when(s < blocks)
@@ -569,10 +574,8 @@
     def _():
         fold_halves(chunks - 1)
         fold_home(chunks - 1)
-        last_copy(chunks - 1).start()
         drain_sum(chunks - 1)
-        together(local(ring_out.at[0], in_s.at[0], fold_sem.at[0]))
-        for k in range(1, chunks):
+        for k in range(chunks - 1):
             last_copy(k).wait_recv()
             together(local(ring_in.at[k], in_s.at[1], fold_sem.at[1]))
 
@@ -582,7 +585,7 @@
                 in_s[0, at, :] = low(wide(in_s[0, at, :]) + wide(in_s[1, at, :]))
 
         together(local(in_s.at[0], final_ref, fold_sem.at[0]))
-        for k in range(1, chunks):
+        for k in range(chunks - 1):
             last_copy(k).wait_send()
             ring_copy(k).wait_send()
 
@@ -621,8 +624,8 @@
         ((2, outer - 1, cut, span), bf16),
         ((2, rows, span), bf16),
         ((2, outer - 1, rows, span), bf16),
-        ((chunks, rows, span), bf16),
-        ((chunks, rows, span), bf16),
+        ((chunks - 1, rows, span), bf16),
+        ((chunks - 1, rows, span), bf16),
     ]
     dma = pltpu.SemaphoreType.DMA
     gathers, sums = 5 * outer - 2, 6 * outer - 2
@@ -753,11 +756,14 @@
             for k, far in enumerate(fars)
         ]
 
-    def third(self, own, near, fars, diagonals):
+    def third(self, own, near, fars, diagonals, swapped):
         mine = [own, near]
         for far, diagonal in zip(fars, diagonals):
             mine += [far, diagonal]
-        return mine + [self.swap_core(part) for part in mine]
+        other = swapped[:2]
+        for far, diagonal in zip(swapped[2:], diagonals):
+            other += [far, self.swap_core(diagonal)]
+        return mine + other
 
 
 def per_device(
@@ -836,8 +842,9 @@
         jnp.concatenate(mixed_parts, axis=0).reshape(full_length, local_width).astype(jnp.bfloat16)
     )
     diagonals = plane.second(near, fars)
-    attended, diagonals = tie(attended, diagonals)
-    cot_all = plane.third(cotangent[0], near, fars, diagonals)
+    swapped = [plane.swap_core(part) for part in (cotangent[0], near, *fars)]
+    attended, diagonals, swapped = tie(attended, diagonals, swapped)
+    cot_all = plane.third(cotangent[0], near, fars, diagonals, swapped)
     heads_own = lax.all_to_all(
         attended.reshape(tensor_count, block_rows, local_width), "tensor", 0, 0
     )
@@ -966,7 +973,6 @@
     grad_k_low = grad_key_raw.astype(jnp.bfloat16)
     grad_v_low = grad_values.reshape(full_length, local_width).astype(jnp.bfloat16)
     query_part = jnp.einsum("ld,lh->dh", gathered, grad_q_low, preferred_element_type=jnp.float32)
-    key_part = jnp.einsum("ld,lh->dh", gathered, grad_k_low, preferred_element_type=jnp.float32)
     value_part = jnp.einsum("ld,lh->dh", gathered, grad_v_low, preferred_element_type=jnp.float32)
     from_query = jnp.einsum("lh,dh->ld", grad_q_low, w_query, preferred_element_type=jnp.float32)
     from_key = jnp.einsum("lh,dh->ld", grad_k_low, w_key, preferred_element_type=jnp.float32)
@@ -980,6 +986,8 @@
     grad_gate = jnp.swapaxes(sums[:, 0], 1, 2)
     grad_up = jnp.swapaxes(sums[:, 1], 1, 2)
     grad_down = sums[:, 2]
+    grad_k_low, grad_gate, grad_up, grad_down = tie(grad_k_low, grad_gate, grad_up, grad_down)
+    key_part = jnp.einsum("ld,lh->dh", gathered, grad_k_low, preferred_element_type=jnp.float32)
     out_part = jnp.einsum("ld,lh->dh", grad_attn_all, attended, preferred_element_type=jnp.float32)
     attn_pull = jax.vjp(rms_scale, token_values, attn_gain)[1]
     grad_tok_norm, attn_part = attn_pull(grad_normed)

time: 1070 us -> 1060 us (level)
  waiting for transfers between devices: 158 us -> 145 us
    ppermute x10, waiting for transfers between devices: 12.6 us -> 0.53 us  [swap_core(): return lax.ppermute(values, 'dp', self.core)]
    unnamed x188 -> x196, local copies, waits for them, and re-layouts: 30.7 us -> 28 us
where the time goes in v5:
time: 1060 us; the launch traced here: 1050 us
  Pallas kernels  557 us (53%)
  waiting for transfers between devices  145 us (14%)
  matrix products  106 us (10%)
  local copies, waits for them, and re-layouts  75.9 us (7%)
  other arithmetic  71.2 us (7%)
  blocking collectives  48.6 us (5%)
  starting transfers between devices  30.2 us (3%)
  between operations  16.9 us (2%)
    pallas_call x1, Pallas kernels, moe(): pl.pallas_call(functools.partial(moe_kernel, sizes), grid=(chunks, 2 * bl...  557 us
    ppermute x2, waiting for transfers between devices, pull(): return lax.ppermute(values, 'dp', pairs)  86.9 us
    all_to_all x1, blocking collectives, per_device(): lax.all_to_all(attended.reshape(tensor_count, block_rows, local_width), '...  48.6 us
    unnamed x196, local copies, waits for them, and re-layouts  28 us
    all_to_all x1, waiting for transfers between devices, per_device(): grad_mixed = lax.all_to_all(grad_heads, 'tensor', 0, 0)  23 us
  transfers between devices with their start and end apart: 33, of which 14 were waited for; matrix products, arithmetic and copies ran while one was open for 20% of the time, Pallas kernels for 0%

profile of v5, /device:TPU:0, one launch (start us, length us, event | category | flops | bytes accessed | tf_op | source)
XLA Modules:
  0.0 1050.1 jit_solution(6259175203030461950)
XLA Ops:
  12.6 3.1 collective-permute-start.1
  20.8 85.7 %collective-permute-done.1.others_refs_2_ = bf16[1024,2048]{1,0:T(8,128)(2,1)} collective-permute-done((bf16[1024,2048]{1,0:T(8,128)(2,1)}, bf16[1024,2048]{1,0:T(8,128)(2,1)}, u32[]{:S(2)}, u32[]{:S(2)}) %collective-permute-start.1) | collective-permute-done | bytes 4194336 | tf_op jit(solution)/shard_map/ppermute | solution.py:715
  108.0 3.2 slice.125
  111.2 3.2 slice.126
  116.9 5.3 multiply_reduce_fusion.9
  124.5 6.8 multiply_reduce_fusion.10
  133.3 3.7 multiply_multiply_fusion
  149.8 4.2 fusion
  159.8 3.0 collective-permute-done.3
  164.0 4.9 pad_maximum_fusion.others_refs_3_
  169.4 48.6 %all_to_all.19 = bf16[4,256,512]{2,1,0:T(8,128)(2,1)S(1)} all-to-all(bf16[4,256,512]{2,1,0:T(8,128)(2,1)S(1)} %bitcast.276), channel_id=1, replica_groups=mesh['dp'=8,'tensor'=4] {'tensor'}, dimensions={0} | all-to-all | bytes 2097152 | tf_op jit(solution)/shard_map/all_to_all | solution.py:848
  236.9 556.6 %moe.1 = (bf16[256,4224]{1,0:T(8,128)(2,1)}, f32[4,3,256,2048]{3,2,1,0:T(8,128)}, bf16[4,256,2176]{2,1,0:T(8,128)(2,1)}, bf16[4,7,256,2176]{3,2,1,0:T(8,128)(2,1...) custom-call(bf16[256,2176]{1,0:T(8,128)(2,1)} %concatenate.44.own_re, ...), custom_call_target="tpu_custom_call" | custom-call | flops 139586437120 | bytes 142606336 | tf_op jit(solution)/shard_map/moe/pallas_call | solution.py:660
  813.5 3.5 all-to-all-start.1
  818.6 23.0 %all-to-all-done.1 = bf16[4,256,512]{2,1,0:T(8,128)(2,1)S(1)} async-done(((bf16[4,256,512]{2,1,0:T(8,128)(2,1)}), bf16[4,256,512]{2,1,0:T(8,128)(2,1)S(1)}, u32[]{:S(2)}, u32[]{:S(2)}) %all-to-all-start.1) | async-done | bytes 1048608 | tf_op jit(solution)/shard_map/all_to_all | solution.py:936
  844.5 4.7 fusion.151
  849.2 5.6 fusion.4
  862.2 9.8 multiply_reduce_fusion.1
  872.0 8.8 multiply_convert_fusion.1
  887.2 3.4 multiply_add_fusion.1
  896.9 4.0 multiply_reduce_fusion.4
  903.7 5.0 convolution_convert_fusion.3
  915.8 6.0 add_convert_fusion
  929.7 9.4 collective-permute-done.16
  943.7 4.4 collective-permute-done.17
  949.8 4.6 convolution_convert_fusion
  956.1 17.8 %slice_bitcast_fusion = (f32[4,256,2048]{2,1,0:T(8,128)}, f32[4,2048,256]{1,2,0:T(8,128)}, f32[4,2048,256]{1,2,0:T(8,128)}) fusion(f32[4,3,256,2048]{3,2,1,0:T(8,128)} %get-tuple-element.53), kind=kLoop, calls=%fused_computation | loop fusion | bytes 50331648 | tf_op jit(solution)/shard_map/squeeze | solution.py:988
  974.0 4.7 convolution_convert_fusion.2
  983.5 8.7 copy.204
  992.1 8.7 copy.205
  1009.5 7.2 collective-permute-done.19
  1031.5 3.1 all-to-all-start.2
  1034.6 5.3 fusion.51
  (394 shorter events, 157.7 us)
Async XLA Ops:
  7.2 100.8 %all-gather.5.cloned.1.call-start = ((), (), s32[]{:S(2)}) async-start(), calls=%async_computation.4 | async-start | bytes 5242880 | tf_op jit(solution)/shard_map/all_gather | solution.py:807
  12.5 205.5 %all-gather.9.cloned.1.call-start = ((), (), s32[]{:S(2)}) async-start(), calls=%async_computation.7 | async-start | bytes 5242880 | tf_op jit(solution)/shard_map/all_gather | solution.py:814
  12.6 94.0 %collective-permute-start.1 = (bf16[1024,2048]{1,0:T(8,128)(2,1)}, bf16[1024,2048]{1,0:T(8,128)(2,1)}, u32[]{:S(2)}, u32[]{:S(2)}) collective-permute-start(bf16[1024,2048]{1,0:T(8,128)(2,1)} %bitcast.291), channel_id=1, source_target_pairs={{16,0},{20,4},{24,8},{28,12},{0,16},{4,20},{8,24},{12,28},{17,1},{... | collective-permute-start | bytes 12582920 | tf_op jit(solution)/shard_map/ppermute | solution.py:715
  15.7 92.3 %collective-permute-start = (bf16[1024,2048]{1,0:T(8,128)(2,1)}, bf16[1024,2048]{1,0:T(8,128)(2,1)}, u32[]{:S(2)}, u32[]{:S(2)}) collective-permute-start(bf16[1024,2048]{1,0:T(8,128)(2,1)} %bitcast.292), channel_id=1, source_target_pairs={{0,8},{4,12},{8,0},{12,4},{16,24},{20,28},{24,16},{28,20},{1,9},{5... | collective-permute-start | bytes 12582920 | tf_op jit(solution)/shard_map/ppermute | solution.py:718
  17.1 151.7 %collective-permute-start.4 = (bf16[1024,2048]{1,0:T(8,128)(2,1)}, bf16[1024,2048]{1,0:T(8,128)(2,1)}, u32[]{:S(2)}, u32[]{:S(2)}) collective-permute-start(bf16[1024,2048]{1,0:T(8,128)(2,1)} %bitcast.293), channel_id=1, source_target_pairs={{0,4},{4,0},{8,12},{12,8},{16,20},{20,16},{24,28},{28,24},{1,5},{5... | collective-permute-start | bytes 12582920 | tf_op jit(solution)/shard_map/ppermute | solution.py:721
  111.2 57.7 %collective-permute-start.5 = (bf16[1024,2048]{1,0:T(8,128)(2,1)}, bf16[1024,2048]{1,0:T(8,128)(2,1)}, u32[]{:S(2)}, u32[]{:S(2)}) collective-permute-start(bf16[1024,2048]{1,0:T(8,128)(2,1)} %collective-permute-done.others_refs_1_), channel_id=1, source_target_pairs={{0,4},{4,0},{8,12},{12,8},{16,20},{20,16},{24,28},{28,24},{1,5},{5... | collective-permute-start | bytes 12582920 | tf_op jit(solution)/shard_map/ppermute | solution.py:721
  114.3 54.5 %collective-permute-start.6 = (bf16[1024,2048]{1,0:T(8,128)(2,1)}, bf16[1024,2048]{1,0:T(8,128)(2,1)}, u32[]{:S(2)}, u32[]{:S(2)}) collective-permute-start(bf16[1024,2048]{1,0:T(8,128)(2,1)} %collective-permute-done.1.others_refs_2_), channel_id=1, source_target_pairs={{0,4},{4,0},{8,12},{12,8},{16,20},{20,16},{24,28},{28,24},{1,5},{5... | collective-permute-start | bytes 12582920 | tf_op jit(solution)/shard_map/ppermute | solution.py:721
  114.8 47.9 %collective-permute-start.3 = (bf16[512,2048]{1,0:T(8,128)(2,1)}, bf16[512,2048]{1,0:T(8,128)(2,1)}, u32[]{:S(2)}, u32[]{:S(2)}) collective-permute-start(bf16[512,2048]{1,0:T(8,128)(2,1)} %slice.126), channel_id=1, source_target_pairs={{0,8},{4,12},{8,0},{12,4},{16,24},{20,28},{24,16},{28,20},{1,9},{5... | collective-permute-start | bytes 6291464 | tf_op jit(solution)/shard_map/ppermute | solution.py:718
  116.4 47.6 %collective-permute-start.2 = (bf16[512,2048]{1,0:T(8,128)(2,1)}, bf16[512,2048]{1,0:T(8,128)(2,1)}, u32[]{:S(2)}, u32[]{:S(2)}) collective-permute-start(bf16[512,2048]{1,0:T(8,128)(2,1)} %slice.125), channel_id=1, source_target_pairs={{16,0},{20,4},{24,8},{28,12},{0,16},{4,20},{8,24},{12,28},{17,1},{... | collective-permute-start | bytes 6291464 | tf_op jit(solution)/shard_map/ppermute | solution.py:715
  218.0 7.5 collective-permute-start.7
  220.0 16.9 %collective-permute-start.8 = (bf16[1024,2048]{1,0:T(8,128)(2,1)}, bf16[1024,2048]{1,0:T(8,128)(2,1)}, u32[]{:S(2)}, u32[]{:S(2)}) collective-permute-start(bf16[1024,2048]{1,0:T(8,128)(2,1)} %pad_maximum_fusion.others_refs_3_), channel_id=1, source_target_pairs={{0,4},{4,0},{8,12},{12,8},{16,20},{20,16},{24,28},{28,24},{1,5},{5... | collective-permute-start | bytes 12582920 | tf_op jit(solution)/shard_map/ppermute | solution.py:721
  813.5 28.1 %all-to-all-start.1 = ((bf16[4,256,512]{2,1,0:T(8,128)(2,1)}), bf16[4,256,512]{2,1,0:T(8,128)(2,1)S(1)}, u32[]{:S(2)}, u32[]{:S(2)}) async-start(bf16[4,256,512]{2,1,0:T(8,128)(2,1)} %pad_maximum_fusion.4), calls=%async_computation.1 | async-start | bytes 2097152 | tf_op jit(solution)/shard_map/all_to_all | solution.py:936
  817.0 105.0 %all-gather.7.cloned.1.call-start = ((), (), s32[]{:S(2)}) async-start(), calls=%async_computation.5 | async-start | bytes 5242880 | tf_op jit(solution)/shard_map/all_gather | solution.py:938
  842.9 185.5 %reduce-scatter.2.cloned.1.call-start = ((), (), s32[]{:S(2)}) async-start(), calls=%async_computation.6 | async-start | bytes 5242880 | tf_op jit(solution)/shard_map/reduce_scatter | solution.py:984
  862.2 59.8 %collective-permute-start.15 = (bf16[2,2,256,512]{3,2,1,0:T(8,128)(2,1)}, bf16[2,2,256,512]{3,2,1,0:T(8,128)(2,1)}, u32[]{:S(2)}, u32[]{:S(2)}) collective-permute-start(bf16[2,2,256,512]{3,2,1,0:T(8,128)(2,1)} %dynamic-slice_bitcast_fusion), channel_id=1, source_target_pairs={{0,4},{4,0},{8,12},{12,8},{16,20},{20,16},{24,28},{28,24},{1,5},{5... | collective-permute-start | bytes 3145736 | tf_op jit(solution)/shard_map/ppermute | solution.py:721
  909.9 16.4 %collective-permute-start.9 = (bf16[2,2,256,512]{3,2,0,1:T(8,128)(2,1)}, bf16[2,2,256,512]{3,2,0,1:T(8,128)(2,1)}, u32[]{:S(2)}, u32[]{:S(2)}) collective-permute-start(bf16[2,2,256,512]{3,2,0,1:T(8,128)(2,1)} %bitcast.251), channel_id=1, source_target_pairs={{0,4},{4,0},{8,12},{12,8},{16,20},{20,16},{24,28},{28,24},{1,5},{5... | collective-permute-start | bytes 3145736 | tf_op jit(solution)/shard_map/ppermute | solution.py:721
  924.8 14.3 %collective-permute-start.16 = (bf16[2,256,512]{2,1,0:T(8,128)(2,1)}, bf16[2,256,512]{2,1,0:T(8,128)(2,1)S(1)}, u32[]{:S(2)}, u32[]{:S(2)}) collective-permute-start(bf16[2,256,512]{2,1,0:T(8,128)(2,1)} %dynamic-slice_bitcast_fusion.3), channel_id=1, source_target_pairs={{0,16},{4,20},{8,24},{12,28},{16,0},{20,4},{24,8},{28,12},{1,17},{... | collective-permute-start | bytes 1572872 | tf_op jit(solution)/shard_map/ppermute | solution.py:725
  927.9 14.0 %collective-permute-start.10 = (bf16[2,256,512]{2,1,0:T(8,128)(2,1)S(1)}, bf16[2,256,512]{2,1,0:T(8,128)(2,1)S(1)}, u32[]{:S(2)}, u32[]{:S(2)}) collective-permute-start(bf16[2,256,512]{2,1,0:T(8,128)(2,1)S(1)} %dynamic-slice_bitcast_fusion.5), channel_id=1, source_target_pairs={{0,8},{4,12},{8,0},{12,4},{16,24},{20,28},{24,16},{28,20},{1,9},{5... | collective-permute-start | bytes 1572872 | tf_op jit(solution)/shard_map/ppermute | solution.py:718
  940.3 7.7 collective-permute-start.17
  942.8 38.8 %collective-permute-start.11 = (bf16[256,512]{1,0:T(8,128)(2,1)}, bf16[256,512]{1,0:T(8,128)(2,1)}, u32[]{:S(2)}, u32[]{:S(2)}) collective-permute-start(bf16[256,512]{1,0:T(8,128)(2,1)} %dynamic-slice_bitcast_fusion.9), channel_id=1, source_target_pairs={{0,16},{4,20},{8,24},{12,28},{16,0},{20,4},{24,8},{28,12},{1,17},{... | collective-permute-start | bytes 786440 | tf_op jit(solution)/shard_map/ppermute | solution.py:725
  949.5 30.3 %collective-permute-start.21 = (f32[2,2,256,33]{2,1,0,3:T(2,128)S(1)}, f32[2,2,256,33]{2,1,0,3:T(2,128)S(1)}, u32[]{:S(2)}, u32[]{:S(2)}) collective-permute-start(f32[2,2,256,33]{2,1,0,3:T(2,128)S(1)} %bitcast.295), channel_id=1, source_target_pairs={{0,4},{4,0},{8,12},{12,8},{16,20},{20,16},{24,28},{28,24},{1,5},{5... | collective-permute-start | bytes 405512 | tf_op jit(solution)/shard_map/ppermute | solution.py:721
  955.6 45.7 %collective-permute-start.18 = (bf16[2,2,256,512]{3,2,0,1:T(8,128)(2,1)}, bf16[2,2,256,512]{3,2,0,1:T(8,128)(2,1)}, u32[]{:S(2)}, u32[]{:S(2)}) collective-permute-start(bf16[2,2,256,512]{3,2,0,1:T(8,128)(2,1)} %bitcast.250), channel_id=1, source_target_pairs={{0,4},{4,0},{8,12},{12,8},{16,20},{20,16},{24,28},{28,24},{1,5},{5... | collective-permute-start | bytes 3145736 | tf_op jit(solution)/shard_map/ppermute | solution.py:721
  979.7 24.9 %collective-permute-start.12 = (bf16[2,2,256,512]{3,2,1,0:T(8,128)(2,1)}, bf16[2,2,256,512]{3,2,1,0:T(8,128)(2,1)}, u32[]{:S(2)}, u32[]{:S(2)}) collective-permute-start(bf16[2,2,256,512]{3,2,1,0:T(8,128)(2,1)} %dynamic-slice_bitcast_fusion.1), channel_id=1, source_target_pairs={{0,4},{4,0},{8,12},{12,8},{16,20},{20,16},{24,28},{28,24},{1,5},{5... | collective-permute-start | bytes 3145736 | tf_op jit(solution)/shard_map/ppermute | solution.py:721
  979.9 20.9 %collective-permute-start.22 = (f32[2,256,33]{1,2,0:T(8,128)S(1)}, f32[2,256,33]{1,2,0:T(8,128)S(1)}, u32[]{:S(2)}, u32[]{:S(2)}) collective-permute-start(f32[2,256,33]{1,2,0:T(8,128)S(1)} %bitcast.296), channel_id=1, source_target_pairs={{0,16},{4,20},{8,24},{12,28},{16,0},{20,4},{24,8},{28,12},{1,17},{... | collective-permute-start | bytes 202760 | tf_op jit(solution)/shard_map/ppermute | solution.py:725
  1002.9 13.8 %collective-permute-start.19 = (bf16[2,256,512]{2,1,0:T(8,128)(2,1)S(1)}, bf16[2,256,512]{2,1,0:T(8,128)(2,1)S(1)}, u32[]{:S(2)}, u32[]{:S(2)}) collective-permute-start(bf16[2,256,512]{2,1,0:T(8,128)(2,1)S(1)} %dynamic-slice_bitcast_fusion.2), channel_id=1, source_target_pairs={{0,8},{4,12},{8,0},{12,4},{16,24},{20,28},{24,16},{28,20},{1,9},{5... | collective-permute-start | bytes 1572872 | tf_op jit(solution)/shard_map/ppermute | solution.py:718
  1006.1 14.8 %collective-permute-start.13 = (bf16[2,256,512]{2,1,0:T(8,128)(2,1)S(1)}, bf16[2,256,512]{2,1,0:T(8,128)(2,1)S(1)}, u32[]{:S(2)}, u32[]{:S(2)}) collective-permute-start(bf16[2,256,512]{2,1,0:T(8,128)(2,1)S(1)} %dynamic-slice_bitcast_fusion.4), channel_id=1, source_target_pairs={{0,16},{4,20},{8,24},{12,28},{16,0},{20,4},{24,8},{28,12},{1,17},{... | collective-permute-start | bytes 1572872 | tf_op jit(solution)/shard_map/ppermute | solution.py:725
  1006.7 14.5 %collective-permute-start.26 = (f32[256,33]{0,1:T(8,128)S(1)}, f32[256,33]{0,1:T(8,128)S(1)}, u32[]{:S(2)}, u32[]{:S(2)}) collective-permute-start(f32[256,33]{0,1:T(8,128)S(1)} %bitcast_add_fusion.2), channel_id=1, source_target_pairs={{0,3},{1,0},{2,1},{3,2},{4,7},{5,4},{6,5},{7,6},{8,11},{9,8},{10,9... | collective-permute-start | bytes 101384 | tf_op jit(solution)/shard_map/ppermute | solution.py:697
  1008.9 12.3 %collective-permute-start.25 = (f32[256,33]{0,1:T(8,128)S(1)}, f32[256,33]{0,1:T(8,128)S(1)}, u32[]{:S(2)}, u32[]{:S(2)}) collective-permute-start(f32[256,33]{0,1:T(8,128)S(1)} %bitcast_add_fusion.2), channel_id=1, source_target_pairs={{0,2},{1,3},{2,0},{3,1},{4,6},{5,7},{6,4},{7,5},{8,10},{9,11},{10,... | collective-permute-start | bytes 101384 | tf_op jit(solution)/shard_map/ppermute | solution.py:697
  1008.9 12.3 %collective-permute-start.24 = (f32[256,33]{0,1:T(8,128)S(1)}, f32[256,33]{0,1:T(8,128)S(1)}, u32[]{:S(2)}, u32[]{:S(2)}) collective-permute-start(f32[256,33]{0,1:T(8,128)S(1)} %bitcast_add_fusion.2), channel_id=1, source_target_pairs={{0,1},{1,2},{2,3},{3,0},{4,5},{5,6},{6,7},{7,4},{8,9},{9,10},{10,1... | collective-permute-start | bytes 101384 | tf_op jit(solution)/shard_map/ppermute | solution.py:697
  1016.9 8.5 collective-permute-start.20
  1021.1 6.4 collective-permute-start.14
  1031.5 10.5 all-to-all-start.2
  (97 other events, 2726.8 us)
Sparse Core Ops, SparseCore 0:
  12.7 83.4 all-gather.4
  115.0 102.3 all-gather.8
  843.1 78.9 all-gather.6
  924.2 75.2 reduce-scatter.1

commit v6 on v5

--- a/solution.py
+++ b/solution.py
@@ -71,6 +71,7 @@
     wd_ref,
     final_ref,
     acc_ref,
+    late_ref,
     mine_ref,
     gather_ref,
     other_ref,
@@ -107,6 +108,7 @@
     ring_recv,
     last_send,
     last_recv,
+    late_sem,
 ):
     outer, chunks, experts, slots, rows, width, extra, all_experts = sizes
     blocks, half, cut = 4 * outer, 2 * outer, rows // 2
@@ -203,7 +205,39 @@
             core_copy(c, q).wait_send()
 
     def sum_copy(c, src, dst, ident, where):
-        return remote(src, dst, sum_send.at[c, ident], sum_recv.at[c, ident], where)
+        def each(act):
+            def columns(size):
+                part = pl.ds(0, size)
+                source, target = src.at[:, part], dst.at[:, part]
+                act(remote(source, target, sum_send.at[c, ident], sum_recv.at[c, ident], where))
+
+            if isinstance(c, int):
+                columns(full if c == chunks - 1 else span)
+                return
+
+            @pl.when(c < chunks - 1)
+            def _():
+                columns(span)
+
+            @pl.when(c == chunks - 1)
+            def _():
+                columns(full)
+
+        class Copy:
+            def start(self):
+                each(lambda copy: copy.start())
+
+            def wait_recv(self):
+                each(lambda copy: copy.wait_recv())
+
+            def wait_send(self):
+                each(lambda copy: copy.wait_send())
+
+        return Copy()
+
+    def late_copy(q, side, slot):
+        owner = ((a + q // 2) % outer) * 4 + ((me // 2 + q) % 2) * 2 + (me + side) % 2
+        return local(out_s.at[slot, :, y_part], late_ref.at[owner], late_sem.at[slot])
 
     def swap_copy(c, q):
         return sum_copy(c, other_ref.at[c % 2, q], core_in.at[c % 2, q], q, core_id)
@@ -491,6 +525,10 @@
     def written(c, o):
         q, slot = half - 1 - o % half, o % 2
 
+        @pl.when(c == chunks - 1)
+        def _():
+            late_copy(q, 1 - o // half, slot).wait()
+
         @pl.when(o < half)
         def _():
             local(out_s.at[slot], other_ref.at[c % 2, q], out_sem.at[slot]).wait()
@@ -537,6 +575,10 @@
         @pl.when(o >= half)
         def _():
             local(core_in.at[j % 2, q], in_s.at[slot], x_sem.at[slot]).wait()
+
+        @pl.when((o >= half) & (j == chunks - 1))
+        def _():
+            in_s[slot, :, full:] = jnp.zeros((rows, width), jnp.bfloat16)
 
         @pl.when(o < half)
         def _():
@@ -553,6 +595,10 @@
         y = dot_nn(picks, crow_s[:, pl.ds(at, slots), :].reshape(flat))
         out_s[slot, :, full:] = low(y + wide(in_s[slot, :, full:]))
 
+        @pl.when(j == chunks - 1)
+        def _():
+            late_copy(q, side, slot).start()
+
         @pl.when(o < half)
         def _():
             local(out_s.at[slot], other_ref.at[j % 2, q], out_sem.at[slot]).start()
@@ -575,6 +621,7 @@
         fold_halves(chunks - 1)
         fold_home(chunks - 1)
         drain_sum(chunks - 1)
+        in_s[0, :, full:] = jnp.zeros((rows, width), jnp.bfloat16)
         for k in range(chunks - 1):
             last_copy(k).wait_recv()
             together(local(ring_in.at[k], in_s.at[1], fold_sem.at[1]))
@@ -615,6 +662,7 @@
     shapes = [
         ((rows, span), bf16),
         ((experts, 3, hidden, width), jnp.float32),
+        ((blocks, rows, width), bf16),
         ((chunks, rows, full), bf16),
         ((chunks if chunks <= 4 else 3, blocks - 1, rows, full), bf16),
         ((2, half, rows, span), bf16),
@@ -655,6 +703,7 @@
         dma((chunks,)),
         dma((chunks,)),
         dma((chunks,)),
+        dma((2,)),
     ]
     flops = 2 * chunks * experts * total * width * (hidden * 9 + 4 * rows)
     results = pl.pallas_call(
@@ -675,7 +724,7 @@
         ),
         name="moe",
     )(own, *cot, picks, wg, wu, wd)
-    return results[:2]
+    return results[:3]
 
 
 def wide(values):
@@ -737,11 +786,17 @@
 
     def scatter(self, values, inner_first):
         kind = values.dtype
-        index = lax.axis_index("dp")
-        core, b, a = index % 2, index // 2 % 2, index // 4
+        return self.scatter_rest(self.fold_core(values), kind, inner_first)
+
+    def fold_core(self, values):
+        core = lax.axis_index("dp") % 2
         parts = values.reshape(self.outer, 2, 2, values.shape[0] // self.count, values.shape[1])
         given = self.swap_core(pick(parts, 1 - core, 2))
-        parts = (wide(pick(parts, core, 2)) + wide(given)).astype(kind)
+        return (wide(pick(parts, core, 2)) + wide(given)).astype(values.dtype)
+
+    def scatter_rest(self, parts, kind, inner_first):
+        index = lax.axis_index("dp")
+        b, a = index // 2 % 2, index // 4
         if inner_first:
             return self.fold_outer(self.fold_inner(parts, b, 1, kind).astype(kind), a, kind)
         return self.fold_inner(self.fold_outer(parts, a, kind).astype(kind), b, 0, kind)
@@ -897,7 +952,7 @@
         jnp.where(slot_column == 3 * all_experts, -(slot_row % slots).astype(jnp.float32), 0.0),
     ).astype(jnp.bfloat16)
     packed = jnp.concatenate([moe_own, meta], axis=1)
-    combined, sums = moe(
+    combined, sums, late = moe(
         packed,
         cot_all,
         picks,
@@ -912,7 +967,6 @@
     combined = wide(combined)
     grad_moe = combined[:, :width]
     grad_probs = combined[:, width : width + all_experts]
-    output = low(residual + combined[:, width + extra :])
     grad_own = lax.dynamic_slice_in_dim(cotangent[0], own_start, block_rows, 0).astype(jnp.float32)
     grad_logits = (
         own_probs * (grad_probs - jnp.sum(own_probs * grad_probs, axis=-1, keepdims=True))
@@ -977,25 +1031,36 @@
     from_query = jnp.einsum("lh,dh->ld", grad_q_low, w_query, preferred_element_type=jnp.float32)
     from_key = jnp.einsum("lh,dh->ld", grad_k_low, w_key, preferred_element_type=jnp.float32)
     from_value = jnp.einsum("lh,dh->ld", grad_v_low, w_value, preferred_element_type=jnp.float32)
-    grad_gathered, grad_attn_all, sums, router_part = tie(
-        low(from_query + from_key + from_value), grad_attn_all, sums, router_part
+    query_part = plane.fold_core(low(query_part))
+    value_part = plane.fold_core(low(value_part))
+    grad_gathered = low(from_query + from_key + from_value)
+    grad_gathered, grad_attn_all, sums, router_part, late, grad_k_late, query_part, value_part = tie(
+        grad_gathered, grad_attn_all, sums, router_part, late, grad_k_low, query_part, value_part
     )
+    cut = width // 2
+    late = plane.fold_core(late.reshape(-1, width))
+    late = [
+        plane.scatter_rest(late[..., :cut], late.dtype, True),
+        plane.scatter_rest(late[..., cut:], late.dtype, False),
+    ]
+    output = low(residual + combined[:, width + extra :] + jnp.concatenate(late, axis=1))
     grad_normed = wide(
         lax.psum_scatter(grad_gathered, "tensor", scatter_dimension=0, tiled=True)
     )
     grad_gate = jnp.swapaxes(sums[:, 0], 1, 2)
     grad_up = jnp.swapaxes(sums[:, 1], 1, 2)
     grad_down = sums[:, 2]
-    grad_k_low, grad_gate, grad_up, grad_down = tie(grad_k_low, grad_gate, grad_up, grad_down)
-    key_part = jnp.einsum("ld,lh->dh", gathered, grad_k_low, preferred_element_type=jnp.float32)
+    key_part = jnp.einsum("ld,lh->dh", gathered, grad_k_late, preferred_element_type=jnp.float32)
+    key_part = plane.fold_core(low(key_part))
+    key_part, grad_gate, grad_up, grad_down = tie(key_part, grad_gate, grad_up, grad_down)
     out_part = jnp.einsum("ld,lh->dh", grad_attn_all, attended, preferred_element_type=jnp.float32)
     attn_pull = jax.vjp(rms_scale, token_values, attn_gain)[1]
     grad_tok_norm, attn_part = attn_pull(grad_normed)
     grad_tokens = (grad_residual + grad_tok_norm).astype(jnp.bfloat16)
     grad_out = plane.scatter(low(out_part), True)
-    grad_value = plane.scatter(low(value_part), False)
-    grad_query = plane.scatter(low(query_part), True)
-    grad_key = plane.scatter(low(key_part), False)
+    grad_value = plane.scatter_rest(value_part, value_part.dtype, False)
+    grad_query = plane.scatter_rest(query_part, query_part.dtype, True)
+    grad_key = plane.scatter_rest(key_part, key_part.dtype, False)
     routing = plane.scatter(jnp.concatenate([router_part, ffn_part[:, None]], axis=1), False)
     routing = ring_sum(routing, tensor_count)
     parts = [v.reshape(data_count, -1) for v in (attn_part, q_part, k_part)]

time: 1060 us -> 1060 us (level)
  Pallas kernels: 557 us -> 524 us
  waiting for transfers between devices: 145 us -> 168 us
    pallas_call x1, Pallas kernels: 557 us -> 524 us  [moe(): pl.pallas_call(functools.partial(moe_kernel, sizes), grid=(chunks, 2 * bl...]
    ppermute x7 -> x9, waiting for transfers between devices: 17.2 us -> 37 us  [swap_inner(): return lax.ppermute(values, 'dp', self.inner)]
    unnamed x196 -> x206, local copies, waits for them, and re-layouts: 28 us -> 30 us
  transfers between devices with their start and end apart: 33 -> 38, of which waited for: 14 -> 17; matrix products, arithmetic and copies ran while one was open for 20% -> 22% of each run, Pallas kernels for 0% -> 0%
where the time goes in v6:
time: 1060 us
  Pallas kernels  524 us (49%)
  waiting for transfers between devices  168 us (16%)
  matrix products  103 us (10%)
  local copies, waits for them, and re-layouts  86.3 us (8%)
  other arithmetic  77.9 us (7%)
  blocking collectives  48.6 us (5%)
  starting transfers between devices  31.2 us (3%)
  between operations  16.7 us (2%)
    pallas_call x1, Pallas kernels, moe(): pl.pallas_call(functools.partial(moe_kernel, sizes), grid=(chunks, 2 * bl...  524 us
    ppermute x2, waiting for transfers between devices, pull(): return lax.ppermute(values, 'dp', pairs)  86.9 us
    all_to_all x1, blocking collectives, per_device(): lax.all_to_all(attended.reshape(tensor_count, block_rows, local_width), '...  48.6 us
    ppermute x9, waiting for transfers between devices, swap_inner(): return lax.ppermute(values, 'dp', self.inner)  37 us
    unnamed x206, local copies, waits for them, and re-layouts  30 us
    all_to_all x1, waiting for transfers between devices, per_device(): grad_mixed = lax.all_to_all(grad_heads, 'tensor', 0, 0)  22.4 us
  transfers between devices with their start and end apart: 38, of which 17 were waited for; matrix products, arithmetic and copies ran while one was open for 22% of the time, Pallas kernels for 0%

profile of v6, /device:TPU:0, one launch (start us, length us, event | category | flops | bytes accessed | tf_op | source)
XLA Modules:
  0.0 1056.1 jit_solution(4841802116254209788)
XLA Ops:
  20.8 85.7 %collective-permute-done.1.others_refs_2_ = bf16[1024,2048]{1,0:T(8,128)(2,1)} collective-permute-done((bf16[1024,2048]{1,0:T(8,128)(2,1)}, bf16[1024,2048]{1,0:T(8,128)(2,1)}, u32[]{:S(2)}, u32[]{:S(2)}) %collective-permute-start.1) | collective-permute-done | bytes 4194336 | tf_op jit(solution)/shard_map/ppermute | solution.py:764
  116.9 5.3 multiply_reduce_fusion.9
  124.6 6.7 multiply_reduce_fusion.10
  133.4 3.7 multiply_multiply_fusion
  149.9 4.2 fusion.1
  164.0 4.9 pad_maximum_fusion.others_refs_3_
  169.4 48.6 %all_to_all.19 = bf16[4,256,512]{2,1,0:T(8,128)(2,1)S(1)} all-to-all(bf16[4,256,512]{2,1,0:T(8,128)(2,1)S(1)} %bitcast.308), channel_id=1, replica_groups=mesh['dp'=8,'tensor'=4] {'tensor'}, dimensions={0} | all-to-all | bytes 2097152 | tf_op jit(solution)/shard_map/all_to_all | solution.py:903
  236.9 524.4 %moe.1 = (bf16[256,4224]{1,0:T(8,128)(2,1)}, f32[4,3,256,2048]{3,2,1,0:T(8,128)}, bf16[8,256,2048]{2,1,0:T(8,128)(2,1)}, bf16[4,256,2176]{2,1,0:T(8,128)(2,1)}, ...) custom-call(bf16[256,2176]{1,0:T(8,128)(2,1)} %concatenate.47.own_re, ...), custom_call_target="tpu_custom_call" | custom-call | flops 139586437120 | bytes 142606336 | tf_op jit(solution)/shard_map/moe/pallas_call | solution.py:709
  781.3 3.5 all-to-all-start.1
  787.0 22.4 %all-to-all-done.1 = bf16[4,256,512]{2,1,0:T(8,128)(2,1)S(1)} async-done(((bf16[4,256,512]{2,1,0:T(8,128)(2,1)}), bf16[4,256,512]{2,1,0:T(8,128)(2,1)S(1)}, u32[]{:S(2)}, u32[]{:S(2)}) %all-to-all-start.1) | async-done | bytes 1048608 | tf_op jit(solution)/shard_map/all_to_all | solution.py:990
  812.4 4.7 fusion.156
  817.1 5.6 fusion.5
  830.1 9.8 multiply_reduce_fusion.1
  839.9 8.8 multiply_convert_fusion.1
  855.0 3.4 multiply_add_fusion.1
  865.4 4.0 multiply_reduce_fusion.4
  872.3 4.9 convolution_convert_fusion.3
  884.3 6.1 add_convert_fusion
  898.9 5.5 dynamic-slice_bitcast_fusion
  904.4 18.2 %slice_bitcast_fusion = (f32[4,256,2048]{2,1,0:T(8,128)}, f32[4,2048,256]{1,2,0:T(8,128)}, f32[4,2048,256]{1,2,0:T(8,128)}) fusion(f32[4,3,256,2048]{3,2,1,0:T(8,128)} %get-tuple-element.62), kind=kLoop, calls=%fused_computation.2 | loop fusion | bytes 50331648 | tf_op jit(solution)/shard_map/squeeze | solution.py:1052
  922.6 5.0 convolution_convert_fusion.1
  930.6 4.7 collective-permute-done.27
  935.5 3.9 collective-permute-done.28
  941.6 4.7 collective-permute-done.31
  946.2 3.7 collective-permute-done.30
  953.7 3.7 collective-permute-done.16
  975.2 8.8 copy.208
  984.1 8.7 copy.209
  998.9 5.2 collective-permute-done.14
  1006.7 12.2 %collective-permute-done.12 = bf16[2,256,1024]{2,1,0:T(8,128)(2,1)S(1)} collective-permute-done((bf16[2,256,1024]{2,1,0:T(8,128)(2,1)S(1)}, bf16[2,256,1024]{2,1,0:T(8,128)(2,1)S(1)}, u32[]{:S(2)}, u32[]{:S(2)}) %collective-permute-start.12) | collective-permute-done | bytes 1048608 | tf_op jit(solution)/shard_map/ppermute | solution.py:767
  1025.4 7.4 collective-permute-done.15
  1040.9 5.1 fusion.55
  (426 shorter events, 185.9 us)
Async XLA Ops:
  7.2 100.8 %all-gather.5.cloned.1.call-start = ((), (), s32[]{:S(2)}) async-start(), calls=%async_computation.4 | async-start | bytes 5242880 | tf_op jit(solution)/shard_map/all_gather | solution.py:862
  12.6 205.5 %all-gather.9.cloned.1.call-start = ((), (), s32[]{:S(2)}) async-start(), calls=%async_computation.7 | async-start | bytes 5242880 | tf_op jit(solution)/shard_map/all_gather | solution.py:869
  12.6 94.0 %collective-permute-start.1 = (bf16[1024,2048]{1,0:T(8,128)(2,1)}, bf16[1024,2048]{1,0:T(8,128)(2,1)}, u32[]{:S(2)}, u32[]{:S(2)}) collective-permute-start(bf16[1024,2048]{1,0:T(8,128)(2,1)} %bitcast.317), channel_id=1, source_target_pairs={{16,0},{20,4},{24,8},{28,12},{0,16},{4,20},{8,24},{12,28},{17,1},{... | collective-permute-start | bytes 12582920 | tf_op jit(solution)/shard_map/ppermute | solution.py:764
  15.7 92.3 %collective-permute-start = (bf16[1024,2048]{1,0:T(8,128)(2,1)}, bf16[1024,2048]{1,0:T(8,128)(2,1)}, u32[]{:S(2)}, u32[]{:S(2)}) collective-permute-start(bf16[1024,2048]{1,0:T(8,128)(2,1)} %bitcast.318), channel_id=1, source_target_pairs={{0,8},{4,12},{8,0},{12,4},{16,24},{20,28},{24,16},{28,20},{1,9},{5... | collective-permute-start | bytes 12582920 | tf_op jit(solution)/shard_map/ppermute | solution.py:767
  17.2 151.7 %collective-permute-start.4 = (bf16[1024,2048]{1,0:T(8,128)(2,1)}, bf16[1024,2048]{1,0:T(8,128)(2,1)}, u32[]{:S(2)}, u32[]{:S(2)}) collective-permute-start(bf16[1024,2048]{1,0:T(8,128)(2,1)} %bitcast.319), channel_id=1, source_target_pairs={{0,4},{4,0},{8,12},{12,8},{16,20},{20,16},{24,28},{28,24},{1,5},{5... | collective-permute-start | bytes 12582920 | tf_op jit(solution)/shard_map/ppermute | solution.py:770
  111.1 57.7 %collective-permute-start.5 = (bf16[1024,2048]{1,0:T(8,128)(2,1)}, bf16[1024,2048]{1,0:T(8,128)(2,1)}, u32[]{:S(2)}, u32[]{:S(2)}) collective-permute-start(bf16[1024,2048]{1,0:T(8,128)(2,1)} %collective-permute-done.others_refs_1_), channel_id=1, source_target_pairs={{0,4},{4,0},{8,12},{12,8},{16,20},{20,16},{24,28},{28,24},{1,5},{5... | collective-permute-start | bytes 12582920 | tf_op jit(solution)/shard_map/ppermute | solution.py:770
  114.3 54.5 %collective-permute-start.6 = (bf16[1024,2048]{1,0:T(8,128)(2,1)}, bf16[1024,2048]{1,0:T(8,128)(2,1)}, u32[]{:S(2)}, u32[]{:S(2)}) collective-permute-start(bf16[1024,2048]{1,0:T(8,128)(2,1)} %collective-permute-done.1.others_refs_2_), channel_id=1, source_target_pairs={{0,4},{4,0},{8,12},{12,8},{16,20},{20,16},{24,28},{28,24},{1,5},{5... | collective-permute-start | bytes 12582920 | tf_op jit(solution)/shard_map/ppermute | solution.py:770
  114.8 47.9 %collective-permute-start.3 = (bf16[512,2048]{1,0:T(8,128)(2,1)}, bf16[512,2048]{1,0:T(8,128)(2,1)}, u32[]{:S(2)}, u32[]{:S(2)}) collective-permute-start(bf16[512,2048]{1,0:T(8,128)(2,1)} %slice.132), channel_id=1, source_target_pairs={{0,8},{4,12},{8,0},{12,4},{16,24},{20,28},{24,16},{28,20},{1,9},{5... | collective-permute-start | bytes 6291464 | tf_op jit(solution)/shard_map/ppermute | solution.py:767
  116.4 47.6 %collective-permute-start.2 = (bf16[512,2048]{1,0:T(8,128)(2,1)}, bf16[512,2048]{1,0:T(8,128)(2,1)}, u32[]{:S(2)}, u32[]{:S(2)}) collective-permute-start(bf16[512,2048]{1,0:T(8,128)(2,1)} %slice.131), channel_id=1, source_target_pairs={{16,0},{20,4},{24,8},{28,12},{0,16},{4,20},{8,24},{12,28},{17,1},{... | collective-permute-start | bytes 6291464 | tf_op jit(solution)/shard_map/ppermute | solution.py:764
  220.0 16.9 %collective-permute-start.8 = (bf16[1024,2048]{1,0:T(8,128)(2,1)}, bf16[1024,2048]{1,0:T(8,128)(2,1)}, u32[]{:S(2)}, u32[]{:S(2)}) collective-permute-start(bf16[1024,2048]{1,0:T(8,128)(2,1)} %pad_maximum_fusion.others_refs_3_), channel_id=1, source_target_pairs={{0,4},{4,0},{8,12},{12,8},{16,20},{20,16},{24,28},{28,24},{1,5},{5... | collective-permute-start | bytes 12582920 | tf_op jit(solution)/shard_map/ppermute | solution.py:770
  781.3 28.1 %all-to-all-start.1 = ((bf16[4,256,512]{2,1,0:T(8,128)(2,1)}), bf16[4,256,512]{2,1,0:T(8,128)(2,1)S(1)}, u32[]{:S(2)}, u32[]{:S(2)}) async-start(bf16[4,256,512]{2,1,0:T(8,128)(2,1)} %pad_maximum_fusion.4), calls=%async_computation.1 | async-start | bytes 2097152 | tf_op jit(solution)/shard_map/all_to_all | solution.py:990
  784.8 109.9 %all-gather.7.cloned.1.call-start = ((), (), s32[]{:S(2)}) async-start(), calls=%async_computation.5 | async-start | bytes 5242880 | tf_op jit(solution)/shard_map/all_gather | solution.py:992
  810.8 224.4 %reduce-scatter.2.cloned.1.call-start = ((), (), s32[]{:S(2)}) async-start(), calls=%async_computation.6 | async-start | bytes 5242880 | tf_op jit(solution)/shard_map/reduce_scatter | solution.py:1048
  830.1 60.3 %collective-permute-start.10 = (bf16[2,2,256,512]{3,2,1,0:T(8,128)(2,1)}, bf16[2,2,256,512]{3,2,1,0:T(8,128)(2,1)}, u32[]{:S(2)}, u32[]{:S(2)}) collective-permute-start(bf16[2,2,256,512]{3,2,1,0:T(8,128)(2,1)} %dynamic-slice_bitcast_fusion.4), channel_id=1, source_target_pairs={{0,4},{4,0},{8,12},{12,8},{16,20},{20,16},{24,28},{28,24},{1,5},{5... | collective-permute-start | bytes 3145736 | tf_op jit(solution)/shard_map/ppermute | solution.py:770
  878.4 14.8 %collective-permute-start.9 = (bf16[2,2,256,512]{3,2,0,1:T(8,128)(2,1)}, bf16[2,2,256,512]{3,2,0,1:T(8,128)(2,1)}, u32[]{:S(2)}, u32[]{:S(2)}) collective-permute-start(bf16[2,2,256,512]{3,2,0,1:T(8,128)(2,1)} %bitcast.279), channel_id=1, source_target_pairs={{0,4},{4,0},{8,12},{12,8},{16,20},{20,16},{24,28},{28,24},{1,5},{5... | collective-permute-start | bytes 3145736 | tf_op jit(solution)/shard_map/ppermute | solution.py:770
  895.8 34.4 %collective-permute-start.26 = (f32[2,2,256,33]{2,1,0,3:T(2,128)S(1)}, f32[2,2,256,33]{2,1,0,3:T(2,128)S(1)}, u32[]{:S(2)}, u32[]{:S(2)}) collective-permute-start(f32[2,2,256,33]{2,1,0,3:T(2,128)S(1)} %bitcast.328), channel_id=1, source_target_pairs={{0,4},{4,0},{8,12},{12,8},{16,20},{20,16},{24,28},{28,24},{1,5},{5... | collective-permute-start | bytes 405512 | tf_op jit(solution)/shard_map/ppermute | solution.py:770
  897.1 54.6 %collective-permute-start.21 = (bf16[2,256,512]{2,1,0:T(8,128)(2,1)}, bf16[2,256,512]{2,1,0:T(8,128)(2,1)}, u32[]{:S(2)}, u32[]{:S(2)}) collective-permute-start(bf16[2,256,512]{2,1,0:T(8,128)(2,1)} %dynamic-slice_bitcast_fusion.6), channel_id=1, source_target_pairs={{0,16},{4,20},{8,24},{12,28},{16,0},{20,4},{24,8},{28,12},{1,17},{... | collective-permute-start | bytes 1572872 | tf_op jit(solution)/shard_map/ppermute | solution.py:774
  904.4 63.6 %collective-permute-start.11 = (bf16[2,2,256,2048]{3,2,1,0:T(8,128)(2,1)}, bf16[2,2,256,2048]{3,2,1,0:T(8,128)(2,1)S(1)}, u32[]{:S(2)}, u32[]{:S(2)}) collective-permute-start(bf16[2,2,256,2048]{3,2,1,0:T(8,128)(2,1)} %dynamic-slice_bitcast_fusion), channel_id=1, source_target_pairs={{0,4},{4,0},{8,12},{12,8},{16,20},{20,16},{24,28},{28,24},{1,5},{5... | collective-permute-start | bytes 12582920 | tf_op jit(solution)/shard_map/ppermute | solution.py:770
  940.5 9.5 collective-permute-start.29
  946.2 11.2 %collective-permute-start.16 = (bf16[2,256,512]{2,1,0:T(8,128)(2,1)S(1)}, bf16[2,256,512]{2,1,0:T(8,128)(2,1)S(1)}, u32[]{:S(2)}, u32[]{:S(2)}) collective-permute-start(bf16[2,256,512]{2,1,0:T(8,128)(2,1)S(1)} %dynamic-slice_bitcast_fusion.8), channel_id=1, source_target_pairs={{0,8},{4,12},{8,0},{12,4},{16,24},{20,28},{24,16},{28,20},{1,9},{5... | collective-permute-start | bytes 1572872 | tf_op jit(solution)/shard_map/ppermute | solution.py:767
  950.0 13.0 %collective-permute-start.23 = (bf16[2,2,256,512]{3,2,0,1:T(8,128)(2,1)S(1)}, bf16[2,2,256,512]{3,2,0,1:T(8,128)(2,1)S(1)}, u32[]{:S(2)}, u32[]{:S(2)}) collective-permute-start(bf16[2,2,256,512]{3,2,0,1:T(8,128)(2,1)S(1)} %bitcast.325), channel_id=1, source_target_pairs={{0,4},{4,0},{8,12},{12,8},{16,20},{20,16},{24,28},{28,24},{1,5},{5... | collective-permute-start | bytes 3145736 | tf_op jit(solution)/shard_map/ppermute | solution.py:770
  950.0 15.3 %collective-permute-start.18 = (bf16[2,2,256,512]{3,2,1,0:T(8,128)(2,1)S(1)}, bf16[2,2,256,512]{3,2,1,0:T(8,128)(2,1)S(1)}, u32[]{:S(2)}, u32[]{:S(2)}) collective-permute-start(bf16[2,2,256,512]{3,2,1,0:T(8,128)(2,1)S(1)} %dynamic-slice_bitcast_fusion.1), channel_id=1, source_target_pairs={{0,4},{4,0},{8,12},{12,8},{16,20},{20,16},{24,28},{28,24},{1,5},{5... | collective-permute-start | bytes 3145736 | tf_op jit(solution)/shard_map/ppermute | solution.py:770
  957.6 15.8 %collective-permute-start.17 = (bf16[256,512]{1,0:T(8,128)(2,1)S(1)}, bf16[256,512]{1,0:T(8,128)(2,1)}, u32[]{:S(2)}, u32[]{:S(2)}) collective-permute-start(bf16[256,512]{1,0:T(8,128)(2,1)S(1)} %dynamic-slice_bitcast_fusion.14), channel_id=1, source_target_pairs={{0,16},{4,20},{8,24},{12,28},{16,0},{20,4},{24,8},{28,12},{1,17},{... | collective-permute-start | bytes 786440 | tf_op jit(solution)/shard_map/ppermute | solution.py:774
  964.1 29.6 %collective-permute-start.24 = (bf16[2,256,512]{2,1,0:T(8,128)(2,1)}, bf16[2,256,512]{2,1,0:T(8,128)(2,1)}, u32[]{:S(2)}, u32[]{:S(2)}) collective-permute-start(bf16[2,256,512]{2,1,0:T(8,128)(2,1)} %dynamic-slice_bitcast_fusion.5), channel_id=1, source_target_pairs={{0,8},{4,12},{8,0},{12,4},{16,24},{20,28},{24,16},{28,20},{1,9},{5... | collective-permute-start | bytes 1572872 | tf_op jit(solution)/shard_map/ppermute | solution.py:767
  966.6 29.9 %collective-permute-start.19 = (bf16[2,256,512]{2,1,0:T(8,128)(2,1)}, bf16[2,256,512]{2,1,0:T(8,128)(2,1)}, u32[]{:S(2)}, u32[]{:S(2)}) collective-permute-start(bf16[2,256,512]{2,1,0:T(8,128)(2,1)} %dynamic-slice_bitcast_fusion.7), channel_id=1, source_target_pairs={{0,16},{4,20},{8,24},{12,28},{16,0},{20,4},{24,8},{28,12},{1,17},{... | collective-permute-start | bytes 1572872 | tf_op jit(solution)/shard_map/ppermute | solution.py:774
  972.9 31.3 %collective-permute-start.14 = (bf16[2,256,1024]{2,1,0:T(8,128)(2,1)}, bf16[2,256,1024]{2,1,0:T(8,128)(2,1)}, u32[]{:S(2)}, u32[]{:S(2)}) collective-permute-start(bf16[2,256,1024]{2,1,0:T(8,128)(2,1)} %dynamic-slice_bitcast_fusion.2), channel_id=1, source_target_pairs={{0,16},{4,20},{8,24},{12,28},{16,0},{20,4},{24,8},{28,12},{1,17},{... | collective-permute-start | bytes 3145736 | tf_op jit(solution)/shard_map/ppermute | solution.py:774
  992.8 26.1 %collective-permute-start.12 = (bf16[2,256,1024]{2,1,0:T(8,128)(2,1)S(1)}, bf16[2,256,1024]{2,1,0:T(8,128)(2,1)S(1)}, u32[]{:S(2)}, u32[]{:S(2)}) collective-permute-start(bf16[2,256,1024]{2,1,0:T(8,128)(2,1)S(1)} %dynamic-slice_bitcast_fusion.3), channel_id=1, source_target_pairs={{0,8},{4,12},{8,0},{12,4},{16,24},{20,28},{24,16},{28,20},{1,9},{5... | collective-permute-start | bytes 3145736 | tf_op jit(solution)/shard_map/ppermute | solution.py:767
  995.0 25.9 %collective-permute-start.25 = (bf16[256,512]{1,0:T(8,128)(2,1)S(1)}, bf16[256,512]{1,0:T(8,128)(2,1)S(1)}, u32[]{:S(2)}, u32[]{:S(2)}) collective-permute-start(bf16[256,512]{1,0:T(8,128)(2,1)S(1)} %dynamic-slice_bitcast_fusion.11), channel_id=1, source_target_pairs={{0,16},{4,20},{8,24},{12,28},{16,0},{20,4},{24,8},{28,12},{1,17},{... | collective-permute-start | bytes 786440 | tf_op jit(solution)/shard_map/ppermute | solution.py:774
  997.6 26.9 %collective-permute-start.20 = (bf16[256,512]{1,0:T(8,128)(2,1)S(1)}, bf16[256,512]{1,0:T(8,128)(2,1)S(1)}, u32[]{:S(2)}, u32[]{:S(2)}) collective-permute-start(bf16[256,512]{1,0:T(8,128)(2,1)S(1)} %dynamic-slice_bitcast_fusion.13), channel_id=1, source_target_pairs={{0,8},{4,12},{8,0},{12,4},{16,24},{20,28},{24,16},{28,20},{1,9},{5... | collective-permute-start | bytes 786440 | tf_op jit(solution)/shard_map/ppermute | solution.py:767
  1005.8 27.0 %collective-permute-start.15 = (bf16[256,1024]{1,0:T(8,128)(2,1)S(1)}, bf16[256,1024]{1,0:T(8,128)(2,1)S(1)}, u32[]{:S(2)}, u32[]{:S(2)}) collective-permute-start(bf16[256,1024]{1,0:T(8,128)(2,1)S(1)} %dynamic-slice_bitcast_fusion.9), channel_id=1, source_target_pairs={{0,8},{4,12},{8,0},{12,4},{16,24},{20,28},{24,16},{28,20},{1,9},{5... | collective-permute-start | bytes 1572872 | tf_op jit(solution)/shard_map/ppermute | solution.py:767
  1019.4 14.6 %collective-permute-start.13 = (bf16[256,1024]{1,0:T(8,128)(2,1)S(1)}, bf16[256,1024]{1,0:T(8,128)(2,1)S(1)}, u32[]{:S(2)}, u32[]{:S(2)}) collective-permute-start(bf16[256,1024]{1,0:T(8,128)(2,1)S(1)} %dynamic-slice_bitcast_fusion.10), channel_id=1, source_target_pairs={{0,16},{4,20},{8,24},{12,28},{16,0},{20,4},{24,8},{28,12},{1,17},{... | collective-permute-start | bytes 1572872 | tf_op jit(solution)/shard_map/ppermute | solution.py:774
  1038.2 10.0 all-to-all-start.2
  (107 other events, 2673.8 us)
Sparse Core Ops, SparseCore 0:
  12.7 83.4 all-gather.4
  115.0 102.3 all-gather.8
  810.9 79.1 all-gather.6
  894.9 78.2 reduce-scatter.1

commit v7 on v6

--- a/solution.py
+++ b/solution.py
@@ -967,6 +967,7 @@
     combined = wide(combined)
     grad_moe = combined[:, :width]
     grad_probs = combined[:, width : width + all_experts]
+    late = plane.fold_core(late.reshape(-1, width))
     grad_own = lax.dynamic_slice_in_dim(cotangent[0], own_start, block_rows, 0).astype(jnp.float32)
     grad_logits = (
         own_probs * (grad_probs - jnp.sum(own_probs * grad_probs, axis=-1, keepdims=True))
@@ -988,7 +989,6 @@
         ]
     )
     grad_mixed = lax.all_to_all(grad_heads, "tensor", 0, 0)
-    grad_mixed, grad_attn = tie(grad_mixed, grad_attn)
     grad_attn_all = lax.all_gather(grad_attn, "tensor", axis=0, tiled=True)
     grad_mixed = grad_mixed.reshape(full_length, -1, head_dim)
     grad_query_parts = []
@@ -1031,14 +1031,10 @@
     from_query = jnp.einsum("lh,dh->ld", grad_q_low, w_query, preferred_element_type=jnp.float32)
     from_key = jnp.einsum("lh,dh->ld", grad_k_low, w_key, preferred_element_type=jnp.float32)
     from_value = jnp.einsum("lh,dh->ld", grad_v_low, w_value, preferred_element_type=jnp.float32)
-    query_part = plane.fold_core(low(query_part))
-    value_part = plane.fold_core(low(value_part))
-    grad_gathered = low(from_query + from_key + from_value)
-    grad_gathered, grad_attn_all, sums, router_part, late, grad_k_late, query_part, value_part = tie(
-        grad_gathered, grad_attn_all, sums, router_part, late, grad_k_low, query_part, value_part
+    grad_gathered, grad_attn_all, sums = tie(
+        low(from_query + from_key + from_value), grad_attn_all, sums
     )
     cut = width // 2
-    late = plane.fold_core(late.reshape(-1, width))
     late = [
         plane.scatter_rest(late[..., :cut], late.dtype, True),
         plane.scatter_rest(late[..., cut:], late.dtype, False),
@@ -1050,17 +1046,16 @@
     grad_gate = jnp.swapaxes(sums[:, 0], 1, 2)
     grad_up = jnp.swapaxes(sums[:, 1], 1, 2)
     grad_down = sums[:, 2]
-    key_part = jnp.einsum("ld,lh->dh", gathered, grad_k_late, preferred_element_type=jnp.float32)
-    key_part = plane.fold_core(low(key_part))
-    key_part, grad_gate, grad_up, grad_down = tie(key_part, grad_gate, grad_up, grad_down)
+    grad_k_low, grad_gate, grad_up, grad_down = tie(grad_k_low, grad_gate, grad_up, grad_down)
+    key_part = jnp.einsum("ld,lh->dh", gathered, grad_k_low, preferred_element_type=jnp.float32)
     out_part = jnp.einsum("ld,lh->dh", grad_attn_all, attended, preferred_element_type=jnp.float32)
     attn_pull = jax.vjp(rms_scale, token_values, attn_gain)[1]
     grad_tok_norm, attn_part = attn_pull(grad_normed)
     grad_tokens = (grad_residual + grad_tok_norm).astype(jnp.bfloat16)
     grad_out = plane.scatter(low(out_part), True)
-    grad_value = plane.scatter_rest(value_part, value_part.dtype, False)
-    grad_query = plane.scatter_rest(query_part, query_part.dtype, True)
-    grad_key = plane.scatter_rest(key_part, key_part.dtype, False)
+    grad_value = plane.scatter(low(value_part), False)
+    grad_query = plane.scatter(low(query_part), True)
+    grad_key = plane.scatter(low(key_part), False)
     routing = plane.scatter(jnp.concatenate([router_part, ffn_part[:, None]], axis=1), False)
     routing = ring_sum(routing, tensor_count)
     parts = [v.reshape(data_count, -1) for v in (attn_part, q_part, k_part)]

time: 1060 us -> 1100 us (1.038)
  starting transfers between devices: 31.2 us -> 42.7 us
  local copies, waits for them, and re-layouts: 86.3 us -> 97.8 us
    ppermute x2, waiting for transfers between devices: 86.9 us -> 1.56 us  [pull(): return lax.ppermute(values, 'dp', pairs)]
    ppermute x9, waiting for transfers between devices: 37 us -> 117 us  [swap_inner(): return lax.ppermute(values, 'dp', self.inner)]
    unnamed x206 -> x196, local copies, waits for them, and re-layouts: 30 us -> 32.8 us
  transfers between devices with their start and end apart: 38 -> 38, of which waited for: 17 -> 16; matrix products, arithmetic and copies ran while one was open for 22% -> 23% of each run, Pallas kernels for 0% -> 0%
where the time goes in v7:
time: 1100 us; the launch traced here: 1090 us
  Pallas kernels  524 us (48%)
  waiting for transfers between devices  162 us (15%)
  matrix products  110 us (10%)
  local copies, waits for them, and re-layouts  97.8 us (9%)
  other arithmetic  85.6 us (8%)
  blocking collectives  51.8 us (5%)
  starting transfers between devices  42.7 us (4%)
  between operations  16.6 us (2%)
    pallas_call x1, Pallas kernels, moe(): pl.pallas_call(functools.partial(moe_kernel, sizes), grid=(chunks, 2 * bl...  524 us
    ppermute x9, waiting for transfers between devices, swap_inner(): return lax.ppermute(values, 'dp', self.inner)  117 us
    all_to_all x1, blocking collectives, per_device(): lax.all_to_all(attended.reshape(tensor_count, block_rows, local_width), '...  51.8 us
    unnamed x196, local copies, waits for them, and re-layouts  32.8 us
    all_to_all x1, waiting for transfers between devices, per_device(): grad_mixed = lax.all_to_all(grad_heads, 'tensor', 0, 0)  23.2 us
  transfers between devices with their start and end apart: 38, of which 16 were waited for; matrix products, arithmetic and copies ran while one was open for 23% of the time, Pallas kernels for 0%

profile of v7, /device:TPU:0, one launch (start us, length us, event | category | flops | bytes accessed | tf_op | source)
XLA Modules:
  0.0 1090.6 jit_solution(16143899811105255553)
XLA Ops:
  20.9 85.7 %collective-permute-done.others_refs_1_ = bf16[1024,2048]{1,0:T(8,128)(2,1)} collective-permute-done((bf16[1024,2048]{1,0:T(8,128)(2,1)}, bf16[1024,2048]{1,0:T(8,128)(2,1)}, u32[]{:S(2)}, u32[]{:S(2)}) %collective-permute-start) | collective-permute-done | bytes 4194336 | tf_op jit(solution)/shard_map/ppermute | solution.py:767
  108.0 3.3 slice.131
  111.3 3.3 slice.132
  119.5 6.6 multiply_reduce_fusion.9
  145.9 4.4 fusion.1
  156.1 20.0 %collective-permute-done.3 = bf16[512,2048]{1,0:T(8,128)(2,1)} collective-permute-done((bf16[512,2048]{1,0:T(8,128)(2,1)}, bf16[512,2048]{1,0:T(8,128)(2,1)}, u32[]{:S(2)}, u32[]{:S(2)}) %collective-permute-start.3) | collective-permute-done | bytes 2097184 | tf_op jit(solution)/shard_map/ppermute | solution.py:767
  176.2 4.8 pad_maximum_fusion.others_refs_3_
  181.6 51.8 %all_to_all.19 = bf16[4,256,512]{2,1,0:T(8,128)(2,1)S(1)} all-to-all(bf16[4,256,512]{2,1,0:T(8,128)(2,1)S(1)} %bitcast.310), channel_id=1, replica_groups=mesh['dp'=8,'tensor'=4] {'tensor'}, dimensions={0} | all-to-all | bytes 2097152 | tf_op jit(solution)/shard_map/all_to_all | solution.py:903
  252.6 524.5 %moe.1 = (bf16[256,4224]{1,0:T(8,128)(2,1)}, f32[4,3,256,2048]{3,2,1,0:T(8,128)}, bf16[8,256,2048]{2,1,0:T(8,128)(2,1)}, bf16[4,256,2176]{2,1,0:T(8,128)(2,1)}, ...) custom-call(bf16[256,2176]{1,0:T(8,128)(2,1)} %concatenate.45.own_re, ...), custom_call_target="tpu_custom_call" | custom-call | flops 139586437120 | bytes 142606336 | tf_op jit(solution)/shard_map/moe/pallas_call | solution.py:709
  798.1 4.3 all-to-all-start.1
  813.4 4.8 dynamic-slice_bitcast_fusion
  818.8 3.7 collective-permute-start.31
  822.5 23.2 %all-to-all-done.1 = bf16[4,256,512]{2,1,0:T(8,128)(2,1)} async-done(((bf16[4,256,512]{2,1,0:T(8,128)(2,1)}), bf16[4,256,512]{2,1,0:T(8,128)(2,1)}, u32[]{:S(2)}, u32[]{:S(2)}) %all-to-all-start.1) | async-done | bytes 1048608 | tf_op jit(solution)/shard_map/all_to_all | solution.py:991
  852.0 5.7 fusion.162
  861.9 11.2 %multiply_reduce_fusion.1 = (f32[4,512]{1,0:T(4,128)S(1)}, f32[4,512]{1,0:T(4,128)S(1)}, f32[4,512,1024]{2,1,0:T(8,128)S(1)}) fusion(f32[4,512]{1,0:T(4,128)S(1)} %log_add_fusion.1, f32[4,512,1024]{2,1,0:T(8,128)} %copy-done.2, pred[1024]{0:T(1024)(128)(4,1)S(1)} %copy-done.78, f32[4,512,1024]{2,1,0:T(8,128)} %fusion.162, f32[4,512]{1,0:T(4,128)S(1)} %log_add_fusion, ...), kind=kOutput, calls=%fused_computation.10 | convolution fusion | flops 557838336 | bytes 35161088 | tf_op jit(solution)/shard_map/qhd,khd->hqk/dot_general | solution.py:1005
  873.0 10.4 multiply_convert_fusion.1
  889.6 3.4 multiply_add_fusion.1
  898.5 4.9 convolution_convert_fusion.3
  905.1 5.3 fusion.5
  917.8 5.8 fusion.163
  930.7 4.3 fusion.164
  942.0 8.1 add_convert_fusion
  952.2 6.9 collective-permute-start.29
  973.9 5.4 fusion
  982.2 18.0 %slice_bitcast_fusion = (f32[4,256,2048]{2,1,0:T(8,128)}, f32[4,2048,256]{1,2,0:T(8,128)}, f32[4,2048,256]{1,2,0:T(8,128)}) fusion(f32[4,3,256,2048]{3,2,1,0:T(8,128)} %get-tuple-element.50), kind=kLoop, calls=%fused_computation.2 | loop fusion | bytes 50331648 | tf_op jit(solution)/shard_map/squeeze | solution.py:1048
  1000.2 4.7 convolution_convert_fusion.2
  1018.9 8.1 collective-permute-done.13
  1028.1 11.5 %collective-permute-done.18 = bf16[2,256,512]{2,1,0:T(8,128)(2,1)S(1)} collective-permute-done((bf16[2,256,512]{2,1,0:T(8,128)(2,1)S(1)}, bf16[2,256,512]{2,1,0:T(8,128)(2,1)S(1)}, u32[]{:S(2)}, u32[]{:S(2)}) %collective-permute-start.18) | collective-permute-done | bytes 524320 | tf_op jit(solution)/shard_map/ppermute | solution.py:774
  1044.1 8.7 copy.208
  1052.8 8.7 copy.209
  1068.5 6.7 all-to-all-start.2
  1075.3 5.1 fusion.55
  (412 shorter events, 190.7 us)
Async XLA Ops:
  7.2 100.8 %all-gather.5.cloned.1.call-start = ((), (), s32[]{:S(2)}) async-start(), calls=%async_computation.4 | async-start | bytes 5242880 | tf_op jit(solution)/shard_map/all_gather | solution.py:862
  12.6 221.1 %all-gather.9.cloned.1.call-start = ((), (), s32[]{:S(2)}) async-start(), calls=%async_computation.7 | async-start | bytes 5242880 | tf_op jit(solution)/shard_map/all_gather | solution.py:869
  12.6 93.9 %collective-permute-start = (bf16[1024,2048]{1,0:T(8,128)(2,1)}, bf16[1024,2048]{1,0:T(8,128)(2,1)}, u32[]{:S(2)}, u32[]{:S(2)}) collective-permute-start(bf16[1024,2048]{1,0:T(8,128)(2,1)} %bitcast.319), channel_id=1, source_target_pairs={{0,8},{4,12},{8,0},{12,4},{16,24},{20,28},{24,16},{28,20},{1,9},{5... | collective-permute-start | bytes 12582920 | tf_op jit(solution)/shard_map/ppermute | solution.py:767
  15.7 92.3 %collective-permute-start.1 = (bf16[1024,2048]{1,0:T(8,128)(2,1)}, bf16[1024,2048]{1,0:T(8,128)(2,1)}, u32[]{:S(2)}, u32[]{:S(2)}) collective-permute-start(bf16[1024,2048]{1,0:T(8,128)(2,1)} %bitcast.320), channel_id=1, source_target_pairs={{16,0},{20,4},{24,8},{28,12},{0,16},{4,20},{8,24},{12,28},{17,1},{... | collective-permute-start | bytes 12582920 | tf_op jit(solution)/shard_map/ppermute | solution.py:764
  17.2 163.9 %collective-permute-start.4 = (bf16[1024,2048]{1,0:T(8,128)(2,1)}, bf16[1024,2048]{1,0:T(8,128)(2,1)}, u32[]{:S(2)}, u32[]{:S(2)}) collective-permute-start(bf16[1024,2048]{1,0:T(8,128)(2,1)} %bitcast.321), channel_id=1, source_target_pairs={{0,4},{4,0},{8,12},{12,8},{16,20},{20,16},{24,28},{28,24},{1,5},{5... | collective-permute-start | bytes 12582920 | tf_op jit(solution)/shard_map/ppermute | solution.py:770
  111.3 69.7 %collective-permute-start.5 = (bf16[1024,2048]{1,0:T(8,128)(2,1)}, bf16[1024,2048]{1,0:T(8,128)(2,1)}, u32[]{:S(2)}, u32[]{:S(2)}) collective-permute-start(bf16[1024,2048]{1,0:T(8,128)(2,1)} %collective-permute-done.others_refs_1_), channel_id=1, source_target_pairs={{0,4},{4,0},{8,12},{12,8},{16,20},{20,16},{24,28},{28,24},{1,5},{5... | collective-permute-start | bytes 12582920 | tf_op jit(solution)/shard_map/ppermute | solution.py:770
  114.6 66.4 %collective-permute-start.6 = (bf16[1024,2048]{1,0:T(8,128)(2,1)}, bf16[1024,2048]{1,0:T(8,128)(2,1)}, u32[]{:S(2)}, u32[]{:S(2)}) collective-permute-start(bf16[1024,2048]{1,0:T(8,128)(2,1)} %collective-permute-done.1.others_refs_2_), channel_id=1, source_target_pairs={{0,4},{4,0},{8,12},{12,8},{16,20},{20,16},{24,28},{28,24},{1,5},{5... | collective-permute-start | bytes 12582920 | tf_op jit(solution)/shard_map/ppermute | solution.py:770
  128.1 48.1 %collective-permute-start.3 = (bf16[512,2048]{1,0:T(8,128)(2,1)}, bf16[512,2048]{1,0:T(8,128)(2,1)}, u32[]{:S(2)}, u32[]{:S(2)}) collective-permute-start(bf16[512,2048]{1,0:T(8,128)(2,1)} %slice.132), channel_id=1, source_target_pairs={{0,8},{4,12},{8,0},{12,4},{16,24},{20,28},{24,16},{28,20},{1,9},{5... | collective-permute-start | bytes 6291464 | tf_op jit(solution)/shard_map/ppermute | solution.py:767
  128.5 47.7 %collective-permute-start.2 = (bf16[512,2048]{1,0:T(8,128)(2,1)}, bf16[512,2048]{1,0:T(8,128)(2,1)}, u32[]{:S(2)}, u32[]{:S(2)}) collective-permute-start(bf16[512,2048]{1,0:T(8,128)(2,1)} %slice.131), channel_id=1, source_target_pairs={{16,0},{20,4},{24,8},{28,12},{0,16},{4,20},{8,24},{12,28},{17,1},{... | collective-permute-start | bytes 6291464 | tf_op jit(solution)/shard_map/ppermute | solution.py:764
  235.7 16.9 %collective-permute-start.8 = (bf16[1024,2048]{1,0:T(8,128)(2,1)}, bf16[1024,2048]{1,0:T(8,128)(2,1)}, u32[]{:S(2)}, u32[]{:S(2)}) collective-permute-start(bf16[1024,2048]{1,0:T(8,128)(2,1)} %pad_maximum_fusion.others_refs_3_), channel_id=1, source_target_pairs={{0,4},{4,0},{8,12},{12,8},{16,20},{20,16},{24,28},{28,24},{1,5},{5... | collective-permute-start | bytes 12582920 | tf_op jit(solution)/shard_map/ppermute | solution.py:770
  798.1 47.6 %all-to-all-start.1 = ((bf16[4,256,512]{2,1,0:T(8,128)(2,1)}), bf16[4,256,512]{2,1,0:T(8,128)(2,1)}, u32[]{:S(2)}, u32[]{:S(2)}) async-start(bf16[4,256,512]{2,1,0:T(8,128)(2,1)} %pad_maximum_fusion.4), calls=%async_computation.1 | async-start | bytes 2097152 | tf_op jit(solution)/shard_map/all_to_all | solution.py:991
  802.4 158.7 %all-gather.7.cloned.1.call-start = ((), (), s32[]{:S(2)}) async-start(), calls=%async_computation.5 | async-start | bytes 5242880 | tf_op jit(solution)/shard_map/all_gather | solution.py:992
  808.8 256.6 %reduce-scatter.2.cloned.1.call-start = ((), (), s32[]{:S(2)}) async-start(), calls=%async_computation.6 | async-start | bytes 5242880 | tf_op jit(solution)/shard_map/reduce_scatter | solution.py:1044
  818.2 155.7 %collective-permute-start.9 = (bf16[2,2,256,2048]{3,2,1,0:T(8,128)(2,1)}, bf16[2,2,256,2048]{3,2,1,0:T(8,128)(2,1)}, u32[]{:S(2)}, u32[]{:S(2)}) collective-permute-start(bf16[2,2,256,2048]{3,2,1,0:T(8,128)(2,1)} %dynamic-slice_bitcast_fusion), channel_id=1, source_target_pairs={{0,4},{4,0},{8,12},{12,8},{16,20},{20,16},{24,28},{28,24},{1,5},{5... | collective-permute-start | bytes 12582920 | tf_op jit(solution)/shard_map/ppermute | solution.py:770
  818.8 145.6 %collective-permute-start.31 = (f32[256,33]{0,1:T(8,128)}, f32[256,33]{0,1:T(8,128)}, u32[]{:S(2)}, u32[]{:S(2)}) collective-permute-start(f32[256,33]{0,1:T(8,128)} %bitcast_add_fusion.1), channel_id=1, source_target_pairs={{0,3},{1,0},{2,1},{3,2},{4,7},{5,4},{6,5},{7,6},{8,11},{9,8},{10,9... | collective-permute-start | bytes 101384 | tf_op jit(solution)/shard_map/ppermute | solution.py:746
  822.5 142.2 %collective-permute-start.30 = (f32[256,33]{0,1:T(8,128)}, f32[256,33]{0,1:T(8,128)}, u32[]{:S(2)}, u32[]{:S(2)}) collective-permute-start(f32[256,33]{0,1:T(8,128)} %bitcast_add_fusion.1), channel_id=1, source_target_pairs={{0,2},{1,3},{2,0},{3,1},{4,6},{5,7},{6,4},{7,5},{8,10},{9,11},{10,... | collective-permute-start | bytes 101384 | tf_op jit(solution)/shard_map/ppermute | solution.py:746
  904.6 30.4 %collective-permute-start.14 = (bf16[2,2,256,512]{3,2,0,1:T(8,128)(2,1)}, bf16[2,2,256,512]{3,2,0,1:T(8,128)(2,1)}, u32[]{:S(2)}, u32[]{:S(2)}) collective-permute-start(bf16[2,2,256,512]{3,2,0,1:T(8,128)(2,1)} %bitcast.286), channel_id=1, source_target_pairs={{0,4},{4,0},{8,12},{12,8},{16,20},{20,16},{24,28},{28,24},{1,5},{5... | collective-permute-start | bytes 3145736 | tf_op jit(solution)/shard_map/ppermute | solution.py:770
  917.7 21.5 %collective-permute-start.20 = (bf16[2,2,256,512]{3,2,1,0:T(8,128)(2,1)}, bf16[2,2,256,512]{3,2,1,0:T(8,128)(2,1)}, u32[]{:S(2)}, u32[]{:S(2)}) collective-permute-start(bf16[2,2,256,512]{3,2,1,0:T(8,128)(2,1)} %dynamic-slice_bitcast_fusion.1), channel_id=1, source_target_pairs={{0,4},{4,0},{8,12},{12,8},{16,20},{20,16},{24,28},{28,24},{1,5},{5... | collective-permute-start | bytes 3145736 | tf_op jit(solution)/shard_map/ppermute | solution.py:770
  937.6 14.6 %collective-permute-start.15 = (bf16[2,256,512]{2,1,0:T(8,128)(2,1)}, bf16[2,256,512]{2,1,0:T(8,128)(2,1)}, u32[]{:S(2)}, u32[]{:S(2)}) collective-permute-start(bf16[2,256,512]{2,1,0:T(8,128)(2,1)} %dynamic-slice_bitcast_fusion.8), channel_id=1, source_target_pairs={{0,8},{4,12},{8,0},{12,4},{16,24},{20,28},{24,16},{28,20},{1,9},{5... | collective-permute-start | bytes 1572872 | tf_op jit(solution)/shard_map/ppermute | solution.py:767
  941.9 19.3 %collective-permute-start.21 = (bf16[2,256,512]{2,1,0:T(8,128)(2,1)}, bf16[2,256,512]{2,1,0:T(8,128)(2,1)}, u32[]{:S(2)}, u32[]{:S(2)}) collective-permute-start(bf16[2,256,512]{2,1,0:T(8,128)(2,1)} %dynamic-slice_bitcast_fusion.6), channel_id=1, source_target_pairs={{0,16},{4,20},{8,24},{12,28},{16,0},{20,4},{24,8},{28,12},{1,17},{... | collective-permute-start | bytes 1572872 | tf_op jit(solution)/shard_map/ppermute | solution.py:774
  952.2 12.7 %collective-permute-start.29 = (f32[256,33]{0,1:T(8,128)}, f32[256,33]{0,1:T(8,128)}, u32[]{:S(2)}, u32[]{:S(2)}) collective-permute-start(f32[256,33]{0,1:T(8,128)} %bitcast_add_fusion.1), channel_id=1, source_target_pairs={{0,1},{1,2},{2,3},{3,0},{4,5},{5,6},{6,7},{7,4},{8,9},{9,10},{10,1... | collective-permute-start | bytes 101384 | tf_op jit(solution)/shard_map/ppermute | solution.py:746
  980.9 28.2 %collective-permute-start.12 = (bf16[2,256,1024]{2,1,0:T(8,128)(2,1)}, bf16[2,256,1024]{2,1,0:T(8,128)(2,1)}, u32[]{:S(2)}, u32[]{:S(2)}) collective-permute-start(bf16[2,256,1024]{2,1,0:T(8,128)(2,1)} %dynamic-slice_bitcast_fusion.3), channel_id=1, source_target_pairs={{0,16},{4,20},{8,24},{12,28},{16,0},{20,4},{24,8},{28,12},{1,17},{... | collective-permute-start | bytes 3145736 | tf_op jit(solution)/shard_map/ppermute | solution.py:774
  981.6 32.1 %collective-permute-start.10 = (bf16[2,256,1024]{2,1,0:T(8,128)(2,1)S(1)}, bf16[2,256,1024]{2,1,0:T(8,128)(2,1)}, u32[]{:S(2)}, u32[]{:S(2)}) collective-permute-start(bf16[2,256,1024]{2,1,0:T(8,128)(2,1)S(1)} %dynamic-slice_bitcast_fusion.4), channel_id=1, source_target_pairs={{0,8},{4,12},{8,0},{12,4},{16,24},{20,28},{24,16},{28,20},{1,9},{5... | collective-permute-start | bytes 3145736 | tf_op jit(solution)/shard_map/ppermute | solution.py:767
  1005.1 11.8 %collective-permute-start.17 = (bf16[2,2,256,512]{3,2,1,0:T(8,128)(2,1)S(1)}, bf16[2,2,256,512]{3,2,1,0:T(8,128)(2,1)S(1)}, u32[]{:S(2)}, u32[]{:S(2)}) collective-permute-start(bf16[2,2,256,512]{3,2,1,0:T(8,128)(2,1)S(1)} %dynamic-slice_bitcast_fusion.2), channel_id=1, source_target_pairs={{0,4},{4,0},{8,12},{12,8},{16,20},{20,16},{24,28},{28,24},{1,5},{5... | collective-permute-start | bytes 3145736 | tf_op jit(solution)/shard_map/ppermute | solution.py:770
  1008.9 9.0 collective-permute-start.23
  1012.1 14.9 %collective-permute-start.13 = (bf16[256,1024]{1,0:T(8,128)(2,1)S(1)}, bf16[256,1024]{1,0:T(8,128)(2,1)S(1)}, u32[]{:S(2)}, u32[]{:S(2)}) collective-permute-start(bf16[256,1024]{1,0:T(8,128)(2,1)S(1)} %dynamic-slice_bitcast_fusion.9), channel_id=1, source_target_pairs={{0,8},{4,12},{8,0},{12,4},{16,24},{20,28},{24,16},{28,20},{1,9},{5... | collective-permute-start | bytes 1572872 | tf_op jit(solution)/shard_map/ppermute | solution.py:767
  1015.4 27.6 %collective-permute-start.11 = (bf16[256,1024]{1,0:T(8,128)(2,1)S(1)}, bf16[256,1024]{1,0:T(8,128)(2,1)S(1)}, u32[]{:S(2)}, u32[]{:S(2)}) collective-permute-start(bf16[256,1024]{1,0:T(8,128)(2,1)S(1)} %dynamic-slice_bitcast_fusion.10), channel_id=1, source_target_pairs={{0,16},{4,20},{8,24},{12,28},{16,0},{20,4},{24,8},{28,12},{1,17},{... | collective-permute-start | bytes 1572872 | tf_op jit(solution)/shard_map/ppermute | solution.py:774
  1017.2 22.4 %collective-permute-start.18 = (bf16[2,256,512]{2,1,0:T(8,128)(2,1)S(1)}, bf16[2,256,512]{2,1,0:T(8,128)(2,1)S(1)}, u32[]{:S(2)}, u32[]{:S(2)}) collective-permute-start(bf16[2,256,512]{2,1,0:T(8,128)(2,1)S(1)} %dynamic-slice_bitcast_fusion.7), channel_id=1, source_target_pairs={{0,16},{4,20},{8,24},{12,28},{16,0},{20,4},{24,8},{28,12},{1,17},{... | collective-permute-start | bytes 1572872 | tf_op jit(solution)/shard_map/ppermute | solution.py:774
  1018.3 22.2 %collective-permute-start.24 = (bf16[2,256,512]{2,1,0:T(8,128)(2,1)S(1)}, bf16[2,256,512]{2,1,0:T(8,128)(2,1)S(1)}, u32[]{:S(2)}, u32[]{:S(2)}) collective-permute-start(bf16[2,256,512]{2,1,0:T(8,128)(2,1)S(1)} %dynamic-slice_bitcast_fusion.5), channel_id=1, source_target_pairs={{0,8},{4,12},{8,0},{12,4},{16,24},{20,28},{24,16},{28,20},{1,9},{5... | collective-permute-start | bytes 1572872 | tf_op jit(solution)/shard_map/ppermute | solution.py:767
  1039.8 21.6 %collective-permute-start.19 = (bf16[256,512]{1,0:T(8,128)(2,1)S(1)}, bf16[256,512]{1,0:T(8,128)(2,1)}, u32[]{:S(2)}, u32[]{:S(2)}) collective-permute-start(bf16[256,512]{1,0:T(8,128)(2,1)S(1)} %dynamic-slice_bitcast_fusion.13), channel_id=1, source_target_pairs={{0,8},{4,12},{8,0},{12,4},{16,24},{20,28},{24,16},{28,20},{1,9},{5... | collective-permute-start | bytes 786440 | tf_op jit(solution)/shard_map/ppermute | solution.py:767
  1041.5 22.0 %collective-permute-start.25 = (bf16[256,512]{1,0:T(8,128)(2,1)}, bf16[256,512]{1,0:T(8,128)(2,1)}, u32[]{:S(2)}, u32[]{:S(2)}) collective-permute-start(bf16[256,512]{1,0:T(8,128)(2,1)} %dynamic-slice_bitcast_fusion.11), channel_id=1, source_target_pairs={{0,16},{4,20},{8,24},{12,28},{16,0},{20,4},{24,8},{28,12},{1,17},{... | collective-permute-start | bytes 786440 | tf_op jit(solution)/shard_map/ppermute | solution.py:774
  1068.5 14.1 %all-to-all-start.2 = ((f32[32,1,288]{2,1,0:T(1,128)}), f32[32,1,288]{2,1,0:T(1,128)S(1)}, u32[]{:S(2)}, u32[]{:S(2)}) async-start(f32[32,1,288]{2,1,0:T(1,128)} %all_to_all.14), calls=%async_computation.3 | async-start | bytes 98304 | tf_op jit(solution)/shard_map/all_to_all | solution.py:1063
  (103 other events, 1652.3 us)
Sparse Core Ops, SparseCore 0:
  12.7 83.4 all-gather.4
  130.3 103.2 all-gather.8
  808.9 88.5 all-gather.6
  961.3 77.5 reduce-scatter.1

commit v8 on v5

--- a/solution.py
+++ b/solution.py
@@ -737,11 +737,17 @@
 
     def scatter(self, values, inner_first):
         kind = values.dtype
-        index = lax.axis_index("dp")
-        core, b, a = index % 2, index // 2 % 2, index // 4
+        return self.scatter_rest(self.fold_core(values), kind, inner_first)
+
+    def fold_core(self, values):
+        core = lax.axis_index("dp") % 2
         parts = values.reshape(self.outer, 2, 2, values.shape[0] // self.count, values.shape[1])
         given = self.swap_core(pick(parts, 1 - core, 2))
-        parts = (wide(pick(parts, core, 2)) + wide(given)).astype(kind)
+        return (wide(pick(parts, core, 2)) + wide(given)).astype(values.dtype)
+
+    def scatter_rest(self, parts, kind, inner_first):
+        index = lax.axis_index("dp")
+        b, a = index // 2 % 2, index // 4
         if inner_first:
             return self.fold_outer(self.fold_inner(parts, b, 1, kind).astype(kind), a, kind)
         return self.fold_inner(self.fold_outer(parts, a, kind).astype(kind), b, 0, kind)
@@ -977,8 +983,8 @@
     from_query = jnp.einsum("lh,dh->ld", grad_q_low, w_query, preferred_element_type=jnp.float32)
     from_key = jnp.einsum("lh,dh->ld", grad_k_low, w_key, preferred_element_type=jnp.float32)
     from_value = jnp.einsum("lh,dh->ld", grad_v_low, w_value, preferred_element_type=jnp.float32)
-    grad_gathered, grad_attn_all, sums, router_part = tie(
-        low(from_query + from_key + from_value), grad_attn_all, sums, router_part
+    grad_gathered, grad_attn_all, sums, router_part, grad_k_late = tie(
+        low(from_query + from_key + from_value), grad_attn_all, sums, router_part, grad_k_low
     )
     grad_normed = wide(
         lax.psum_scatter(grad_gathered, "tensor", scatter_dimension=0, tiled=True)
@@ -986,8 +992,9 @@
     grad_gate = jnp.swapaxes(sums[:, 0], 1, 2)
     grad_up = jnp.swapaxes(sums[:, 1], 1, 2)
     grad_down = sums[:, 2]
-    grad_k_low, grad_gate, grad_up, grad_down = tie(grad_k_low, grad_gate, grad_up, grad_down)
-    key_part = jnp.einsum("ld,lh->dh", gathered, grad_k_low, preferred_element_type=jnp.float32)
+    key_part = jnp.einsum("ld,lh->dh", gathered, grad_k_late, preferred_element_type=jnp.float32)
+    key_part = plane.fold_core(low(key_part))
+    key_part, grad_gate, grad_up, grad_down = tie(key_part, grad_gate, grad_up, grad_down)
     out_part = jnp.einsum("ld,lh->dh", grad_attn_all, attended, preferred_element_type=jnp.float32)
     attn_pull = jax.vjp(rms_scale, token_values, attn_gain)[1]
     grad_tok_norm, attn_part = attn_pull(grad_normed)
@@ -995,7 +1002,7 @@
     grad_out = plane.scatter(low(out_part), True)
     grad_value = plane.scatter(low(value_part), False)
     grad_query = plane.scatter(low(query_part), True)
-    grad_key = plane.scatter(low(key_part), False)
+    grad_key = plane.scatter_rest(key_part, key_part.dtype, False)
     routing = plane.scatter(jnp.concatenate([router_part, ffn_part[:, None]], axis=1), False)
     routing = ring_sum(routing, tensor_count)
     parts = [v.reshape(data_count, -1) for v in (attn_part, q_part, k_part)]

time: 1060 us -> 1050 us (level)
    unnamed x196 -> x204, local copies, waits for them, and re-layouts: 28 us -> 30 us
  transfers between devices with their start and end apart: 33 -> 33, of which waited for: 14 -> 13; matrix products, arithmetic and copies ran while one was open for 20% -> 20% of each run, Pallas kernels for 0% -> 0%
where the time goes in v8:
time: 1050 us
  Pallas kernels  557 us (53%)
  waiting for transfers between devices  139 us (13%)
  matrix products  104 us (10%)
  local copies, waits for them, and re-layouts  79.1 us (8%)
  other arithmetic  71.9 us (7%)
  blocking collectives  48.6 us (5%)
  starting transfers between devices  30.2 us (3%)
  between operations  16.9 us (2%)
    pallas_call x1, Pallas kernels, moe(): pl.pallas_call(functools.partial(moe_kernel, sizes), grid=(chunks, 2 * bl...  557 us
    ppermute x2, waiting for transfers between devices, pull(): return lax.ppermute(values, 'dp', pairs)  86.9 us
    all_to_all x1, blocking collectives, per_device(): lax.all_to_all(attended.reshape(tensor_count, block_rows, local_width), '...  48.6 us
    unnamed x204, local copies, waits for them, and re-layouts  30 us
    all_to_all x1, waiting for transfers between devices, per_device(): grad_mixed = lax.all_to_all(grad_heads, 'tensor', 0, 0)  22.9 us
  transfers between devices with their start and end apart: 33, of which 13 were waited for; matrix products, arithmetic and copies ran while one was open for 20% of the time, Pallas kernels for 0%

profile of v8, /device:TPU:0, one launch (start us, length us, event | category | flops | bytes accessed | tf_op | source)
XLA Modules:
  0.0 1046.4 jit_solution(16521260292700436242)
XLA Ops:
  12.6 3.1 collective-permute-start.1
  20.9 85.7 %collective-permute-done.1.others_refs_2_ = bf16[1024,2048]{1,0:T(8,128)(2,1)} collective-permute-done((bf16[1024,2048]{1,0:T(8,128)(2,1)}, bf16[1024,2048]{1,0:T(8,128)(2,1)}, u32[]{:S(2)}, u32[]{:S(2)}) %collective-permute-start.1) | collective-permute-done | bytes 4194336 | tf_op jit(solution)/shard_map/ppermute | solution.py:715
  108.0 3.2 slice.125
  111.2 3.2 slice.126
  117.0 5.3 multiply_reduce_fusion.9
  124.5 6.8 multiply_reduce_fusion.10
  133.4 3.7 multiply_multiply_fusion
  149.9 4.2 fusion
  154.1 2.8 fusion.40
  159.9 2.9 collective-permute-done.3
  164.0 4.9 pad_maximum_fusion.others_refs_3_
  169.5 48.6 %all_to_all.19 = bf16[4,256,512]{2,1,0:T(8,128)(2,1)S(1)} all-to-all(bf16[4,256,512]{2,1,0:T(8,128)(2,1)S(1)} %bitcast.276), channel_id=1, replica_groups=mesh['dp'=8,'tensor'=4] {'tensor'}, dimensions={0} | all-to-all | bytes 2097152 | tf_op jit(solution)/shard_map/all_to_all | solution.py:854
  236.9 556.6 %moe.1 = (bf16[256,4224]{1,0:T(8,128)(2,1)}, f32[4,3,256,2048]{3,2,1,0:T(8,128)}, bf16[4,256,2176]{2,1,0:T(8,128)(2,1)}, bf16[4,7,256,2176]{3,2,1,0:T(8,128)(2,1...) custom-call(bf16[256,2176]{1,0:T(8,128)(2,1)} %concatenate.44.own_re, ...), custom_call_target="tpu_custom_call" | custom-call | flops 139586437120 | bytes 142606336 | tf_op jit(solution)/shard_map/moe/pallas_call | solution.py:660
  813.5 3.5 all-to-all-start.1
  818.6 22.9 %all-to-all-done.1 = bf16[4,256,512]{2,1,0:T(8,128)(2,1)S(1)} async-done(((bf16[4,256,512]{2,1,0:T(8,128)(2,1)}), bf16[4,256,512]{2,1,0:T(8,128)(2,1)S(1)}, u32[]{:S(2)}, u32[]{:S(2)}) %all-to-all-start.1) | async-done | bytes 1048608 | tf_op jit(solution)/shard_map/all_to_all | solution.py:942
  844.5 4.7 fusion.151
  849.2 5.6 fusion.4
  862.2 9.8 multiply_reduce_fusion.1
  872.0 8.8 multiply_convert_fusion.1
  887.1 3.4 multiply_add_fusion.1
  896.8 4.0 multiply_reduce_fusion.4
  903.6 5.0 convolution_convert_fusion.3
  915.7 6.0 add_convert_fusion
  930.0 9.0 collective-permute-done.16
  945.5 2.8 collective-permute-done.17
  953.9 4.6 convolution_convert_fusion
  965.1 17.8 %slice_bitcast_fusion = (f32[4,256,2048]{2,1,0:T(8,128)}, f32[4,2048,256]{1,2,0:T(8,128)}, f32[4,2048,256]{1,2,0:T(8,128)}) fusion(f32[4,3,256,2048]{3,2,1,0:T(8,128)} %get-tuple-element.55), kind=kLoop, calls=%fused_computation | loop fusion | bytes 50331648 | tf_op jit(solution)/shard_map/squeeze | solution.py:994
  990.1 8.1 collective-permute-done.19
  1002.8 8.7 copy.204
  1011.5 8.8 copy.205
  1027.4 3.4 all-to-all-start.2
  1030.8 5.3 fusion.51
  (402 shorter events, 156.5 us)
Async XLA Ops:
  7.2 100.8 %all-gather.5.cloned.1.call-start = ((), (), s32[]{:S(2)}) async-start(), calls=%async_computation.4 | async-start | bytes 5242880 | tf_op jit(solution)/shard_map/all_gather | solution.py:813
  12.6 205.5 %all-gather.9.cloned.1.call-start = ((), (), s32[]{:S(2)}) async-start(), calls=%async_computation.7 | async-start | bytes 5242880 | tf_op jit(solution)/shard_map/all_gather | solution.py:820
  12.6 94.0 %collective-permute-start.1 = (bf16[1024,2048]{1,0:T(8,128)(2,1)}, bf16[1024,2048]{1,0:T(8,128)(2,1)}, u32[]{:S(2)}, u32[]{:S(2)}) collective-permute-start(bf16[1024,2048]{1,0:T(8,128)(2,1)} %bitcast.291), channel_id=1, source_target_pairs={{16,0},{20,4},{24,8},{28,12},{0,16},{4,20},{8,24},{12,28},{17,1},{... | collective-permute-start | bytes 12582920 | tf_op jit(solution)/shard_map/ppermute | solution.py:715
  15.7 92.3 %collective-permute-start = (bf16[1024,2048]{1,0:T(8,128)(2,1)}, bf16[1024,2048]{1,0:T(8,128)(2,1)}, u32[]{:S(2)}, u32[]{:S(2)}) collective-permute-start(bf16[1024,2048]{1,0:T(8,128)(2,1)} %bitcast.292), channel_id=1, source_target_pairs={{0,8},{4,12},{8,0},{12,4},{16,24},{20,28},{24,16},{28,20},{1,9},{5... | collective-permute-start | bytes 12582920 | tf_op jit(solution)/shard_map/ppermute | solution.py:718
  17.2 151.7 %collective-permute-start.4 = (bf16[1024,2048]{1,0:T(8,128)(2,1)}, bf16[1024,2048]{1,0:T(8,128)(2,1)}, u32[]{:S(2)}, u32[]{:S(2)}) collective-permute-start(bf16[1024,2048]{1,0:T(8,128)(2,1)} %bitcast.293), channel_id=1, source_target_pairs={{0,4},{4,0},{8,12},{12,8},{16,20},{20,16},{24,28},{28,24},{1,5},{5... | collective-permute-start | bytes 12582920 | tf_op jit(solution)/shard_map/ppermute | solution.py:721
  111.2 57.7 %collective-permute-start.5 = (bf16[1024,2048]{1,0:T(8,128)(2,1)}, bf16[1024,2048]{1,0:T(8,128)(2,1)}, u32[]{:S(2)}, u32[]{:S(2)}) collective-permute-start(bf16[1024,2048]{1,0:T(8,128)(2,1)} %collective-permute-done.others_refs_1_), channel_id=1, source_target_pairs={{0,4},{4,0},{8,12},{12,8},{16,20},{20,16},{24,28},{28,24},{1,5},{5... | collective-permute-start | bytes 12582920 | tf_op jit(solution)/shard_map/ppermute | solution.py:721
  114.4 54.5 %collective-permute-start.6 = (bf16[1024,2048]{1,0:T(8,128)(2,1)}, bf16[1024,2048]{1,0:T(8,128)(2,1)}, u32[]{:S(2)}, u32[]{:S(2)}) collective-permute-start(bf16[1024,2048]{1,0:T(8,128)(2,1)} %collective-permute-done.1.others_refs_2_), channel_id=1, source_target_pairs={{0,4},{4,0},{8,12},{12,8},{16,20},{20,16},{24,28},{28,24},{1,5},{5... | collective-permute-start | bytes 12582920 | tf_op jit(solution)/shard_map/ppermute | solution.py:721
  114.9 47.9 %collective-permute-start.3 = (bf16[512,2048]{1,0:T(8,128)(2,1)}, bf16[512,2048]{1,0:T(8,128)(2,1)}, u32[]{:S(2)}, u32[]{:S(2)}) collective-permute-start(bf16[512,2048]{1,0:T(8,128)(2,1)} %slice.126), channel_id=1, source_target_pairs={{0,8},{4,12},{8,0},{12,4},{16,24},{20,28},{24,16},{28,20},{1,9},{5... | collective-permute-start | bytes 6291464 | tf_op jit(solution)/shard_map/ppermute | solution.py:718
  116.4 47.6 %collective-permute-start.2 = (bf16[512,2048]{1,0:T(8,128)(2,1)}, bf16[512,2048]{1,0:T(8,128)(2,1)}, u32[]{:S(2)}, u32[]{:S(2)}) collective-permute-start(bf16[512,2048]{1,0:T(8,128)(2,1)} %slice.125), channel_id=1, source_target_pairs={{16,0},{20,4},{24,8},{28,12},{0,16},{4,20},{8,24},{12,28},{17,1},{... | collective-permute-start | bytes 6291464 | tf_op jit(solution)/shard_map/ppermute | solution.py:715
  218.1 7.5 collective-permute-start.7
  220.1 16.9 %collective-permute-start.8 = (bf16[1024,2048]{1,0:T(8,128)(2,1)}, bf16[1024,2048]{1,0:T(8,128)(2,1)}, u32[]{:S(2)}, u32[]{:S(2)}) collective-permute-start(bf16[1024,2048]{1,0:T(8,128)(2,1)} %pad_maximum_fusion.others_refs_3_), channel_id=1, source_target_pairs={{0,4},{4,0},{8,12},{12,8},{16,20},{20,16},{24,28},{28,24},{1,5},{5... | collective-permute-start | bytes 12582920 | tf_op jit(solution)/shard_map/ppermute | solution.py:721
  813.5 28.0 %all-to-all-start.1 = ((bf16[4,256,512]{2,1,0:T(8,128)(2,1)}), bf16[4,256,512]{2,1,0:T(8,128)(2,1)S(1)}, u32[]{:S(2)}, u32[]{:S(2)}) async-start(bf16[4,256,512]{2,1,0:T(8,128)(2,1)} %pad_maximum_fusion.4), calls=%async_computation.1 | async-start | bytes 2097152 | tf_op jit(solution)/shard_map/all_to_all | solution.py:942
  817.0 104.9 %all-gather.7.cloned.1.call-start = ((), (), s32[]{:S(2)}) async-start(), calls=%async_computation.5 | async-start | bytes 5242880 | tf_op jit(solution)/shard_map/all_gather | solution.py:944
  842.9 181.4 %reduce-scatter.2.cloned.1.call-start = ((), (), s32[]{:S(2)}) async-start(), calls=%async_computation.6 | async-start | bytes 5242880 | tf_op jit(solution)/shard_map/reduce_scatter | solution.py:990
  862.2 59.8 %collective-permute-start.15 = (bf16[2,2,256,512]{3,2,1,0:T(8,128)(2,1)}, bf16[2,2,256,512]{3,2,1,0:T(8,128)(2,1)}, u32[]{:S(2)}, u32[]{:S(2)}) collective-permute-start(bf16[2,2,256,512]{3,2,1,0:T(8,128)(2,1)} %dynamic-slice_bitcast_fusion), channel_id=1, source_target_pairs={{0,4},{4,0},{8,12},{12,8},{16,20},{20,16},{24,28},{28,24},{1,5},{5... | collective-permute-start | bytes 3145736 | tf_op jit(solution)/shard_map/ppermute | solution.py:721
  909.8 16.3 %collective-permute-start.9 = (bf16[2,2,256,512]{3,2,0,1:T(8,128)(2,1)}, bf16[2,2,256,512]{3,2,0,1:T(8,128)(2,1)}, u32[]{:S(2)}, u32[]{:S(2)}) collective-permute-start(bf16[2,2,256,512]{3,2,0,1:T(8,128)(2,1)} %bitcast.251), channel_id=1, source_target_pairs={{0,4},{4,0},{8,12},{12,8},{16,20},{20,16},{24,28},{28,24},{1,5},{5... | collective-permute-start | bytes 3145736 | tf_op jit(solution)/shard_map/ppermute | solution.py:721
  924.7 14.3 %collective-permute-start.16 = (bf16[2,256,512]{2,1,0:T(8,128)(2,1)}, bf16[2,256,512]{2,1,0:T(8,128)(2,1)S(1)}, u32[]{:S(2)}, u32[]{:S(2)}) collective-permute-start(bf16[2,256,512]{2,1,0:T(8,128)(2,1)} %dynamic-slice_bitcast_fusion.3), channel_id=1, source_target_pairs={{0,16},{4,20},{8,24},{12,28},{16,0},{20,4},{24,8},{28,12},{1,17},{... | collective-permute-start | bytes 1572872 | tf_op jit(solution)/shard_map/ppermute | solution.py:725
  928.5 14.3 %collective-permute-start.10 = (bf16[2,256,512]{2,1,0:T(8,128)(2,1)}, bf16[2,256,512]{2,1,0:T(8,128)(2,1)S(1)}, u32[]{:S(2)}, u32[]{:S(2)}) collective-permute-start(bf16[2,256,512]{2,1,0:T(8,128)(2,1)} %dynamic-slice_bitcast_fusion.5), channel_id=1, source_target_pairs={{0,8},{4,12},{8,0},{12,4},{16,24},{20,28},{24,16},{28,20},{1,9},{5... | collective-permute-start | bytes 1572872 | tf_op jit(solution)/shard_map/ppermute | solution.py:718
  940.2 8.1 collective-permute-start.17
  943.8 7.3 collective-permute-start.11
  953.8 10.6 %collective-permute-start.21 = (f32[2,2,256,33]{2,1,0,3:T(2,128)S(1)}, f32[2,2,256,33]{2,1,0,3:T(2,128)S(1)}, u32[]{:S(2)}, u32[]{:S(2)}) collective-permute-start(f32[2,2,256,33]{2,1,0,3:T(2,128)S(1)} %bitcast.295), channel_id=1, source_target_pairs={{0,4},{4,0},{8,12},{12,8},{16,20},{20,16},{24,28},{28,24},{1,5},{5... | collective-permute-start | bytes 405512 | tf_op jit(solution)/shard_map/ppermute | solution.py:721
  959.7 24.7 %collective-permute-start.18 = (bf16[2,2,256,512]{3,2,0,1:T(8,128)(2,1)}, bf16[2,2,256,512]{3,2,0,1:T(8,128)(2,1)S(1)}, u32[]{:S(2)}, u32[]{:S(2)}) collective-permute-start(bf16[2,2,256,512]{3,2,0,1:T(8,128)(2,1)} %bitcast.250), channel_id=1, source_target_pairs={{0,4},{4,0},{8,12},{12,8},{16,20},{20,16},{24,28},{28,24},{1,5},{5... | collective-permute-start | bytes 3145736 | tf_op jit(solution)/shard_map/ppermute | solution.py:721
  963.8 21.6 %collective-permute-start.12 = (bf16[2,2,256,512]{3,2,1,0:T(8,128)(2,1)S(1)}, bf16[2,2,256,512]{3,2,1,0:T(8,128)(2,1)S(1)}, u32[]{:S(2)}, u32[]{:S(2)}) collective-permute-start(bf16[2,2,256,512]{3,2,1,0:T(8,128)(2,1)S(1)} %dynamic-slice_bitcast_fusion.1), channel_id=1, source_target_pairs={{0,4},{4,0},{8,12},{12,8},{16,20},{20,16},{24,28},{28,24},{1,5},{5... | collective-permute-start | bytes 3145736 | tf_op jit(solution)/shard_map/ppermute | solution.py:721
  964.6 18.4 %collective-permute-start.22 = (f32[2,256,33]{1,2,0:T(8,128)S(1)}, f32[2,256,33]{1,2,0:T(8,128)S(1)}, u32[]{:S(2)}, u32[]{:S(2)}) collective-permute-start(f32[2,256,33]{1,2,0:T(8,128)S(1)} %bitcast.296), channel_id=1, source_target_pairs={{0,16},{4,20},{8,24},{12,28},{16,0},{20,4},{24,8},{28,12},{1,17},{... | collective-permute-start | bytes 202760 | tf_op jit(solution)/shard_map/ppermute | solution.py:725
  984.7 13.5 %collective-permute-start.19 = (bf16[2,256,512]{2,1,0:T(8,128)(2,1)S(1)}, bf16[2,256,512]{2,1,0:T(8,128)(2,1)S(1)}, u32[]{:S(2)}, u32[]{:S(2)}) collective-permute-start(bf16[2,256,512]{2,1,0:T(8,128)(2,1)S(1)} %dynamic-slice_bitcast_fusion.2), channel_id=1, source_target_pairs={{0,8},{4,12},{8,0},{12,4},{16,24},{20,28},{24,16},{28,20},{1,9},{5... | collective-permute-start | bytes 1572872 | tf_op jit(solution)/shard_map/ppermute | solution.py:718
  985.8 13.5 %collective-permute-start.13 = (bf16[2,256,512]{2,1,0:T(8,128)(2,1)S(1)}, bf16[2,256,512]{2,1,0:T(8,128)(2,1)S(1)}, u32[]{:S(2)}, u32[]{:S(2)}) collective-permute-start(bf16[2,256,512]{2,1,0:T(8,128)(2,1)S(1)} %dynamic-slice_bitcast_fusion.4), channel_id=1, source_target_pairs={{0,16},{4,20},{8,24},{12,28},{16,0},{20,4},{24,8},{28,12},{1,17},{... | collective-permute-start | bytes 1572872 | tf_op jit(solution)/shard_map/ppermute | solution.py:725
  987.4 14.2 %collective-permute-start.26 = (f32[256,33]{0,1:T(8,128)S(1)}, f32[256,33]{0,1:T(8,128)S(1)}, u32[]{:S(2)}, u32[]{:S(2)}) collective-permute-start(f32[256,33]{0,1:T(8,128)S(1)} %bitcast_add_fusion.2), channel_id=1, source_target_pairs={{0,3},{1,0},{2,1},{3,2},{4,7},{5,4},{6,5},{7,6},{8,11},{9,8},{10,9... | collective-permute-start | bytes 101384 | tf_op jit(solution)/shard_map/ppermute | solution.py:697
  989.5 12.1 %collective-permute-start.25 = (f32[256,33]{0,1:T(8,128)S(1)}, f32[256,33]{0,1:T(8,128)S(1)}, u32[]{:S(2)}, u32[]{:S(2)}) collective-permute-start(f32[256,33]{0,1:T(8,128)S(1)} %bitcast_add_fusion.2), channel_id=1, source_target_pairs={{0,2},{1,3},{2,0},{3,1},{4,6},{5,7},{6,4},{7,5},{8,10},{9,11},{10,... | collective-permute-start | bytes 101384 | tf_op jit(solution)/shard_map/ppermute | solution.py:697
  989.5 12.1 %collective-permute-start.24 = (f32[256,33]{0,1:T(8,128)S(1)}, f32[256,33]{0,1:T(8,128)S(1)}, u32[]{:S(2)}, u32[]{:S(2)}) collective-permute-start(f32[256,33]{0,1:T(8,128)S(1)} %bitcast_add_fusion.2), channel_id=1, source_target_pairs={{0,1},{1,2},{2,3},{3,0},{4,5},{5,6},{6,7},{7,4},{8,9},{9,10},{10,1... | collective-permute-start | bytes 101384 | tf_op jit(solution)/shard_map/ppermute | solution.py:697
  998.5 21.8 %collective-permute-start.20 = (bf16[256,512]{1,0:T(8,128)(2,1)S(1)}, bf16[256,512]{1,0:T(8,128)(2,1)}, u32[]{:S(2)}, u32[]{:S(2)}) collective-permute-start(bf16[256,512]{1,0:T(8,128)(2,1)S(1)} %dynamic-slice_bitcast_fusion.6), channel_id=1, source_target_pairs={{0,16},{4,20},{8,24},{12,28},{16,0},{20,4},{24,8},{28,12},{1,17},{... | collective-permute-start | bytes 786440 | tf_op jit(solution)/shard_map/ppermute | solution.py:725
  1000.3 22.0 %collective-permute-start.14 = (bf16[256,512]{1,0:T(8,128)(2,1)}, bf16[256,512]{1,0:T(8,128)(2,1)}, u32[]{:S(2)}, u32[]{:S(2)}) collective-permute-start(bf16[256,512]{1,0:T(8,128)(2,1)} %dynamic-slice_bitcast_fusion.8), channel_id=1, source_target_pairs={{0,8},{4,12},{8,0},{12,4},{16,24},{20,28},{24,16},{28,20},{1,9},{5... | collective-permute-start | bytes 786440 | tf_op jit(solution)/shard_map/ppermute | solution.py:718
  1027.4 10.8 %all-to-all-start.2 = ((f32[32,1,288]{2,1,0:T(1,128)}), f32[32,1,288]{2,1,0:T(1,128)S(1)}, u32[]{:S(2)}, u32[]{:S(2)}) async-start(f32[32,1,288]{2,1,0:T(1,128)} %all_to_all.14), calls=%async_computation.3 | async-start | bytes 98304 | tf_op jit(solution)/shard_map/all_to_all | solution.py:1010
  (101 other events, 2741.4 us)
Sparse Core Ops, SparseCore 0:
  12.7 83.4 all-gather.4
  115.0 102.3 all-gather.8
  843.0 78.8 all-gather.6
  924.1 77.8 reduce-scatter.1
